TPU v7x, 512 devices: a whole 4x8x8 slice. The times are simulated.
512 devices in a mesh: dp: 64 (over z, x, core), class: 8 (over y).
Axes of the slice: x: 4, y: 8, z: 8, core: 2. Of those that a mesh axis runs over, the one named last changes fastest.
Arguments:
- embeddings: bfloat16 [16384, 1024], P('dp', 'class'), may hold values from -28 to 28, as said below
- labels: bfloat16 [16384, 4096], P('dp', 'class'), may hold values from -55 to 55
- head_weight: bfloat16 [1024, 4096], P(None, 'class'), may hold values from -0.1875 to 0.1875
- send_blocks: int32 [64, 64], P('dp'), may hold values from 0 to 1
- nbr_source: int32 [16384, 32], P('dp'), may hold values from 0 to 63
- nbr_offset: int32 [16384, 32], P('dp'), may hold values from 0 to 127
- counts: int32 [16384], P('dp'), may hold values from 1 to 32
Outputs:
- target_logits: bfloat16 [16384, 4096], P('dp', 'class')
- head_grad: bfloat16 [1024, 4096], P(None, 'class')
Inputs may be any that keep to these rules, and one draw needn't show every extreme that they name: Each image of the embeddings has entries within the range. `send_blocks`: entry [p, q] names which of dp index p's own 2 blocks dp index q receives from p. The neighbour lies in the block that this dp index receives from dp index nbr_source. Only the first counts[r] neighbours of image r are used.
All inputs are finite; a program needn't handle non-finite values.
Results may differ from a plain program's by a relative error of at most 0.0062.
Values may be sent and summed in bfloat16 or wider, within the bound.
A program may use at most 64 MiB of HBM per device.

v0:
```python
import math

import jax
import jax.numpy as jnp
from jax import lax
from jax.sharding import PartitionSpec as P

D = 1024
C = 4096
BLOCK = 128


def on_device(embeddings, labels, head_weight, send_blocks, nbr_source, nbr_offset, counts):
    rows = embeddings.shape[0]
    width_part = embeddings.shape[1]
    class_part = labels.shape[1]
    dp_count = lax.axis_size("dp")
    nbrs = nbr_source.shape[1]
    picks = send_blocks[0]
    out_emb = embeddings.reshape(rows // BLOCK, BLOCK, width_part)[picks]
    out_lab = labels.reshape(rows // BLOCK, BLOCK, class_part)[picks]
    pool_emb, pool_lab = (
        lax.all_to_all(out_emb, "dp", split_axis=0, concat_axis=0, tiled=True),
        lax.all_to_all(out_lab, "dp", split_axis=0, concat_axis=0, tiled=True),
    )
    pool_emb = pool_emb.reshape(dp_count * BLOCK, width_part)
    pool_lab = pool_lab.reshape(dp_count * BLOCK, class_part)
    located = nbr_source * BLOCK + nbr_offset
    step_rows = min(128, rows)
    count_steps = rows // step_rows
    located_steps = located.reshape(count_steps, step_rows, nbrs)

    def partial_block(args):
        emb_blk, where_blk = args
        near = pool_emb[where_blk]
        return jnp.einsum("rd,rkd->rk", emb_blk, near, preferred_element_type=jnp.float32)

    partial_value = lax.map(
        partial_block, (embeddings.reshape(count_steps, step_rows, width_part), located_steps)
    ).reshape(rows, nbrs)
    scores = lax.psum(partial_value, "class")
    valid = lax.broadcasted_iota(jnp.int32, (rows, nbrs), 1) < counts[:, None]
    logits = jnp.where(valid, scores / math.sqrt(D), -1e30)
    top = jnp.max(logits, axis=1, keepdims=True)
    expd = jnp.where(valid, jnp.exp(logits - top), 0.0)
    weights = (expd / jnp.sum(expd, axis=1, keepdims=True)).astype(jnp.bfloat16)

    def label_block(args):
        weight_blk, where_blk = args
        near = pool_lab[where_blk]
        return jnp.einsum("rk,rkc->rc", weight_blk, near, preferred_element_type=jnp.float32)

    spread = lax.map(
        label_block, (weights.reshape(count_steps, step_rows, nbrs), located_steps)
    ).reshape(rows, class_part)
    target = 4.0 * spread + labels.astype(jnp.float32)
    full_emb = lax.all_gather(embeddings, "class", axis=1, tiled=True)
    head = jnp.dot(full_emb, head_weight, preferred_element_type=jnp.float32)
    z_local = jnp.max(target, axis=1, keepdims=True)
    h_local = jnp.max(head, axis=1, keepdims=True)
    z_top, h_top = lax.pmax((z_local, h_local), "class")
    z_part = jnp.sum(jnp.exp(target - z_top), axis=1, keepdims=True)
    h_part = jnp.sum(jnp.exp(head - h_top), axis=1, keepdims=True)
    z_total, h_total = lax.psum((z_part, h_part), "class")
    prob_target = jnp.exp(target - z_top) / z_total
    prob_head = jnp.exp(head - h_top) / h_total
    diff = (C * (prob_head - prob_target)).astype(jnp.bfloat16)
    part_grad = lax.dot_general(
        full_emb, diff, (((0,), (0,)), ((), ())), preferred_element_type=jnp.float32
    )
    scale = 1.0 / math.sqrt(rows * dp_count)
    limit = 0.5 * math.sqrt(D * C)
    summed = lax.psum(part_grad, "dp") * scale
    squared = lax.psum(jnp.sum(summed * summed), "class")
    factor = jnp.minimum(1.0, limit / jnp.sqrt(squared))
    head_grad = (summed * factor).astype(jnp.bfloat16)
    return (target.astype(jnp.bfloat16), head_grad)


def solution(mesh):
    return jax.shard_map(
        on_device,
        mesh=mesh,
        in_specs=(
            P("dp", "class"),
            P("dp", "class"),
            P(None, "class"),
            P("dp", None),
            P("dp", None),
            P("dp", None),
            P("dp"),
        ),
        out_specs=(P("dp", "class"), P(None, "class")),
        check_vma=False,
    )
```

profile of v0, /device:TPU:1, one launch (start us, length us, event | category | flops | bytes accessed | tf_op | source)
XLA Modules:
  0.0 581.4 jit_solution(2350793517152833636)
XLA Ops:
  7.9 3.0 gather_fusion.2
  10.9 15.0 %all-to-all-start = ((bf16[64,128,128]{2,1,0:T(8,128)(2,1)}), bf16[64,128,128]{2,1,0:T(8,128)(2,1)S(1)}, u32[]{:S(2)}, u32[]{:S(2)}) async-start(bf16[64,128,128]{2,1,0:T(8,128)(2,1)} %gather_fusion.2), calls=%async_computation | async-start | bytes 4194304 | tf_op jit(solution)/shard_map/all_to_all | solution.py:23
  25.9 5.4 gather_fusion.3
  31.3 44.3 %all-to-all-done = bf16[64,128,128]{2,1,0:T(8,128)(2,1)S(1)} async-done(((bf16[64,128,128]{2,1,0:T(8,128)(2,1)}), bf16[64,128,128]{2,1,0:T(8,128)(2,1)S(1)}, u32[]{:S(2)}, u32[]{:S(2)}) %all-to-all-start) | async-done | bytes 2097184 | tf_op jit(solution)/shard_map/all_to_all | solution.py:23
  75.6 7.2 %all-to-all-start.1 = ((bf16[64,128,512]{2,1,0:T(8,128)(2,1)}), bf16[64,128,512]{2,1,0:T(8,128)(2,1)}, u32[]{:S(2)}, u32[]{:S(2)}) async-start(bf16[64,128,512]{2,1,0:T(8,128)(2,1)} %gather_fusion.3), calls=%async_computation.1 | async-start | bytes 16777216 | tf_op jit(solution)/shard_map/all_to_all | solution.py:24
  84.4 22.7 %all_gather.3 = bf16[256,1024]{1,0:T(8,128)(2,1)S(1)} all-gather(bf16[256,128]{1,0:T(8,128)(2,1)S(1)} %copy-done.2), channel_id=1, replica_groups=mesh['dp'=64,'class'=8] {'class'}, dimensions={1}, use_global_device_ids=true | all-gather | bytes 589824 | tf_op jit(solution)/shard_map/all_gather | solution.py:57
  109.8 37.0 %while.20 = (s32[]{:T(128)}, f32[2,128,32]{2,1,0:T(8,128)}, bf16[2,128,128]{2,1,0:T(8,128)(2,1)S(1)}, s32[2,128,32]{2,1,0:T(8,128)}, bf16[8192,128]{1,0:T(8,128)(2,1)S(1)}, /*index=5*/s32[]{:T(128)}) while((s32[]{:T(128)}, f32[2,128,32]{2,1,0:T(8,128)}, bf16[2,128,128]{2,1,0:T(8,128)(2,1)S(1)}, s32[2,128,32]{2,1,0:T(8,128)}, ...), condition=%wide.region_1.2_spmd, body=%wide.region_0.1_spmd.sunk | while | flops 1064962 | bytes 3457613 | solution.py:38
  110.7 15.0 %gather_fusion = bf16[4096,128]{1,0:T(8,128)(2,1)} fusion(bf16[8192,128]{1,0:T(8,128)(2,1)S(1)} %get-tuple-element.170, s32[4096]{0:T(1024)S(1)} %broadcast_clamp_fusion.4), kind=kCustom, calls=%fused_computation.clone.1 | custom fusion | bytes 2113536 | tf_op jit(solution)/shard_map/while/body/eval_jaxpr/gather | solution.py:35
  125.7 1.9 fusion.31
  129.2 15.0 %gather_fusion = bf16[4096,128]{1,0:T(8,128)(2,1)} fusion(bf16[8192,128]{1,0:T(8,128)(2,1)S(1)} %get-tuple-element.170, s32[4096]{0:T(1024)S(1)} %broadcast_clamp_fusion.4), kind=kCustom, calls=%fused_computation.clone.1 | custom fusion | bytes 2113536 | tf_op jit(solution)/shard_map/while/body/eval_jaxpr/gather | solution.py:35
  146.7 24.2 %psum.35 = f32[256,32]{1,0:T(8,128)S(1)} all-reduce(f32[256,32]{1,0:T(8,128)} %bitcast.79), channel_id=1, replica_groups=mesh['dp'=64,'class'=8] {'class'}, use_global_device_ids=true, to_apply=%region_2.3 | all-reduce | flops 8192 | bytes 65536 | tf_op jit(solution)/shard_map/psum | solution.py:41
  173.5 92.2 %all-to-all-done.1 = bf16[64,128,512]{2,1,0:T(8,128)(2,1)} async-done(((bf16[64,128,512]{2,1,0:T(8,128)(2,1)}), bf16[64,128,512]{2,1,0:T(8,128)(2,1)}, u32[]{:S(2)}, u32[]{:S(2)}) %all-to-all-start.1) | async-done | bytes 8388640 | tf_op jit(solution)/shard_map/all_to_all | solution.py:24
  265.7 53.2 %while.21 = (s32[]{:T(128)}, f32[2,128,512]{2,1,0:T(8,128)}, bf16[2,128,32]{2,1,0:T(8,128)(2,1)S(1)}, s32[2,128,32]{2,1,0:T(8,128)}, bf16[8192,512]{1,0:T(8,128)(2,1)}, /*index=5*/s32[]{:T(128)}) while((s32[]{:T(128)}, f32[2,128,512]{2,1,0:T(8,128)}, bf16[2,128,32]{2,1,0:T(8,128)(2,1)S(1)}, s32[2,128,32]{2,1,0:T(8,128)}, ...), condition=%wide.region_6.7_spmd, body=%wide.region_5.6_spmd.sunk | while | flops 4210690 | bytes 17703048 | solution.py:53
  266.7 21.9 %gather_fusion.1 = bf16[4096,512]{1,0:T(8,128)(2,1)} fusion(bf16[8192,512]{1,0:T(8,128)(2,1)} %get-tuple-element.188, s32[4096]{0:T(1024)S(1)} %broadcast_clamp_fusion.5), kind=kCustom, calls=%fused_computation.1.clone.1 | custom fusion | bytes 8404992 | tf_op jit(solution)/shard_map/while/body/eval_jaxpr/gather | solution.py:50
  288.5 2.9 fusion.34
  293.3 21.9 %gather_fusion.1 = bf16[4096,512]{1,0:T(8,128)(2,1)} fusion(bf16[8192,512]{1,0:T(8,128)(2,1)} %get-tuple-element.188, s32[4096]{0:T(1024)S(1)} %broadcast_clamp_fusion.5), kind=kCustom, calls=%fused_computation.1.clone.1 | custom fusion | bytes 8404992 | tf_op jit(solution)/shard_map/while/body/eval_jaxpr/gather | solution.py:50
  315.1 2.9 fusion.34
  320.2 13.9 %all-reduce.1 = (f32[256]{0:T(256)S(1)}, f32[256]{0:T(256)S(1)}) all-reduce(f32[256]{0:T(256)S(1)} %fusion.13, f32[256]{0:T(256)S(1)} %copy-done.10), channel_id=1, replica_groups=mesh['dp'=64,'class'=8] {'class'}, use_global_device_ids=true, to_apply=%region_12.13 | all-reduce | flops 512 | bytes 4096 | tf_op jit(solution)/shard_map/pmax | solution.py:61
  335.0 11.2 %all-reduce = (f32[256]{0:T(256)S(1)}, f32[256]{0:T(256)S(1)}) all-reduce(f32[256]{0:T(256)S(1)} %get-tuple-element.86, f32[256]{0:T(256)S(1)} %get-tuple-element.91), channel_id=1, replica_groups=mesh['dp'=64,'class'=8] {'class'}, use_global_device_ids=true, to_apply=%region_14.15 | all-reduce | flops 512 | bytes 4096 | tf_op jit(solution)/shard_map/psum | solution.py:64
  346.2 2.0 convolution_bitcast_fusion
  348.2 205.4 %all-reduce.4.cloned.1.call-done = f32[1024,512]{0,1:T(8,128)} async-done(((f32[1024,512]{0,1:T(8,128)}), f32[1024,512]{0,1:T(8,128)}) %all-reduce.4.cloned.1.call-update) | async-done | bytes 2097168 | tf_op jit(solution)/shard_map/psum | solution.py:73
  553.6 2.9 multiply_reduce_fusion
  556.5 13.8 %psum.39 = f32[]{:T(128)} all-reduce(f32[]{:T(128)} %multiply_reduce_fusion), channel_id=1, replica_groups=mesh['dp'=64,'class'=8] {'class'}, use_global_device_ids=true, to_apply=%region_17.18 | all-reduce | flops 1 | bytes 8 | tf_op jit(solution)/shard_map/psum | solution.py:74
  572.2 2.3 copy.12
  (63 shorter events, 19.7 us)
Async XLA Ops:
  7.2 100.7 %copy-start = (bf16[1024,512]{1,0:T(8,128)(2,1)S(1)}, bf16[1024,512]{1,0:T(8,128)(2,1)}, u32[]{:S(2)}) copy-start(bf16[1024,512]{1,0:T(8,128)(2,1)} %param.13) | copy-start | bytes 3145732
  10.9 15.0 %copy-start.1 = (bf16[256,512]{1,0:T(8,128)(2,1)S(1)}, bf16[256,512]{1,0:T(8,128)(2,1)}, u32[]{:S(2)}) copy-start(bf16[256,512]{1,0:T(8,128)(2,1)} %param.12) | copy-start | bytes 786436
  10.9 64.7 %all-to-all-start = ((bf16[64,128,128]{2,1,0:T(8,128)(2,1)}), bf16[64,128,128]{2,1,0:T(8,128)(2,1)S(1)}, u32[]{:S(2)}, u32[]{:S(2)}) async-start(bf16[64,128,128]{2,1,0:T(8,128)(2,1)} %gather_fusion.2), calls=%async_computation | async-start | bytes 4194304 | tf_op jit(solution)/shard_map/all_to_all | solution.py:23
  31.3 51.6 %copy-start.9 = (s32[256,32]{0,1:T(8,128)S(1)}, s32[256,32]{0,1:T(8,128)}, u32[]{:S(2)}) copy-start(s32[256,32]{0,1:T(8,128)} %param.16) | copy-start | bytes 98308
  31.3 53.1 %copy-start.2 = (bf16[256,128]{1,0:T(8,128)(2,1)S(1)}, bf16[256,128]{1,0:T(8,128)(2,1)}, u32[]{:S(2)}) copy-start(bf16[256,128]{1,0:T(8,128)(2,1)} %param.11) | copy-start | bytes 196612
  75.6 190.1 %all-to-all-start.1 = ((bf16[64,128,512]{2,1,0:T(8,128)(2,1)}), bf16[64,128,512]{2,1,0:T(8,128)(2,1)}, u32[]{:S(2)}, u32[]{:S(2)}) async-start(bf16[64,128,512]{2,1,0:T(8,128)(2,1)} %gather_fusion.3), calls=%async_computation.1 | async-start | bytes 16777216 | tf_op jit(solution)/shard_map/all_to_all | solution.py:24
  82.8 470.7 %all-reduce.4.cloned.1.call-start = ((), (), s32[]{:S(2)}) async-start(), calls=%async_computation.2 | async-start | bytes 4194304 | tf_op jit(solution)/shard_map/psum | solution.py:73
  107.1 0.8 copy-start.4
  265.7 54.5 %copy-start.10 = (f32[256]{0:T(256)S(1)}, f32[256]{0:T(256)}, u32[]{:S(2)}) copy-start(f32[256]{0:T(256)} %get-tuple-element.89) | copy-start | bytes 3076
  288.5 2.9 copy-start.7
  291.5 0.8 copy-start.8
  315.1 2.9 copy-start.7
  318.1 0.8 copy-start.8
  318.9 15.2 %copy-start.6 = (f32[256,512]{1,0:T(8,128)S(1)}, f32[256,512]{1,0:T(8,128)}, u32[]{:S(2)}) copy-start(f32[256,512]{1,0:T(8,128)} %get-tuple-element.90) | copy-start | bytes 1572868
  318.9 27.3 %copy-start.5 = (bf16[256,1024]{1,0:T(8,128)(2,1)S(1)}, bf16[256,1024]{1,0:T(8,128)(2,1)}, u32[]{:S(2)}) copy-start(bf16[256,1024]{1,0:T(8,128)(2,1)} %copy-done.4) | copy-start | bytes 1572868
  553.6 17.4 %copy-start.3 = (f32[1024,512]{0,1:T(8,128)S(1)}, f32[1024,512]{0,1:T(8,128)}, u32[]{:S(2)}) copy-start(f32[1024,512]{0,1:T(8,128)} %all-reduce.4.cloned.1.call-done) | copy-start | bytes 6291460
Sparse Core Ops, SparseCore 0:
  348.3 205.1 all-reduce.3
where the time goes:
time: 586 us; the launch traced here: 581 us
  waiting for transfers between devices  342 us (58%)
  local copies, waits for them, and re-layouts  89.3 us (15%)
  blocking collectives  85.7 us (15%)
  starting transfers between devices  22.3 us (4%)
  between operations  14.8 us (3%)
  other arithmetic  13.9 us (2%)
  matrix products  13.4 us (2%)
    psum x1, waiting for transfers between devices, on_device(): summed = lax.psum(part_grad, 'dp') * scale  205 us
    all_to_all x1, waiting for transfers between devices, on_device(): lax.all_to_all(out_lab, 'dp', split_axis=0, concat_axis=0, tiled=True)  92.2 us
    all_to_all x1, waiting for transfers between devices, on_device(): lax.all_to_all(out_emb, 'dp', split_axis=0, concat_axis=0, tiled=True)  44.3 us
    gather x2, local copies, waits for them, and re-layouts, label_block(): near = pool_lab[where_blk]  43.7 us
    gather x2, local copies, waits for them, and re-layouts, partial_block(): near = pool_emb[where_blk]  30.1 us
    psum x1, blocking collectives, on_device(): scores = lax.psum(partial_value, 'class')  24.2 us
    all_gather x1, blocking collectives, on_device(): full_emb = lax.all_gather(embeddings, 'class', axis=1, tiled=True)  22.7 us
    all_to_all x1, starting transfers between devices, on_device(): lax.all_to_all(out_emb, 'dp', split_axis=0, concat_axis=0, tiled=True)  15 us
  transfers between devices with their start and end apart: 3, of which 3 were waited for; matrix products, arithmetic and copies ran while one was open for 8% of the time, Pallas kernels for 0%

commit v1 on v0

v1 whole, which is shorter than its diff:
```python
import math

import jax
import jax.numpy as jnp
from jax import lax
from jax.sharding import PartitionSpec as P

D = 1024
C = 4096
BLOCK = 128


def _combine_stats(local_max, local_sum):
    both = lax.all_gather(jnp.stack([local_max, local_sum], axis=0), "class", axis=0)
    maxes, sums = both[:, 0], both[:, 1]
    top = jnp.max(maxes, axis=0)
    total = jnp.sum(sums * jnp.exp(maxes - top[None, :]), axis=0)
    return top, total


def on_device(embeddings, labels, head_weight, send_blocks, nbr_source, nbr_offset, counts):
    rows = embeddings.shape[0]
    width_part = embeddings.shape[1]
    class_part = labels.shape[1]
    dp_count = lax.axis_size("dp")
    nbrs = nbr_source.shape[1]
    picks = send_blocks[0]
    out_emb = embeddings.reshape(rows // BLOCK, BLOCK, width_part)[picks]
    out_lab = labels.reshape(rows // BLOCK, BLOCK, class_part)[picks]
    pool_emb = lax.all_to_all(out_emb, "dp", split_axis=0, concat_axis=0, tiled=True)
    pool_lab = lax.all_to_all(out_lab, "dp", split_axis=0, concat_axis=0, tiled=True)
    pool_rows = dp_count * BLOCK
    pool_emb = pool_emb.reshape(pool_rows, width_part)
    pool_lab = pool_lab.reshape(pool_rows, class_part)
    located = nbr_source * BLOCK + nbr_offset

    full_emb = lax.all_gather(embeddings, "class", axis=1, tiled=True)
    head = jnp.dot(full_emb, head_weight, preferred_element_type=jnp.float32)
    h_top, h_total = _combine_stats(
        jnp.max(head, axis=1),
        jnp.sum(jnp.exp(head - jnp.max(head, axis=1, keepdims=True)), axis=1),
    )
    prob_head = jnp.exp(head - h_top[:, None]) / h_total[:, None]

    near = pool_emb[located]
    partial_value = jnp.einsum(
        "rd,rkd->rk", embeddings, near, preferred_element_type=jnp.float32
    )
    scores = lax.psum(partial_value, "class")
    valid = lax.broadcasted_iota(jnp.int32, (rows, nbrs), 1) < counts[:, None]
    logits = jnp.where(valid, scores / math.sqrt(D), -1e30)
    top = jnp.max(logits, axis=1, keepdims=True)
    expd = jnp.where(valid, jnp.exp(logits - top), 0.0)
    weights = (expd / jnp.sum(expd, axis=1, keepdims=True)).astype(jnp.bfloat16)

    row_ids = lax.broadcasted_iota(jnp.int32, (rows, nbrs), 0)
    dense = jnp.zeros((rows, pool_rows), jnp.float32).at[row_ids, located].add(
        weights.astype(jnp.float32)
    )
    dense_hi = dense.astype(jnp.bfloat16)
    dense_lo = (dense - dense_hi.astype(jnp.float32)).astype(jnp.bfloat16)
    spread = jnp.dot(dense_hi, pool_lab, preferred_element_type=jnp.float32) + jnp.dot(
        dense_lo, pool_lab, preferred_element_type=jnp.float32
    )
    target = 4.0 * spread + labels.astype(jnp.float32)
    z_local = jnp.max(target, axis=1)
    z_top, z_total = _combine_stats(
        z_local, jnp.sum(jnp.exp(target - z_local[:, None]), axis=1)
    )
    prob_target = jnp.exp(target - z_top[:, None]) / z_total[:, None]
    diff = (C * (prob_head - prob_target)).astype(jnp.bfloat16)
    part_grad = lax.dot_general(
        full_emb, diff, (((0,), (0,)), ((), ())), preferred_element_type=jnp.float32
    )
    scale = 1.0 / math.sqrt(rows * dp_count)
    limit = 0.5 * math.sqrt(D * C)
    summed = lax.psum_scatter(part_grad, "dp", scatter_dimension=0, tiled=True) * scale
    squared = lax.psum(jnp.sum(summed * summed), ("dp", "class"))
    factor = jnp.minimum(1.0, limit / jnp.sqrt(squared))
    head_grad = lax.all_gather((summed * factor).astype(jnp.bfloat16), "dp", axis=0, tiled=True)
    return (target.astype(jnp.bfloat16), head_grad)


def solution(mesh):
    return jax.shard_map(
        on_device,
        mesh=mesh,
        in_specs=(
            P("dp", "class"),
            P("dp", "class"),
            P(None, "class"),
            P("dp", None),
            P("dp", None),
            P("dp", None),
            P("dp"),
        ),
        out_specs=(P("dp", "class"), P(None, "class")),
        check_vma=False,
    )
```

time: 586 us -> 645 us (1.10)
  blocking collectives: 85.7 us -> 184 us
  waiting for transfers between devices: 342 us -> 293 us
  other arithmetic: 13.9 us -> 52.6 us
  local copies, waits for them, and re-layouts: 89.3 us -> 57.8 us
  matrix products: 13.4 us -> 20.5 us
    psum x1 -> x0, waiting for transfers between devices: 205 us -> none  [on_device(): summed = lax.psum(part_grad, 'dp') * scale]
    reduce_scatter x0 -> x1, waiting for transfers between devices: none -> 148 us  [on_device(): lax.psum_scatter(part_grad, 'dp', scatter_dimension=0, tiled=True) * scale]
    all_gather x0 -> x1, waiting for transfers between devices: none -> 79.7 us  [on_device(): lax.all_gather((summed * factor).astype(jnp.bfloat16), 'dp', axis=0, tile...]
    psum x2 -> x1, blocking collectives: 25 us -> 100 us  [on_device(): squared = lax.psum(jnp.sum(summed * summed), ('dp', 'class'))]
    all_to_all x1, waiting for transfers between devices: 92.2 us -> 21 us  [on_device(): lax.all_to_all(out_lab, 'dp', split_axis=0, concat_axis=0, tiled=True)]
    unnamed x0 -> x6, other arithmetic: none -> 47.3 us
    gather x4 -> x1, local copies, waits for them, and re-layouts: 73.8 us -> 29.2 us  [on_device(): near = pool_emb[located]]
    all_gather x0 -> x2, blocking collectives: none -> 36.2 us  [_combine_stats(): lax.all_gather(jnp.stack([local_max, local_sum], axis=0), 'class', axis=0)]
  transfers between devices with their start and end apart: 3 -> 4, of which waited for: 3 -> 4; matrix products, arithmetic and copies ran while one was open for 8% -> 16% of each run, Pallas kernels for 0% -> 0%
where the time goes in v1:
time: 645 us
  waiting for transfers between devices  293 us (45%)
  blocking collectives  184 us (29%)
  local copies, waits for them, and re-layouts  57.8 us (9%)
  other arithmetic  52.6 us (8%)
  starting transfers between devices  22.2 us (3%)
  matrix products  20.5 us (3%)
  between operations  15 us (2%)
    reduce_scatter x1, waiting for transfers between devices, on_device(): lax.psum_scatter(part_grad, 'dp', scatter_dimension=0, tiled=True) * scale  148 us
    psum x1, blocking collectives, on_device(): squared = lax.psum(jnp.sum(summed * summed), ('dp', 'class'))  100 us
    all_gather x1, waiting for transfers between devices, on_device(): lax.all_gather((summed * factor).astype(jnp.bfloat16), 'dp', axis=0, tile...  79.7 us
    unnamed x6, other arithmetic  47.3 us
    all_to_all x1, waiting for transfers between devices, on_device(): lax.all_to_all(out_emb, 'dp', split_axis=0, concat_axis=0, tiled=True)  44.3 us
    all_gather x2, blocking collectives, _combine_stats(): lax.all_gather(jnp.stack([local_max, local_sum], axis=0), 'class', axis=0)  36.2 us
    gather x1, local copies, waits for them, and re-layouts, on_device(): near = pool_emb[located]  29.2 us
    psum x1, blocking collectives, on_device(): scores = lax.psum(partial_value, 'class')  24.4 us
  transfers between devices with their start and end apart: 4, of which 4 were waited for; matrix products, arithmetic and copies ran while one was open for 16% of the time, Pallas kernels for 0%

profile of v1, /device:TPU:1, one launch (start us, length us, event | category | flops | bytes accessed | tf_op | source)
XLA Modules:
  0.0 644.6 jit_solution(2418893639809104688)
XLA Ops:
  8.0 3.0 gather_fusion
  11.0 14.8 %all-to-all-start = ((bf16[64,128,128]{2,1,0:T(8,128)(2,1)}), bf16[64,128,128]{2,1,0:T(8,128)(2,1)S(1)}, u32[]{:S(2)}, u32[]{:S(2)}) async-start(bf16[64,128,128]{2,1,0:T(8,128)(2,1)} %gather_fusion), calls=%async_computation | async-start | bytes 4194304 | tf_op jit(solution)/shard_map/all_to_all | solution.py:30
  25.8 5.4 gather_fusion.2
  31.2 44.3 %all-to-all-done = bf16[64,128,128]{2,1,0:T(8,128)(2,1)S(1)} async-done(((bf16[64,128,128]{2,1,0:T(8,128)(2,1)}), bf16[64,128,128]{2,1,0:T(8,128)(2,1)S(1)}, u32[]{:S(2)}, u32[]{:S(2)}) %all-to-all-start) | async-done | bytes 2097184 | tf_op jit(solution)/shard_map/all_to_all | solution.py:30
  75.5 7.2 %all-to-all-start.1 = ((bf16[64,128,512]{2,1,0:T(8,128)(2,1)}), bf16[64,128,512]{2,1,0:T(8,128)(2,1)}, u32[]{:S(2)}, u32[]{:S(2)}) async-start(bf16[64,128,512]{2,1,0:T(8,128)(2,1)} %gather_fusion.2), calls=%async_computation.1 | async-start | bytes 16777216 | tf_op jit(solution)/shard_map/all_to_all | solution.py:31
  85.3 1.6 reshape.99
  86.9 1.0 reshape.85
  87.9 22.7 %all_gather.18 = bf16[256,1024]{1,0:T(8,128)(2,1)S(1)} all-gather(bf16[256,128]{1,0:T(8,128)(2,1)S(1)} %copy-done.2), channel_id=1, replica_groups=mesh['dp'=64,'class'=8] {'class'}, dimensions={1}, use_global_device_ids=true | all-gather | bytes 589824 | tf_op jit(solution)/shard_map/all_gather | solution.py:37
  112.9 18.0 %all-gather.2 = f32[8,2,256]{2,1,0:T(2,128)S(1)} all-gather(f32[1,2,256]{2,1,0:T(2,128)S(1)} %maximum_bitcast_fusion), channel_id=2, replica_groups=mesh['dp'=64,'class'=8] {'class'}, dimensions={0}, use_global_device_ids=true | all-gather | bytes 18432 | tf_op jit(solution)/shard_map/all_gather | solution.py:14
  131.0 29.2 %gather_fusion.1 = bf16[8192,128]{1,0:T(8,128)(2,1)} fusion(bf16[8192,128]{1,0:T(8,128)(2,1)S(1)} %bitcast.55, s32[8192]{0:T(1024)S(1)} %broadcast_clamp_fusion), kind=kCustom, calls=%fused_computation.1 | custom fusion | bytes 4227072 | tf_op jit(solution)/shard_map/gather | solution.py:45
  160.2 2.8 fusion.20
  163.0 24.4 %psum.14 = f32[256,32]{1,0:T(8,128)S(1)} all-reduce(f32[256,32]{1,0:T(8,128)S(1)} %bitcast.61), channel_id=1, replica_groups=mesh['dp'=64,'class'=8] {'class'}, use_global_device_ids=true, to_apply=%region_0.0 | all-reduce | flops 8192 | bytes 65536 | tf_op jit(solution)/shard_map/psum | solution.py:49
  188.1 47.1 %scatter_custom_fusion = f32[2097152]{0:T(1024)} fusion(s32[8192]{0:T(1024)} %reshape.99, f32[8192]{0:T(1024)S(1)} %reshape.101, f32[]{:T(128)} %constant.13.clone.1), kind=kCustom, calls=%fused_computation.6 | custom fusion | flops 8192 | bytes 8389120
  235.2 9.4 %reshape.74 = f32[256,8192]{1,0:T(8,128)} reshape(f32[2097152]{0:T(1024)} %scatter_custom_fusion) | data formatting | bytes 16777216 | tf_op jit(solution)/shard_map/scatter-add | solution.py:57
  244.6 21.0 %all-to-all-done.1 = bf16[64,128,512]{2,1,0:T(8,128)(2,1)} async-done(((bf16[64,128,512]{2,1,0:T(8,128)(2,1)}), bf16[64,128,512]{2,1,0:T(8,128)(2,1)}, u32[]{:S(2)}, u32[]{:S(2)}) %all-to-all-start.1) | async-done | bytes 8388640 | tf_op jit(solution)/shard_map/all_to_all | solution.py:31
  265.6 10.6 %fusion = f32[256,512]{1,0:T(8,128)S(1)} fusion(bf16[8192,512]{1,0:T(8,128)(2,1)} %bitcast.10, f32[256,8192]{1,0:T(8,128)} %reshape.74), kind=kOutput, calls=%fused_computation.5 | convolution fusion | flops 2155872256 | bytes 17301504 | tf_op jit(solution)/shard_map/dot_general | solution.py:62
  276.3 5.9 fusion.33
  283.1 18.3 %all-gather.3 = f32[8,2,256]{2,1,0:T(2,128)S(1)} all-gather(f32[1,2,256]{2,1,0:T(2,128)S(1)} %maximum_bitcast_fusion.1), channel_id=3, replica_groups=mesh['dp'=64,'class'=8] {'class'}, dimensions={0}, use_global_device_ids=true | all-gather | bytes 18432 | tf_op jit(solution)/shard_map/all_gather | solution.py:14
  302.1 1.9 copy.28
  304.1 147.5 %reduce-scatter.4.cloned.1.call-done = f32[16,512]{1,0:T(8,128)} async-done(((f32[1024,512]{1,0:T(8,128)}), f32[16,512]{1,0:T(8,128)}) %reduce-scatter.4.cloned.1.call-update) | async-done | bytes 32784 | tf_op jit(solution)/shard_map/reduce_scatter | solution.py:77
  453.2 100.5 %psum.15 = f32[]{:T(128)} all-reduce(f32[]{:T(128)} %multiply_reduce_fusion), channel_id=1, replica_groups=mesh['dp'=64,'class'=8] {'dp','class'}, use_global_device_ids=true, to_apply=%region_14.15 | all-reduce | flops 1 | bytes 8 | tf_op jit(solution)/shard_map/psum | solution.py:78
  554.3 1.4 multiply_convert_fusion.2
  555.7 79.7 %all-gather.6.cloned.1.call-done = bf16[1024,512]{1,0:T(8,128)(2,1)} async-done(((bf16[16,512]{1,0:T(8,128)(2,1)}), bf16[1024,512]{1,0:T(8,128)(2,1)}) %all-gather.6.cloned.1.call-update) | async-done | bytes 1048592 | tf_op jit(solution)/shard_map/all_gather | solution.py:80
  635.5 2.3 copy.49
  (54 shorter events, 9.7 us)
Async XLA Ops:
  7.2 104.2 %copy-start = (bf16[1024,512]{1,0:T(8,128)(2,1)S(1)}, bf16[1024,512]{1,0:T(8,128)(2,1)}, u32[]{:S(2)}) copy-start(bf16[1024,512]{1,0:T(8,128)(2,1)} %param.9) | copy-start | bytes 3145732
  7.2 18.6 %copy-start.1 = (bf16[256,512]{1,0:T(8,128)(2,1)S(1)}, bf16[256,512]{1,0:T(8,128)(2,1)}, u32[]{:S(2)}) copy-start(bf16[256,512]{1,0:T(8,128)(2,1)} %param.8) | copy-start | bytes 786436
  11.0 64.5 %all-to-all-start = ((bf16[64,128,128]{2,1,0:T(8,128)(2,1)}), bf16[64,128,128]{2,1,0:T(8,128)(2,1)S(1)}, u32[]{:S(2)}, u32[]{:S(2)}) async-start(bf16[64,128,128]{2,1,0:T(8,128)(2,1)} %gather_fusion), calls=%async_computation | async-start | bytes 4194304 | tf_op jit(solution)/shard_map/all_to_all | solution.py:30
  31.2 51.6 %copy-start.8 = (s32[256,32]{0,1:T(8,128)S(1)}, s32[256,32]{0,1:T(8,128)}, u32[]{:S(2)}) copy-start(s32[256,32]{0,1:T(8,128)} %param.12) | copy-start | bytes 98308
  31.2 53.1 %copy-start.10 = (s32[2]{0:T(128)S(1)}, s32[2]{0:T(128)}, u32[]{:S(2)}) copy-start(s32[2]{0:T(128)} %constant.33) | copy-start | bytes 28
  31.2 53.2 %copy-start.11 = (s32[2]{0:T(128)S(1)}, s32[2]{0:T(128)}, u32[]{:S(2)}) copy-start(s32[2]{0:T(128)} %constant.36) | copy-start | bytes 28
  31.2 56.7 %copy-start.2 = (bf16[256,128]{1,0:T(8,128)(2,1)S(1)}, bf16[256,128]{1,0:T(8,128)(2,1)}, u32[]{:S(2)}) copy-start(bf16[256,128]{1,0:T(8,128)(2,1)} %param.7) | copy-start | bytes 196612
  75.5 190.1 %all-to-all-start.1 = ((bf16[64,128,512]{2,1,0:T(8,128)(2,1)}), bf16[64,128,512]{2,1,0:T(8,128)(2,1)}, u32[]{:S(2)}, u32[]{:S(2)}) async-start(bf16[64,128,512]{2,1,0:T(8,128)(2,1)} %gather_fusion.2), calls=%async_computation.1 | async-start | bytes 16777216 | tf_op jit(solution)/shard_map/all_to_all | solution.py:31
  82.7 368.9 %reduce-scatter.4.cloned.1.call-start = ((), (), s32[]{:S(2)}) async-start(), calls=%async_computation.4 | async-start | bytes 2129920 | tf_op jit(solution)/shard_map/reduce_scatter | solution.py:77
  110.6 0.8 copy-start.4
  111.9 0.8 copy-start.6
  131.0 56.4 %copy-start.9 = (s32[256]{0:T(256)S(1)}, s32[256]{0:T(256)}, u32[]{:S(2)}) copy-start(s32[256]{0:T(256)} %param.13) | copy-start | bytes 3076
  265.6 10.6 %copy-start.3 = (f32[256,8192]{1,0:T(8,128)S(1)}, f32[256,8192]{1,0:T(8,128)}, u32[]{:S(2)}) copy-start(f32[256,8192]{1,0:T(8,128)} %reshape.74) | copy-start | bytes 25165828
  276.3 25.1 %copy-start.5 = (bf16[256,1024]{1,0:T(8,128)(2,1)S(1)}, bf16[256,1024]{1,0:T(8,128)(2,1)}, u32[]{:S(2)}) copy-start(bf16[256,1024]{1,0:T(8,128)(2,1)} %copy-done.4) | copy-start | bytes 1572868
  276.3 25.1 %copy-start.7 = (f32[256,512]{1,0:T(8,128)S(1)}, f32[256,512]{1,0:T(8,128)}, u32[]{:S(2)}) copy-start(f32[256,512]{1,0:T(8,128)} %copy-done.6) | copy-start | bytes 1572868
  304.0 331.4 %all-gather.6.cloned.1.call-start = ((), (), s32[]{:S(2)}) async-start(), calls=%async_computation.3 | async-start | bytes 1064960 | tf_op jit(solution)/shard_map/all_gather | solution.py:80
Sparse Core Ops, SparseCore 0:
  304.2 147.3 reduce-scatter.3
  555.8 79.5 all-gather.5

commit v2 on v1

--- a/solution.py
+++ b/solution.py
@@ -3,11 +3,142 @@
 import jax
 import jax.numpy as jnp
 from jax import lax
+from jax.experimental import pallas as pl
+from jax.experimental.pallas import tpu as pltpu
 from jax.sharding import PartitionSpec as P
+import functools
 
 D = 1024
 C = 4096
 BLOCK = 128
+
+MESH = pl.DeviceIdType.MESH
+
+def _grad_kernel(n, ncls, scale, limit, part_ref, out_ref, recv, gath, nrm_dp, nrm_cls,
+                 send_a, recv_a, send_b, recv_b, send_c, recv_c, send_d, recv_d):
+    me = lax.axis_index("dp")
+    cj = lax.axis_index("class")
+    rows = part_ref.shape[0] // n
+
+    def peer(d):
+        return lax.rem(me + d, n)
+
+    barrier = pltpu.get_barrier_semaphore()
+
+    def greet(d, c):
+        pl.semaphore_signal(barrier, 1, device_id=(peer(d), cj), device_id_type=MESH)
+        return c
+    lax.fori_loop(1, n, greet, 0)
+    for e in range(1, ncls):
+        pl.semaphore_signal(barrier, 1, device_id=(me, lax.rem(cj + e, ncls)), device_id_type=MESH)
+    pl.semaphore_wait(barrier, n - 1 + ncls - 1)
+
+    def slot(i):
+        return pl.ds(pl.multiple_of(i * rows, rows), rows)
+
+    def rs_desc(t, s):
+        return pltpu.make_async_remote_copy(
+            src_ref=part_ref.at[slot(t)], dst_ref=recv.at[slot(s)],
+            send_sem=send_a.at[t], recv_sem=recv_a.at[s],
+            device_id=(t, cj), device_id_type=MESH)
+
+    def rs_start(d, c):
+        rs_desc(peer(d), me).start()
+        return c
+    lax.fori_loop(1, n, rs_start, 0)
+
+    def rs_wait(d, c):
+        rs_desc(peer(d), me).wait_send()
+        rs_desc(me, peer(d)).wait_recv()
+        return c
+    lax.fori_loop(1, n, rs_wait, 0)
+
+    def add(d, acc):
+        return acc + recv[slot(peer(d)), :]
+    acc = lax.fori_loop(1, n, add, part_ref[slot(me), :])
+    summed = acc * scale
+    sq = jnp.sum(summed * summed, axis=(0, 1), keepdims=True)
+    nrm_dp[me] = jnp.broadcast_to(sq, nrm_dp.shape[1:])
+
+    def b_desc(t, s):
+        return pltpu.make_async_remote_copy(
+            src_ref=nrm_dp.at[s], dst_ref=nrm_dp.at[s],
+            send_sem=send_b.at[t], recv_sem=recv_b.at[s],
+            device_id=(t, cj), device_id_type=MESH)
+
+    def b_start(d, c):
+        b_desc(peer(d), me).start()
+        return c
+    lax.fori_loop(1, n, b_start, 0)
+
+    def b_wait(d, c):
+        b_desc(peer(d), me).wait_send()
+        b_desc(me, peer(d)).wait_recv()
+        return c
+    lax.fori_loop(1, n, b_wait, 0)
+
+    def b_add(d, acc):
+        return acc + nrm_dp[peer(d)]
+    col = lax.fori_loop(1, n, b_add, nrm_dp[me])
+    nrm_cls[cj] = col
+
+    def c_desc(t, s):
+        return pltpu.make_async_remote_copy(
+            src_ref=nrm_cls.at[s], dst_ref=nrm_cls.at[s],
+            send_sem=send_c.at[t], recv_sem=recv_c.at[s],
+            device_id=(me, t), device_id_type=MESH)
+
+    for e in range(1, ncls):
+        c_desc(lax.rem(cj + e, ncls), cj).start()
+    for e in range(1, ncls):
+        c_desc(lax.rem(cj + e, ncls), cj).wait_send()
+        c_desc(cj, lax.rem(cj + e, ncls)).wait_recv()
+    tot = col
+    for e in range(1, ncls):
+        tot = tot + nrm_cls[lax.rem(cj + e, ncls)]
+    factor = jnp.minimum(1.0, limit / jnp.sqrt(tot))
+    fac = jnp.broadcast_to(factor[0:1, 0:1], summed.shape)
+    gath[slot(me), :] = (summed * fac).astype(gath.dtype)
+
+    def d_desc(t, s):
+        return pltpu.make_async_remote_copy(
+            src_ref=gath.at[slot(s)], dst_ref=gath.at[slot(s)],
+            send_sem=send_d.at[t], recv_sem=recv_d.at[s],
+            device_id=(t, cj), device_id_type=MESH)
+
+    def d_start(d, c):
+        d_desc(peer(d), me).start()
+        return c
+    lax.fori_loop(1, n, d_start, 0)
+
+    def d_wait(d, c):
+        d_desc(peer(d), me).wait_send()
+        d_desc(me, peer(d)).wait_recv()
+        return c
+    lax.fori_loop(1, n, d_wait, 0)
+    out_ref[...] = gath[...]
+
+
+def grad_reduce(part_grad, n, ncls, scale, limit):
+    width = part_grad.shape[1]
+    total_rows = part_grad.shape[0]
+    return pl.pallas_call(
+        functools.partial(_grad_kernel, n, ncls, scale, limit),
+        out_shape=jax.ShapeDtypeStruct((total_rows, width), jnp.bfloat16),
+        in_specs=[pl.BlockSpec(memory_space=pltpu.VMEM)],
+        out_specs=pl.BlockSpec(memory_space=pltpu.VMEM),
+        scratch_shapes=[
+            pltpu.VMEM((total_rows, width), jnp.float32),
+            pltpu.VMEM((total_rows, width), jnp.bfloat16),
+            pltpu.VMEM((n, 8, 128), jnp.float32),
+            pltpu.VMEM((ncls, 8, 128), jnp.float32),
+            pltpu.SemaphoreType.DMA((n,)), pltpu.SemaphoreType.DMA((n,)),
+            pltpu.SemaphoreType.DMA((n,)), pltpu.SemaphoreType.DMA((n,)),
+            pltpu.SemaphoreType.DMA((ncls,)), pltpu.SemaphoreType.DMA((ncls,)),
+            pltpu.SemaphoreType.DMA((n,)), pltpu.SemaphoreType.DMA((n,)),
+        ],
+        compiler_params=pltpu.CompilerParams(collective_id=0, has_side_effects=True),
+    )(part_grad)
 
 
 def _combine_stats(local_max, local_sum):
@@ -74,10 +205,7 @@
     )
     scale = 1.0 / math.sqrt(rows * dp_count)
     limit = 0.5 * math.sqrt(D * C)
-    summed = lax.psum_scatter(part_grad, "dp", scatter_dimension=0, tiled=True) * scale
-    squared = lax.psum(jnp.sum(summed * summed), ("dp", "class"))
-    factor = jnp.minimum(1.0, limit / jnp.sqrt(squared))
-    head_grad = lax.all_gather((summed * factor).astype(jnp.bfloat16), "dp", axis=0, tiled=True)
+    head_grad = grad_reduce(part_grad, dp_count, lax.axis_size("class"), scale, limit)
     return (target.astype(jnp.bfloat16), head_grad)
 
 

time: 645 us -> 412 us (0.64)
  waiting for transfers between devices: 293 us -> 65.4 us
  Pallas kernels: 0 us -> 112 us
  blocking collectives: 184 us -> 83.4 us
  between operations: 15 us -> 0.86 us
    reduce_scatter x1 -> x0, waiting for transfers between devices: 148 us -> none  [on_device(): lax.psum_scatter(part_grad, 'dp', scatter_dimension=0, tiled=True) * scale]
    pallas_call x0 -> x1, Pallas kernels: none -> 112 us  [grad_reduce(): pl.pallas_call(functools.partial(_grad_kernel, n, ncls, scale, limit), ou...]
    psum x1 -> x0, blocking collectives: 100 us -> none  [on_device(): squared = lax.psum(jnp.sum(summed * summed), ('dp', 'class'))]
    all_gather x1 -> x0, waiting for transfers between devices: 79.7 us -> none  [on_device(): lax.all_gather((summed * factor).astype(jnp.bfloat16), 'dp', axis=0, tile...]
  transfers between devices with their start and end apart: 4 -> 2, of which waited for: 4 -> 2; matrix products, arithmetic and copies ran while one was open for 16% -> 24% of each run, Pallas kernels for 0% -> 0%
where the time goes in v2:
time: 412 us
  Pallas kernels  112 us (27%)
  blocking collectives  83.4 us (20%)
  waiting for transfers between devices  65.4 us (16%)
  local copies, waits for them, and re-layouts  55 us (13%)
  other arithmetic  50.6 us (12%)
  starting transfers between devices  22.1 us (5%)
  matrix products  21.9 us (5%)
    pallas_call x1, Pallas kernels, grad_reduce(): pl.pallas_call(functools.partial(_grad_kernel, n, ncls, scale, limit), ou...  112 us
    unnamed x6, other arithmetic  47.3 us
    all_to_all x1, waiting for transfers between devices, on_device(): lax.all_to_all(out_emb, 'dp', split_axis=0, concat_axis=0, tiled=True)  44.3 us
    all_gather x2, blocking collectives, _combine_stats(): lax.all_gather(jnp.stack([local_max, local_sum], axis=0), 'class', axis=0)  36.2 us
    gather x1, local copies, waits for them, and re-layouts, on_device(): near = pool_emb[located]  29.2 us
    psum x1, blocking collectives, on_device(): scores = lax.psum(partial_value, 'class')  24.4 us
    all_gather x1, blocking collectives, on_device(): full_emb = lax.all_gather(embeddings, 'class', axis=1, tiled=True)  22.7 us
    all_to_all x1, waiting for transfers between devices, on_device(): lax.all_to_all(out_lab, 'dp', split_axis=0, concat_axis=0, tiled=True)  21.1 us
  transfers between devices with their start and end apart: 2, of which 2 were waited for; matrix products, arithmetic and copies ran while one was open for 24% of the time, Pallas kernels for 0%

profile of v2, /device:TPU:1, one launch (start us, length us, event | category | flops | bytes accessed | tf_op | source)
XLA Modules:
  0.0 411.6 jit_solution(7407478340223445347)
XLA Ops:
  1.4 3.0 gather_fusion
  4.4 14.8 %all-to-all-start = ((bf16[64,128,128]{2,1,0:T(8,128)(2,1)}), bf16[64,128,128]{2,1,0:T(8,128)(2,1)S(1)}, u32[]{:S(2)}, u32[]{:S(2)}) async-start(bf16[64,128,128]{2,1,0:T(8,128)(2,1)} %gather_fusion), calls=%async_computation | async-start | bytes 4194304 | tf_op jit(solution)/shard_map/all_to_all | solution.py:161
  19.3 5.3 %gather_fusion.2 = bf16[64,128,512]{2,1,0:T(8,128)(2,1)} fusion(bf16[2,128,512]{2,1,0:T(8,128)(2,1)S(1)} %bitcast.53, s32[1024]{0:T(1024)S(1)} %pad_clamp_fusion), kind=kCustom, calls=%fused_computation.2 | custom fusion | bytes 16777472 | tf_op jit(solution)/shard_map/gather | solution.py:160
  24.6 44.3 %all-to-all-done = bf16[64,128,128]{2,1,0:T(8,128)(2,1)S(1)} async-done(((bf16[64,128,128]{2,1,0:T(8,128)(2,1)}), bf16[64,128,128]{2,1,0:T(8,128)(2,1)S(1)}, u32[]{:S(2)}, u32[]{:S(2)}) %all-to-all-start) | async-done | bytes 2097184 | tf_op jit(solution)/shard_map/all_to_all | solution.py:161
  68.9 7.2 %all-to-all-start.1 = ((bf16[64,128,512]{2,1,0:T(8,128)(2,1)}), bf16[64,128,512]{2,1,0:T(8,128)(2,1)}, u32[]{:S(2)}, u32[]{:S(2)}) async-start(bf16[64,128,512]{2,1,0:T(8,128)(2,1)} %gather_fusion.2), calls=%async_computation.1 | async-start | bytes 16777216 | tf_op jit(solution)/shard_map/all_to_all | solution.py:162
  78.7 1.6 reshape.99
  80.3 1.0 reshape.85
  81.3 22.7 %all_gather.15 = bf16[256,1024]{1,0:T(8,128)(2,1)S(1)} all-gather(bf16[256,128]{1,0:T(8,128)(2,1)S(1)} %copy-done.2), channel_id=1, replica_groups=mesh['dp'=64,'class'=8] {'class'}, dimensions={1}, use_global_device_ids=true | all-gather | bytes 589824 | tf_op jit(solution)/shard_map/all_gather | solution.py:168
  104.0 0.8 copy-done.4
  105.3 0.8 copy-done.6
  106.3 18.0 %all-gather.2 = f32[8,2,256]{2,1,0:T(2,128)S(1)} all-gather(f32[1,2,256]{2,1,0:T(2,128)S(1)} %maximum_bitcast_fusion), channel_id=2, replica_groups=mesh['dp'=64,'class'=8] {'class'}, dimensions={0}, use_global_device_ids=true | all-gather | bytes 18432 | tf_op jit(solution)/shard_map/all_gather | solution.py:145
  124.4 29.2 %gather_fusion.1 = bf16[8192,128]{1,0:T(8,128)(2,1)} fusion(bf16[8192,128]{1,0:T(8,128)(2,1)S(1)} %bitcast.54, s32[8192]{0:T(1024)S(1)} %broadcast_clamp_fusion), kind=kCustom, calls=%fused_computation.1 | custom fusion | bytes 4227072 | tf_op jit(solution)/shard_map/gather | solution.py:176
  153.6 2.8 fusion.20
  156.4 24.4 %psum.7 = f32[256,32]{1,0:T(8,128)S(1)} all-reduce(f32[256,32]{1,0:T(8,128)S(1)} %bitcast.60), channel_id=1, replica_groups=mesh['dp'=64,'class'=8] {'class'}, use_global_device_ids=true, to_apply=%region_0.0 | all-reduce | flops 8192 | bytes 65536 | tf_op jit(solution)/shard_map/psum | solution.py:180
  181.5 47.1 %scatter_custom_fusion = f32[2097152]{0:T(1024)} fusion(s32[8192]{0:T(1024)} %reshape.99, f32[8192]{0:T(1024)S(1)} %reshape.101, f32[]{:T(128)} %constant.10.clone.1), kind=kCustom, calls=%fused_computation.6 | custom fusion | flops 8192 | bytes 8389120
  228.6 9.4 %reshape.74 = f32[256,8192]{1,0:T(8,128)} reshape(f32[2097152]{0:T(1024)} %scatter_custom_fusion) | data formatting | bytes 16777216 | tf_op jit(solution)/shard_map/scatter-add | solution.py:188
  238.0 21.1 %all-to-all-done.1 = bf16[64,128,512]{2,1,0:T(8,128)(2,1)} async-done(((bf16[64,128,512]{2,1,0:T(8,128)(2,1)}), bf16[64,128,512]{2,1,0:T(8,128)(2,1)}, u32[]{:S(2)}, u32[]{:S(2)}) %all-to-all-start.1) | async-done | bytes 8388640 | tf_op jit(solution)/shard_map/all_to_all | solution.py:162
  259.1 10.6 %fusion = f32[256,512]{1,0:T(8,128)S(1)} fusion(bf16[8192,512]{1,0:T(8,128)(2,1)} %bitcast.10, f32[256,8192]{1,0:T(8,128)} %reshape.74), kind=kOutput, calls=%fused_computation.5 | convolution fusion | flops 2155872256 | bytes 17301504 | tf_op jit(solution)/shard_map/dot_general | solution.py:193
  269.8 5.9 %fusion.33 = (f32[256]{0:T(256)S(1)}, f32[256,512]{1,0:T(8,128)S(1)}) fusion(bf16[256,512]{1,0:T(8,128)(2,1)S(1)} %copy-done.1, f32[256,512]{1,0:T(8,128)S(1)} %fusion, bf16[8192,512]{1,0:T(8,128)(2,1)} %bitcast.10, f32[256,8192]{1,0:T(8,128)S(1)} %copy-done.3), kind=kOutput, calls=%fused_computation.56 | convolution fusion | flops 2150235904 | bytes 18088960 | tf_op jit(solution)/shard_map/dot_general | solution.py:193
  275.7 0.9 exponential_reduce_fusion
  276.5 18.2 %all-gather.3 = f32[8,2,256]{2,1,0:T(2,128)S(1)} all-gather(f32[1,2,256]{2,1,0:T(2,128)S(1)} %maximum_bitcast_fusion.1), channel_id=3, replica_groups=mesh['dp'=64,'class'=8] {'class'}, dimensions={0}, use_global_device_ids=true | all-gather | bytes 18432 | tf_op jit(solution)/shard_map/all_gather | solution.py:145
  294.9 2.1 convolution_bitcast_fusion.part_ref
  296.9 112.4 %shard_map.86 = bf16[1024,512]{1,0:T(8,128)(2,1)} custom-call(f32[1024,512]{1,0:T(8,128)} %convolution_bitcast_fusion.part_ref), custom_call_target="tpu_custom_call" | custom-call | tf_op jit(solution)/shard_map/pallas_call | solution.py:125
  409.4 2.3 copy.43
  (44 shorter events, 4.8 us)
Async XLA Ops:
  0.6 104.1 %copy-start = (bf16[1024,512]{1,0:T(8,128)(2,1)S(1)}, bf16[1024,512]{1,0:T(8,128)(2,1)}, u32[]{:S(2)}) copy-start(bf16[1024,512]{1,0:T(8,128)(2,1)} %param.9) | copy-start | bytes 3145732
  0.6 18.6 %copy-start.1 = (bf16[256,512]{1,0:T(8,128)(2,1)S(1)}, bf16[256,512]{1,0:T(8,128)(2,1)}, u32[]{:S(2)}) copy-start(bf16[256,512]{1,0:T(8,128)(2,1)} %param.8) | copy-start | bytes 786436
  4.4 64.5 %all-to-all-start = ((bf16[64,128,128]{2,1,0:T(8,128)(2,1)}), bf16[64,128,128]{2,1,0:T(8,128)(2,1)S(1)}, u32[]{:S(2)}, u32[]{:S(2)}) async-start(bf16[64,128,128]{2,1,0:T(8,128)(2,1)} %gather_fusion), calls=%async_computation | async-start | bytes 4194304 | tf_op jit(solution)/shard_map/all_to_all | solution.py:161
  24.6 51.6 %copy-start.8 = (s32[256,32]{0,1:T(8,128)S(1)}, s32[256,32]{0,1:T(8,128)}, u32[]{:S(2)}) copy-start(s32[256,32]{0,1:T(8,128)} %param.12) | copy-start | bytes 98308
  24.6 53.1 %copy-start.10 = (s32[2]{0:T(128)S(1)}, s32[2]{0:T(128)}, u32[]{:S(2)}) copy-start(s32[2]{0:T(128)} %constant.27) | copy-start | bytes 28
  24.6 53.2 %copy-start.11 = (s32[2]{0:T(128)S(1)}, s32[2]{0:T(128)}, u32[]{:S(2)}) copy-start(s32[2]{0:T(128)} %constant.30) | copy-start | bytes 28
  24.6 56.7 %copy-start.2 = (bf16[256,128]{1,0:T(8,128)(2,1)S(1)}, bf16[256,128]{1,0:T(8,128)(2,1)}, u32[]{:S(2)}) copy-start(bf16[256,128]{1,0:T(8,128)(2,1)} %param.7) | copy-start | bytes 196612
  68.9 190.1 %all-to-all-start.1 = ((bf16[64,128,512]{2,1,0:T(8,128)(2,1)}), bf16[64,128,512]{2,1,0:T(8,128)(2,1)}, u32[]{:S(2)}, u32[]{:S(2)}) async-start(bf16[64,128,512]{2,1,0:T(8,128)(2,1)} %gather_fusion.2), calls=%async_computation.1 | async-start | bytes 16777216 | tf_op jit(solution)/shard_map/all_to_all | solution.py:162
  104.0 0.8 copy-start.4
  105.3 0.8 copy-start.6
  124.4 56.4 %copy-start.9 = (s32[256]{0:T(256)S(1)}, s32[256]{0:T(256)}, u32[]{:S(2)}) copy-start(s32[256]{0:T(256)} %param.13) | copy-start | bytes 3076
  259.1 10.6 %copy-start.3 = (f32[256,8192]{1,0:T(8,128)S(1)}, f32[256,8192]{1,0:T(8,128)}, u32[]{:S(2)}) copy-start(f32[256,8192]{1,0:T(8,128)} %reshape.74) | copy-start | bytes 25165828
  269.7 25.1 %copy-start.5 = (bf16[256,1024]{1,0:T(8,128)(2,1)S(1)}, bf16[256,1024]{1,0:T(8,128)(2,1)}, u32[]{:S(2)}) copy-start(bf16[256,1024]{1,0:T(8,128)(2,1)} %copy-done.4) | copy-start | bytes 1572868
  269.7 25.1 %copy-start.7 = (f32[256,512]{1,0:T(8,128)S(1)}, f32[256,512]{1,0:T(8,128)}, u32[]{:S(2)}) copy-start(f32[256,512]{1,0:T(8,128)} %copy-done.6) | copy-start | bytes 1572868

commit v3 on v1

--- a/solution.py
+++ b/solution.py
@@ -3,15 +3,239 @@
 import jax
 import jax.numpy as jnp
 from jax import lax
+from jax.experimental import pallas as pl
+from jax.experimental.pallas import tpu as pltpu
 from jax.sharding import PartitionSpec as P
+import functools
 
 D = 1024
 C = 4096
 BLOCK = 128
 
-
-def _combine_stats(local_max, local_sum):
-    both = lax.all_gather(jnp.stack([local_max, local_sum], axis=0), "class", axis=0)
+MESH = pl.DeviceIdType.MESH
+
+def _grad_kernel(nk, nx, nz, ncls, scale, limit, part_ref, out_ref,
+                 recv1, acc1, recv2, acc2, recv3, gath, nrm_dp, nrm_cls,
+                 s1, r1, s2, r2, s3, r3, sb, rb, sc, rc, g3s, g3r, g2s, g2r, g1s, g1r):
+    n = nk * nx * nz
+    me = lax.axis_index("dp")
+    cj = lax.axis_index("class")
+    kc = lax.rem(me, nk)
+    xc = lax.rem(me // nk, nx)
+    zc = me // (nk * nx)
+    total = part_ref.shape[0]
+    half = total // nk
+    quarter = half // nx
+    piece = quarter // nz
+
+    def dev(z, x, k):
+        return ((z * nx + x) * nk + k, cj)
+
+    def rows(start, size):
+        return pl.ds(pl.multiple_of(start, size), size)
+
+    barrier = pltpu.get_barrier_semaphore()
+
+    def greet(d, c):
+        pl.semaphore_signal(barrier, 1, device_id=(lax.rem(me + d, n), cj), device_id_type=MESH)
+        return c
+    lax.fori_loop(1, n, greet, 0)
+    for e in range(1, ncls):
+        pl.semaphore_signal(barrier, 1, device_id=(me, lax.rem(cj + e, ncls)), device_id_type=MESH)
+    pl.semaphore_wait(barrier, n - 1 + ncls - 1)
+
+    def exchange(peers, make):
+        for p in peers:
+            make(p, True).start()
+        for p in peers:
+            make(p, True).wait_send()
+            make(p, False).wait_recv()
+
+    k_peers = [lax.rem(kc + e, nk) for e in range(1, nk)]
+
+    def m1(p, mine):
+        if mine:
+            return pltpu.make_async_remote_copy(
+                src_ref=part_ref.at[rows(p * half, half)], dst_ref=recv1.at[kc],
+                send_sem=s1.at[p], recv_sem=r1.at[kc], device_id=dev(zc, xc, p), device_id_type=MESH)
+        return pltpu.make_async_remote_copy(
+            src_ref=part_ref.at[rows(kc * half, half)], dst_ref=recv1.at[p],
+            send_sem=s1.at[kc], recv_sem=r1.at[p], device_id=dev(zc, xc, p), device_id_type=MESH)
+    exchange(k_peers, m1)
+    a1 = part_ref[rows(kc * half, half), :]
+    for p in k_peers:
+        a1 = a1 + recv1[p]
+    acc1[...] = a1
+
+    x_peers = [lax.rem(xc + e, nx) for e in range(1, nx)]
+
+    def m2(p, mine):
+        if mine:
+            return pltpu.make_async_remote_copy(
+                src_ref=acc1.at[rows(p * quarter, quarter)], dst_ref=recv2.at[xc],
+                send_sem=s2.at[p], recv_sem=r2.at[xc], device_id=dev(zc, p, kc), device_id_type=MESH)
+        return pltpu.make_async_remote_copy(
+            src_ref=acc1.at[rows(xc * quarter, quarter)], dst_ref=recv2.at[p],
+            send_sem=s2.at[xc], recv_sem=r2.at[p], device_id=dev(zc, p, kc), device_id_type=MESH)
+    exchange(x_peers, m2)
+    a2 = acc1[rows(xc * quarter, quarter), :]
+    for p in x_peers:
+        a2 = a2 + recv2[p]
+    acc2[...] = a2
+
+    z_peers = [lax.rem(zc + e, nz) for e in range(1, nz)]
+
+    def m3(p, mine):
+        if mine:
+            return pltpu.make_async_remote_copy(
+                src_ref=acc2.at[rows(p * piece, piece)], dst_ref=recv3.at[zc],
+                send_sem=s3.at[p], recv_sem=r3.at[zc], device_id=dev(p, xc, kc), device_id_type=MESH)
+        return pltpu.make_async_remote_copy(
+            src_ref=acc2.at[rows(zc * piece, piece)], dst_ref=recv3.at[p],
+            send_sem=s3.at[zc], recv_sem=r3.at[p], device_id=dev(p, xc, kc), device_id_type=MESH)
+    exchange(z_peers, m3)
+    a3 = acc2[rows(zc * piece, piece), :]
+    for p in z_peers:
+        a3 = a3 + recv3[p]
+    summed = a3 * scale
+
+    sq = jnp.sum(summed * summed, axis=(0, 1), keepdims=True)
+    nrm_dp[me] = jnp.broadcast_to(sq, nrm_dp.shape[1:])
+
+    def b_desc(t, s):
+        return pltpu.make_async_remote_copy(
+            src_ref=nrm_dp.at[s], dst_ref=nrm_dp.at[s],
+            send_sem=sb.at[t], recv_sem=rb.at[s],
+            device_id=(t, cj), device_id_type=MESH)
+
+    def b_start(d, c):
+        b_desc(lax.rem(me + d, n), me).start()
+        return c
+    lax.fori_loop(1, n, b_start, 0)
+
+    def b_wait(d, c):
+        b_desc(lax.rem(me + d, n), me).wait_send()
+        b_desc(me, lax.rem(me + d, n)).wait_recv()
+        return c
+    lax.fori_loop(1, n, b_wait, 0)
+
+    def b_add(d, acc):
+        return acc + nrm_dp[lax.rem(me + d, n)]
+    col = lax.fori_loop(1, n, b_add, nrm_dp[me])
+    nrm_cls[cj] = col
+
+    def c_desc(t, s):
+        return pltpu.make_async_remote_copy(
+            src_ref=nrm_cls.at[s], dst_ref=nrm_cls.at[s],
+            send_sem=sc.at[t], recv_sem=rc.at[s],
+            device_id=(me, t), device_id_type=MESH)
+
+    c_peers = [lax.rem(cj + e, ncls) for e in range(1, ncls)]
+    for t in c_peers:
+        c_desc(t, cj).start()
+    for t in c_peers:
+        c_desc(t, cj).wait_send()
+        c_desc(cj, t).wait_recv()
+    tot = col
+    for t in c_peers:
+        tot = tot + nrm_cls[t]
+    factor = jnp.minimum(1.0, limit / jnp.sqrt(tot))
+    fac = jnp.broadcast_to(factor[0:1, 0:1], summed.shape)
+    own = kc * half + xc * quarter + zc * piece
+    gath[rows(own, piece), :] = (summed * fac).astype(gath.dtype)
+
+    def g3(p, mine):
+        src = own if mine else kc * half + xc * quarter + p * piece
+        return pltpu.make_async_remote_copy(
+            src_ref=gath.at[rows(src, piece)], dst_ref=gath.at[rows(src, piece)],
+            send_sem=g3s.at[p], recv_sem=g3r.at[zc if mine else p],
+            device_id=dev(p, xc, kc), device_id_type=MESH)
+    exchange(z_peers, g3)
+
+    def g2(p, mine):
+        src = kc * half + (xc if mine else p) * quarter
+        return pltpu.make_async_remote_copy(
+            src_ref=gath.at[rows(src, quarter)], dst_ref=gath.at[rows(src, quarter)],
+            send_sem=g2s.at[p], recv_sem=g2r.at[xc if mine else p],
+            device_id=dev(zc, p, kc), device_id_type=MESH)
+    exchange(x_peers, g2)
+
+    def g1(p, mine):
+        src = (kc if mine else p) * half
+        return pltpu.make_async_remote_copy(
+            src_ref=gath.at[rows(src, half)], dst_ref=gath.at[rows(src, half)],
+            send_sem=g1s.at[p], recv_sem=g1r.at[kc if mine else p],
+            device_id=dev(zc, xc, p), device_id_type=MESH)
+    exchange(k_peers, g1)
+    out_ref[...] = gath[...]
+
+
+def grad_reduce(part_grad, n, ncls, scale, limit, nk=2, nx=4):
+    nz = n // (nk * nx)
+    width = part_grad.shape[1]
+    total = part_grad.shape[0]
+    half = total // nk
+    quarter = half // nx
+    piece = quarter // nz
+    dma = pltpu.SemaphoreType.DMA
+    return pl.pallas_call(
+        functools.partial(_grad_kernel, nk, nx, nz, ncls, scale, limit),
+        out_shape=jax.ShapeDtypeStruct((total, width), jnp.bfloat16),
+        in_specs=[pl.BlockSpec(memory_space=pltpu.VMEM)],
+        out_specs=pl.BlockSpec(memory_space=pltpu.VMEM),
+        scratch_shapes=[
+            pltpu.VMEM((nk, half, width), jnp.float32),
+            pltpu.VMEM((half, width), jnp.float32),
+            pltpu.VMEM((nx, quarter, width), jnp.float32),
+            pltpu.VMEM((quarter, width), jnp.float32),
+            pltpu.VMEM((nz, piece, width), jnp.float32),
+            pltpu.VMEM((total, width), jnp.bfloat16),
+            pltpu.VMEM((n, 8, 128), jnp.float32),
+            pltpu.VMEM((ncls, 8, 128), jnp.float32),
+            dma((nk,)), dma((nk,)), dma((nx,)), dma((nx,)), dma((nz,)), dma((nz,)),
+            dma((n,)), dma((n,)), dma((ncls,)), dma((ncls,)),
+            dma((nz,)), dma((nz,)), dma((nx,)), dma((nx,)), dma((nk,)), dma((nk,)),
+        ],
+        compiler_params=pltpu.CompilerParams(collective_id=0, has_side_effects=True),
+    )(part_grad)
+
+
+def _class_gather_kernel(ncls, x_ref, out_ref, buf, ssem, rsem):
+    me = lax.axis_index("dp")
+    cj = lax.axis_index("class")
+    peers = [lax.rem(cj + e, ncls) for e in range(1, ncls)]
+    barrier = pltpu.get_barrier_semaphore()
+    for t in peers:
+        pl.semaphore_signal(barrier, 1, device_id=(me, t), device_id_type=MESH)
+    pl.semaphore_wait(barrier, ncls - 1)
+
+    def desc(t, s):
+        return pltpu.make_async_remote_copy(
+            src_ref=x_ref, dst_ref=buf.at[s], send_sem=ssem.at[t], recv_sem=rsem.at[s],
+            device_id=(me, t), device_id_type=MESH)
+    for t in peers:
+        desc(t, cj).start()
+    buf[cj] = x_ref[...]
+    for t in peers:
+        desc(t, cj).wait_send()
+        desc(cj, t).wait_recv()
+    out_ref[...] = buf[...]
+
+
+def class_gather(x, ncls, cid):
+    dma = pltpu.SemaphoreType.DMA
+    return pl.pallas_call(
+        functools.partial(_class_gather_kernel, ncls),
+        out_shape=jax.ShapeDtypeStruct((ncls,) + x.shape, x.dtype),
+        in_specs=[pl.BlockSpec(memory_space=pltpu.VMEM)],
+        out_specs=pl.BlockSpec(memory_space=pltpu.VMEM),
+        scratch_shapes=[pltpu.VMEM((ncls,) + x.shape, x.dtype), dma((ncls,)), dma((ncls,))],
+        compiler_params=pltpu.CompilerParams(collective_id=cid, has_side_effects=True),
+    )(x)
+
+
+def _combine_stats(local_max, local_sum, cid):
+    both = class_gather(jnp.stack([local_max, local_sum], axis=0), lax.axis_size("class"), cid)
     maxes, sums = both[:, 0], both[:, 1]
     top = jnp.max(maxes, axis=0)
     total = jnp.sum(sums * jnp.exp(maxes - top[None, :]), axis=0)
@@ -39,6 +263,7 @@
     h_top, h_total = _combine_stats(
         jnp.max(head, axis=1),
         jnp.sum(jnp.exp(head - jnp.max(head, axis=1, keepdims=True)), axis=1),
+        1,
     )
     prob_head = jnp.exp(head - h_top[:, None]) / h_total[:, None]
 
@@ -65,7 +290,7 @@
     target = 4.0 * spread + labels.astype(jnp.float32)
     z_local = jnp.max(target, axis=1)
     z_top, z_total = _combine_stats(
-        z_local, jnp.sum(jnp.exp(target - z_local[:, None]), axis=1)
+        z_local, jnp.sum(jnp.exp(target - z_local[:, None]), axis=1), 2
     )
     prob_target = jnp.exp(target - z_top[:, None]) / z_total[:, None]
     diff = (C * (prob_head - prob_target)).astype(jnp.bfloat16)
@@ -74,10 +299,7 @@
     )
     scale = 1.0 / math.sqrt(rows * dp_count)
     limit = 0.5 * math.sqrt(D * C)
-    summed = lax.psum_scatter(part_grad, "dp", scatter_dimension=0, tiled=True) * scale
-    squared = lax.psum(jnp.sum(summed * summed), ("dp", "class"))
-    factor = jnp.minimum(1.0, limit / jnp.sqrt(squared))
-    head_grad = lax.all_gather((summed * factor).astype(jnp.bfloat16), "dp", axis=0, tiled=True)
+    head_grad = grad_reduce(part_grad, dp_count, lax.axis_size("class"), scale, limit)
     return (target.astype(jnp.bfloat16), head_grad)
 
 

time: 645 us -> 364 us (0.56)
  waiting for transfers between devices: 293 us -> 72.2 us
  blocking collectives: 184 us -> 48 us
  Pallas kernels: 0 us -> 89.6 us
  between operations: 15 us -> 0.87 us
    reduce_scatter x1 -> x0, waiting for transfers between devices: 148 us -> none  [on_device(): lax.psum_scatter(part_grad, 'dp', scatter_dimension=0, tiled=True) * scale]
    psum x1 -> x0, blocking collectives: 100 us -> none  [on_device(): squared = lax.psum(jnp.sum(summed * summed), ('dp', 'class'))]
    pallas_call x0 -> x3, Pallas kernels: none -> 89.6 us  [the longest x1 71.4 us: grad_reduce(): pl.pallas_call(functools.partial(_grad_kernel, nk, nx, nz, ncls, scale, l...]
    all_gather x1 -> x0, waiting for transfers between devices: 79.7 us -> none  [on_device(): lax.all_gather((summed * factor).astype(jnp.bfloat16), 'dp', axis=0, tile...]
    all_gather x2 -> x0, blocking collectives: 36.2 us -> none  [_combine_stats(): lax.all_gather(jnp.stack([local_max, local_sum], axis=0), 'class', axis=0)]
    all_to_all x1, waiting for transfers between devices: 21 us -> 27.9 us  [on_device(): lax.all_to_all(out_lab, 'dp', split_axis=0, concat_axis=0, tiled=True)]
    unnamed x6 -> x4, other arithmetic: 47.3 us -> 47.3 us
  transfers between devices with their start and end apart: 4 -> 2, of which waited for: 4 -> 2; matrix products, arithmetic and copies ran while one was open for 16% -> 28% of each run, Pallas kernels for 0% -> 2%
where the time goes in v3:
time: 364 us; the launch traced here: 363 us
  Pallas kernels  89.6 us (25%)
  waiting for transfers between devices  72.2 us (20%)
  local copies, waits for them, and re-layouts  55.1 us (15%)
  other arithmetic  53.3 us (15%)
  blocking collectives  48 us (13%)
  starting transfers between devices  22.1 us (6%)
  matrix products  21.9 us (6%)
    pallas_call x1, Pallas kernels, grad_reduce(): pl.pallas_call(functools.partial(_grad_kernel, nk, nx, nz, ncls, scale, l...  71.4 us
    unnamed x4, other arithmetic  47.3 us
    all_to_all x1, waiting for transfers between devices, on_device(): lax.all_to_all(out_emb, 'dp', split_axis=0, concat_axis=0, tiled=True)  44.2 us
    gather x1, local copies, waits for them, and re-layouts, on_device(): near = pool_emb[located]  29.2 us
    all_to_all x1, waiting for transfers between devices, on_device(): lax.all_to_all(out_lab, 'dp', split_axis=0, concat_axis=0, tiled=True)  27.9 us
    psum x1, blocking collectives, on_device(): scores = lax.psum(partial_value, 'class')  25.3 us
    all_gather x1, blocking collectives, on_device(): full_emb = lax.all_gather(embeddings, 'class', axis=1, tiled=True)  22.7 us
    pallas_call x2, Pallas kernels, class_gather(): pl.pallas_call(functools.partial(_class_gather_kernel, ncls), out_shape=j...  18.2 us
  transfers between devices with their start and end apart: 2, of which 2 were waited for; matrix products, arithmetic and copies ran while one was open for 28% of the time, Pallas kernels for 2%

profile of v3, /device:TPU:1, one launch (start us, length us, event | category | flops | bytes accessed | tf_op | source)
XLA Modules:
  0.0 363.0 jit_solution(14607447304454875348)
XLA Ops:
  1.4 3.0 gather_fusion
  4.4 14.8 %all-to-all-start = ((bf16[64,128,128]{2,1,0:T(8,128)(2,1)}), bf16[64,128,128]{2,1,0:T(8,128)(2,1)S(1)}, u32[]{:S(2)}, u32[]{:S(2)}) async-start(bf16[64,128,128]{2,1,0:T(8,128)(2,1)} %gather_fusion), calls=%async_computation | async-start | bytes 4194304 | tf_op jit(solution)/shard_map/all_to_all | solution.py:254
  19.3 5.4 %gather_fusion.2 = bf16[64,128,512]{2,1,0:T(8,128)(2,1)} fusion(bf16[2,128,512]{2,1,0:T(8,128)(2,1)S(1)} %bitcast.49, s32[1024]{0:T(1024)S(1)} %pad_clamp_fusion), kind=kCustom, calls=%fused_computation.2 | custom fusion | bytes 16777472 | tf_op jit(solution)/shard_map/gather | solution.py:253
  24.7 44.2 %all-to-all-done = bf16[64,128,128]{2,1,0:T(8,128)(2,1)S(1)} async-done(((bf16[64,128,128]{2,1,0:T(8,128)(2,1)}), bf16[64,128,128]{2,1,0:T(8,128)(2,1)S(1)}, u32[]{:S(2)}, u32[]{:S(2)}) %all-to-all-start) | async-done | bytes 2097184 | tf_op jit(solution)/shard_map/all_to_all | solution.py:254
  68.9 7.2 %all-to-all-start.1 = ((bf16[64,128,512]{2,1,0:T(8,128)(2,1)}), bf16[64,128,512]{2,1,0:T(8,128)(2,1)}, u32[]{:S(2)}, u32[]{:S(2)}) async-start(bf16[64,128,512]{2,1,0:T(8,128)(2,1)} %gather_fusion.2), calls=%async_computation.1 | async-start | bytes 16777216 | tf_op jit(solution)/shard_map/all_to_all | solution.py:255
  78.7 1.6 reshape.99
  80.3 1.0 reshape.85
  81.3 22.7 %all_gather.3 = bf16[256,1024]{1,0:T(8,128)(2,1)S(1)} all-gather(bf16[256,128]{1,0:T(8,128)(2,1)S(1)} %copy-done.2), channel_id=1, replica_groups=mesh['dp'=64,'class'=8] {'class'}, dimensions={1}, use_global_device_ids=true | all-gather | bytes 589824 | tf_op jit(solution)/shard_map/all_gather | solution.py:261
  106.9 8.9 %shard_map.86 = f32[8,2,256]{2,1,0:T(2,128)} custom-call(f32[2,256]{1,0:T(2,128)} %pad_maximum_fusion.x_ref), custom_call_target="tpu_custom_call" | custom-call | tf_op jit(solution)/shard_map/pallas_call | solution.py:227
  115.9 0.8 slice_reduce_fusion.1
  116.7 29.2 %gather_fusion.1 = bf16[8192,128]{1,0:T(8,128)(2,1)} fusion(bf16[8192,128]{1,0:T(8,128)(2,1)S(1)} %bitcast.50, s32[8192]{0:T(1024)S(1)} %broadcast_clamp_fusion), kind=kCustom, calls=%fused_computation.1 | custom fusion | bytes 4227072 | tf_op jit(solution)/shard_map/gather | solution.py:270
  146.0 2.8 fusion.20
  148.7 25.3 %psum.7 = f32[256,32]{1,0:T(8,128)S(1)} all-reduce(f32[256,32]{1,0:T(8,128)S(1)} %bitcast.56), channel_id=1, replica_groups=mesh['dp'=64,'class'=8] {'class'}, use_global_device_ids=true, to_apply=%region_0.0 | all-reduce | flops 8192 | bytes 65536 | tf_op jit(solution)/shard_map/psum | solution.py:274
  174.7 47.1 %scatter_custom_fusion = f32[2097152]{0:T(1024)} fusion(s32[8192]{0:T(1024)} %reshape.99, f32[8192]{0:T(1024)S(1)} %reshape.101, f32[]{:T(128)} %constant.10.clone.1), kind=kCustom, calls=%fused_computation.6 | custom fusion | flops 8192 | bytes 8389120
  221.8 9.4 %reshape.74 = f32[256,8192]{1,0:T(8,128)} reshape(f32[2097152]{0:T(1024)} %scatter_custom_fusion) | data formatting | bytes 16777216 | tf_op jit(solution)/shard_map/scatter-add | solution.py:282
  231.2 27.9 %all-to-all-done.1 = bf16[64,128,512]{2,1,0:T(8,128)(2,1)} async-done(((bf16[64,128,512]{2,1,0:T(8,128)(2,1)}), bf16[64,128,512]{2,1,0:T(8,128)(2,1)}, u32[]{:S(2)}, u32[]{:S(2)}) %all-to-all-start.1) | async-done | bytes 8388640 | tf_op jit(solution)/shard_map/all_to_all | solution.py:255
  259.1 10.6 %fusion = f32[256,512]{1,0:T(8,128)S(1)} fusion(bf16[8192,512]{1,0:T(8,128)(2,1)} %bitcast.10, f32[256,8192]{1,0:T(8,128)} %reshape.74), kind=kOutput, calls=%fused_computation.5 | convolution fusion | flops 2155872256 | bytes 17301504 | tf_op jit(solution)/shard_map/dot_general | solution.py:287
  269.8 5.9 %fusion.35 = (f32[256]{0:T(256)S(1)}, f32[256,512]{1,0:T(8,128)S(1)}) fusion(bf16[256,512]{1,0:T(8,128)(2,1)S(1)} %copy-done.1, f32[256,512]{1,0:T(8,128)S(1)} %fusion, bf16[8192,512]{1,0:T(8,128)(2,1)} %bitcast.10, f32[256,8192]{1,0:T(8,128)S(1)} %copy-done.3), kind=kOutput, calls=%fused_computation.56 | convolution fusion | flops 2150235904 | bytes 18088960 | tf_op jit(solution)/shard_map/dot_general | solution.py:287
  275.7 0.9 exponential_reduce_fusion
  277.1 9.3 %shard_map.87 = f32[8,2,256]{2,1,0:T(2,128)} custom-call(f32[2,256]{1,0:T(2,128)} %pad_maximum_fusion.1.x_ref), custom_call_target="tpu_custom_call" | custom-call | tf_op jit(solution)/shard_map/pallas_call | solution.py:227
  286.4 0.8 slice_reduce_fusion
  287.3 2.1 convolution_bitcast_fusion.part_ref
  289.4 71.4 %shard_map.88 = bf16[1024,512]{1,0:T(8,128)(2,1)} custom-call(f32[1024,512]{1,0:T(8,128)} %convolution_bitcast_fusion.part_ref), custom_call_target="tpu_custom_call" | custom-call | tf_op jit(solution)/shard_map/pallas_call | solution.py:181
  360.8 2.3 copy.53
  (44 shorter events, 7.5 us)
Async XLA Ops:
  0.6 104.1 %copy-start = (bf16[1024,512]{1,0:T(8,128)(2,1)S(1)}, bf16[1024,512]{1,0:T(8,128)(2,1)}, u32[]{:S(2)}) copy-start(bf16[1024,512]{1,0:T(8,128)(2,1)} %param.9) | copy-start | bytes 3145732
  0.6 18.6 %copy-start.1 = (bf16[256,512]{1,0:T(8,128)(2,1)S(1)}, bf16[256,512]{1,0:T(8,128)(2,1)}, u32[]{:S(2)}) copy-start(bf16[256,512]{1,0:T(8,128)(2,1)} %param.8) | copy-start | bytes 786436
  4.4 64.5 %all-to-all-start = ((bf16[64,128,128]{2,1,0:T(8,128)(2,1)}), bf16[64,128,128]{2,1,0:T(8,128)(2,1)S(1)}, u32[]{:S(2)}, u32[]{:S(2)}) async-start(bf16[64,128,128]{2,1,0:T(8,128)(2,1)} %gather_fusion), calls=%async_computation | async-start | bytes 4194304 | tf_op jit(solution)/shard_map/all_to_all | solution.py:254
  24.7 51.5 %copy-start.8 = (s32[256,32]{0,1:T(8,128)S(1)}, s32[256,32]{0,1:T(8,128)}, u32[]{:S(2)}) copy-start(s32[256,32]{0,1:T(8,128)} %param.12) | copy-start | bytes 98308
  24.7 53.1 %copy-start.10 = (s32[2]{0:T(128)S(1)}, s32[2]{0:T(128)}, u32[]{:S(2)}) copy-start(s32[2]{0:T(128)} %constant.27) | copy-start | bytes 28
  24.7 53.1 %copy-start.11 = (s32[2]{0:T(128)S(1)}, s32[2]{0:T(128)}, u32[]{:S(2)}) copy-start(s32[2]{0:T(128)} %constant.30) | copy-start | bytes 28
  24.7 56.6 %copy-start.2 = (bf16[256,128]{1,0:T(8,128)(2,1)S(1)}, bf16[256,128]{1,0:T(8,128)(2,1)}, u32[]{:S(2)}) copy-start(bf16[256,128]{1,0:T(8,128)(2,1)} %param.7) | copy-start | bytes 196612
  68.9 190.1 %all-to-all-start.1 = ((bf16[64,128,512]{2,1,0:T(8,128)(2,1)}), bf16[64,128,512]{2,1,0:T(8,128)(2,1)}, u32[]{:S(2)}, u32[]{:S(2)}) async-start(bf16[64,128,512]{2,1,0:T(8,128)(2,1)} %gather_fusion.2), calls=%async_computation.1 | async-start | bytes 16777216 | tf_op jit(solution)/shard_map/all_to_all | solution.py:255
  104.0 0.8 copy-start.4
  105.3 0.8 copy-start.6
  116.7 57.3 %copy-start.9 = (s32[256]{0:T(256)S(1)}, s32[256]{0:T(256)}, u32[]{:S(2)}) copy-start(s32[256]{0:T(256)} %param.13) | copy-start | bytes 3076
  259.1 10.6 %copy-start.3 = (f32[256,8192]{1,0:T(8,128)S(1)}, f32[256,8192]{1,0:T(8,128)}, u32[]{:S(2)}) copy-start(f32[256,8192]{1,0:T(8,128)} %reshape.74) | copy-start | bytes 25165828
  269.7 17.5 %copy-start.5 = (bf16[256,1024]{1,0:T(8,128)(2,1)S(1)}, bf16[256,1024]{1,0:T(8,128)(2,1)}, u32[]{:S(2)}) copy-start(bf16[256,1024]{1,0:T(8,128)(2,1)} %copy-done.4) | copy-start | bytes 1572868
  269.7 17.5 %copy-start.7 = (f32[256,512]{1,0:T(8,128)S(1)}, f32[256,512]{1,0:T(8,128)}, u32[]{:S(2)}) copy-start(f32[256,512]{1,0:T(8,128)} %copy-done.6) | copy-start | bytes 1572868

commit v4 on v3

--- a/solution.py
+++ b/solution.py
@@ -98,6 +98,8 @@
     for p in z_peers:
         a3 = a3 + recv3[p]
     summed = a3 * scale
+    own = kc * half + xc * quarter + zc * piece
+    gath[rows(own, piece), :] = summed.astype(gath.dtype)
 
     sq = jnp.sum(summed * summed, axis=(0, 1), keepdims=True)
     nrm_dp[me] = jnp.broadcast_to(sq, nrm_dp.shape[1:])
@@ -112,6 +114,23 @@
         b_desc(lax.rem(me + d, n), me).start()
         return c
     lax.fori_loop(1, n, b_start, 0)
+
+    def g3(p, mine):
+        src = own if mine else kc * half + xc * quarter + p * piece
+        return pltpu.make_async_remote_copy(
+            src_ref=gath.at[rows(src, piece)], dst_ref=gath.at[rows(src, piece)],
+            send_sem=g3s.at[p], recv_sem=g3r.at[zc if mine else p],
+            device_id=dev(p, xc, kc), device_id_type=MESH)
+    exchange(z_peers, g3)
+
+    def g2(p, mine):
+        src = kc * half + (xc if mine else p) * quarter
+        return pltpu.make_async_remote_copy(
+            src_ref=gath.at[rows(src, quarter)], dst_ref=gath.at[rows(src, quarter)],
+            send_sem=g2s.at[p], recv_sem=g2r.at[xc if mine else p],
+            device_id=dev(zc, p, kc), device_id_type=MESH)
+    for p in x_peers:
+        g2(p, True).start()
 
     def b_wait(d, c):
         b_desc(lax.rem(me + d, n), me).wait_send()
@@ -133,6 +152,18 @@
     c_peers = [lax.rem(cj + e, ncls) for e in range(1, ncls)]
     for t in c_peers:
         c_desc(t, cj).start()
+    for p in x_peers:
+        g2(p, True).wait_send()
+        g2(p, False).wait_recv()
+
+    def g1(p, mine):
+        src = (kc if mine else p) * half
+        return pltpu.make_async_remote_copy(
+            src_ref=gath.at[rows(src, half)], dst_ref=gath.at[rows(src, half)],
+            send_sem=g1s.at[p], recv_sem=g1r.at[kc if mine else p],
+            device_id=dev(zc, xc, p), device_id_type=MESH)
+    for p in k_peers:
+        g1(p, True).start()
     for t in c_peers:
         c_desc(t, cj).wait_send()
         c_desc(cj, t).wait_recv()
@@ -140,34 +171,11 @@
     for t in c_peers:
         tot = tot + nrm_cls[t]
     factor = jnp.minimum(1.0, limit / jnp.sqrt(tot))
-    fac = jnp.broadcast_to(factor[0:1, 0:1], summed.shape)
-    own = kc * half + xc * quarter + zc * piece
-    gath[rows(own, piece), :] = (summed * fac).astype(gath.dtype)
-
-    def g3(p, mine):
-        src = own if mine else kc * half + xc * quarter + p * piece
-        return pltpu.make_async_remote_copy(
-            src_ref=gath.at[rows(src, piece)], dst_ref=gath.at[rows(src, piece)],
-            send_sem=g3s.at[p], recv_sem=g3r.at[zc if mine else p],
-            device_id=dev(p, xc, kc), device_id_type=MESH)
-    exchange(z_peers, g3)
-
-    def g2(p, mine):
-        src = kc * half + (xc if mine else p) * quarter
-        return pltpu.make_async_remote_copy(
-            src_ref=gath.at[rows(src, quarter)], dst_ref=gath.at[rows(src, quarter)],
-            send_sem=g2s.at[p], recv_sem=g2r.at[xc if mine else p],
-            device_id=dev(zc, p, kc), device_id_type=MESH)
-    exchange(x_peers, g2)
-
-    def g1(p, mine):
-        src = (kc if mine else p) * half
-        return pltpu.make_async_remote_copy(
-            src_ref=gath.at[rows(src, half)], dst_ref=gath.at[rows(src, half)],
-            send_sem=g1s.at[p], recv_sem=g1r.at[kc if mine else p],
-            device_id=dev(zc, xc, p), device_id_type=MESH)
-    exchange(k_peers, g1)
-    out_ref[...] = gath[...]
+    for p in k_peers:
+        g1(p, True).wait_send()
+        g1(p, False).wait_recv()
+    fac = jnp.broadcast_to(factor[0:1, 0:1], out_ref.shape)
+    out_ref[...] = (gath[...].astype(jnp.float32) * fac).astype(out_ref.dtype)
 
 
 def grad_reduce(part_grad, n, ncls, scale, limit, nk=2, nx=4):

time: 364 us -> 356 us (0.978)
  Pallas kernels: 89.6 us -> 81.9 us
    pallas_call x1, Pallas kernels: 71.4 us -> 63.7 us  [grad_reduce(): pl.pallas_call(functools.partial(_grad_kernel, nk, nx, nz, ncls, scale, l...]
  transfers between devices with their start and end apart: 2 -> 2, of which waited for: 2 -> 2; matrix products, arithmetic and copies ran while one was open for 28% -> 29% of each run, Pallas kernels for 2% -> 3%
where the time goes in v4:
time: 356 us; the launch traced here: 355 us
  Pallas kernels  81.9 us (23%)
  waiting for transfers between devices  72.2 us (20%)
  local copies, waits for them, and re-layouts  55.1 us (15%)
  other arithmetic  53.4 us (15%)
  blocking collectives  48 us (13%)
  starting transfers between devices  22.1 us (6%)
  matrix products  21.9 us (6%)
    pallas_call x1, Pallas kernels, grad_reduce(): pl.pallas_call(functools.partial(_grad_kernel, nk, nx, nz, ncls, scale, l...  63.7 us
    unnamed x4, other arithmetic  47.3 us
    all_to_all x1, waiting for transfers between devices, on_device(): lax.all_to_all(out_emb, 'dp', split_axis=0, concat_axis=0, tiled=True)  44.3 us
    gather x1, local copies, waits for them, and re-layouts, on_device(): near = pool_emb[located]  29.2 us
    all_to_all x1, waiting for transfers between devices, on_device(): lax.all_to_all(out_lab, 'dp', split_axis=0, concat_axis=0, tiled=True)  27.9 us
    psum x1, blocking collectives, on_device(): scores = lax.psum(partial_value, 'class')  25.3 us
    all_gather x1, blocking collectives, on_device(): full_emb = lax.all_gather(embeddings, 'class', axis=1, tiled=True)  22.7 us
    pallas_call x2, Pallas kernels, class_gather(): pl.pallas_call(functools.partial(_class_gather_kernel, ncls), out_shape=j...  18.2 us
  transfers between devices with their start and end apart: 2, of which 2 were waited for; matrix products, arithmetic and copies ran while one was open for 29% of the time, Pallas kernels for 3%

profile of v4, /device:TPU:1, one launch (start us, length us, event | category | flops | bytes accessed | tf_op | source)
XLA Modules:
  0.0 355.3 jit_solution(18125575230112637064)
XLA Ops:
  1.4 3.0 gather_fusion
  4.4 14.8 %all-to-all-start = ((bf16[64,128,128]{2,1,0:T(8,128)(2,1)}), bf16[64,128,128]{2,1,0:T(8,128)(2,1)S(1)}, u32[]{:S(2)}, u32[]{:S(2)}) async-start(bf16[64,128,128]{2,1,0:T(8,128)(2,1)} %gather_fusion), calls=%async_computation | async-start | bytes 4194304 | tf_op jit(solution)/shard_map/all_to_all | solution.py:262
  19.3 5.4 %gather_fusion.2 = bf16[64,128,512]{2,1,0:T(8,128)(2,1)} fusion(bf16[2,128,512]{2,1,0:T(8,128)(2,1)S(1)} %bitcast.49, s32[1024]{0:T(1024)S(1)} %pad_clamp_fusion), kind=kCustom, calls=%fused_computation.2 | custom fusion | bytes 16777472 | tf_op jit(solution)/shard_map/gather | solution.py:261
  24.7 44.3 %all-to-all-done = bf16[64,128,128]{2,1,0:T(8,128)(2,1)S(1)} async-done(((bf16[64,128,128]{2,1,0:T(8,128)(2,1)}), bf16[64,128,128]{2,1,0:T(8,128)(2,1)S(1)}, u32[]{:S(2)}, u32[]{:S(2)}) %all-to-all-start) | async-done | bytes 2097184 | tf_op jit(solution)/shard_map/all_to_all | solution.py:262
  68.9 7.2 %all-to-all-start.1 = ((bf16[64,128,512]{2,1,0:T(8,128)(2,1)}), bf16[64,128,512]{2,1,0:T(8,128)(2,1)}, u32[]{:S(2)}, u32[]{:S(2)}) async-start(bf16[64,128,512]{2,1,0:T(8,128)(2,1)} %gather_fusion.2), calls=%async_computation.1 | async-start | bytes 16777216 | tf_op jit(solution)/shard_map/all_to_all | solution.py:263
  78.7 1.6 reshape.99
  80.3 1.0 reshape.85
  81.3 22.7 %all_gather.3 = bf16[256,1024]{1,0:T(8,128)(2,1)S(1)} all-gather(bf16[256,128]{1,0:T(8,128)(2,1)S(1)} %copy-done.2), channel_id=1, replica_groups=mesh['dp'=64,'class'=8] {'class'}, dimensions={1}, use_global_device_ids=true | all-gather | bytes 589824 | tf_op jit(solution)/shard_map/all_gather | solution.py:269
  106.9 8.9 %shard_map.86 = f32[8,2,256]{2,1,0:T(2,128)} custom-call(f32[2,256]{1,0:T(2,128)} %pad_maximum_fusion.x_ref), custom_call_target="tpu_custom_call" | custom-call | tf_op jit(solution)/shard_map/pallas_call | solution.py:235
  115.9 0.8 slice_reduce_fusion.1
  116.7 29.2 %gather_fusion.1 = bf16[8192,128]{1,0:T(8,128)(2,1)} fusion(bf16[8192,128]{1,0:T(8,128)(2,1)S(1)} %bitcast.50, s32[8192]{0:T(1024)S(1)} %broadcast_clamp_fusion), kind=kCustom, calls=%fused_computation.1 | custom fusion | bytes 4227072 | tf_op jit(solution)/shard_map/gather | solution.py:278
  146.0 2.8 fusion.20
  148.7 25.3 %psum.7 = f32[256,32]{1,0:T(8,128)S(1)} all-reduce(f32[256,32]{1,0:T(8,128)S(1)} %bitcast.56), channel_id=1, replica_groups=mesh['dp'=64,'class'=8] {'class'}, use_global_device_ids=true, to_apply=%region_0.0 | all-reduce | flops 8192 | bytes 65536 | tf_op jit(solution)/shard_map/psum | solution.py:282
  174.7 47.1 %scatter_custom_fusion = f32[2097152]{0:T(1024)} fusion(s32[8192]{0:T(1024)} %reshape.99, f32[8192]{0:T(1024)S(1)} %reshape.101, f32[]{:T(128)} %constant.10.clone.1), kind=kCustom, calls=%fused_computation.6 | custom fusion | flops 8192 | bytes 8389120
  221.8 9.4 %reshape.74 = f32[256,8192]{1,0:T(8,128)} reshape(f32[2097152]{0:T(1024)} %scatter_custom_fusion) | data formatting | bytes 16777216 | tf_op jit(solution)/shard_map/scatter-add | solution.py:290
  231.2 27.9 %all-to-all-done.1 = bf16[64,128,512]{2,1,0:T(8,128)(2,1)} async-done(((bf16[64,128,512]{2,1,0:T(8,128)(2,1)}), bf16[64,128,512]{2,1,0:T(8,128)(2,1)}, u32[]{:S(2)}, u32[]{:S(2)}) %all-to-all-start.1) | async-done | bytes 8388640 | tf_op jit(solution)/shard_map/all_to_all | solution.py:263
  259.1 10.6 %fusion = f32[256,512]{1,0:T(8,128)S(1)} fusion(bf16[8192,512]{1,0:T(8,128)(2,1)} %bitcast.10, f32[256,8192]{1,0:T(8,128)} %reshape.74), kind=kOutput, calls=%fused_computation.5 | convolution fusion | flops 2155872256 | bytes 17301504 | tf_op jit(solution)/shard_map/dot_general | solution.py:295
  269.8 5.9 %fusion.35 = (f32[256]{0:T(256)S(1)}, f32[256,512]{1,0:T(8,128)S(1)}) fusion(bf16[256,512]{1,0:T(8,128)(2,1)S(1)} %copy-done.1, f32[256,512]{1,0:T(8,128)S(1)} %fusion, bf16[8192,512]{1,0:T(8,128)(2,1)} %bitcast.10, f32[256,8192]{1,0:T(8,128)S(1)} %copy-done.3), kind=kOutput, calls=%fused_computation.56 | convolution fusion | flops 2150235904 | bytes 18088960 | tf_op jit(solution)/shard_map/dot_general | solution.py:295
  275.7 0.9 exponential_reduce_fusion
  277.1 9.3 %shard_map.87 = f32[8,2,256]{2,1,0:T(2,128)} custom-call(f32[2,256]{1,0:T(2,128)} %pad_maximum_fusion.1.x_ref), custom_call_target="tpu_custom_call" | custom-call | tf_op jit(solution)/shard_map/pallas_call | solution.py:235
  286.4 0.8 slice_reduce_fusion
  287.3 2.1 convolution_bitcast_fusion.part_ref
  289.4 63.7 %shard_map.88 = bf16[1024,512]{1,0:T(8,128)(2,1)} custom-call(f32[1024,512]{1,0:T(8,128)} %convolution_bitcast_fusion.part_ref), custom_call_target="tpu_custom_call" | custom-call | tf_op jit(solution)/shard_map/pallas_call | solution.py:189
  353.1 2.3 copy.53
  (44 shorter events, 7.5 us)
Async XLA Ops:
  0.6 104.1 %copy-start = (bf16[1024,512]{1,0:T(8,128)(2,1)S(1)}, bf16[1024,512]{1,0:T(8,128)(2,1)}, u32[]{:S(2)}) copy-start(bf16[1024,512]{1,0:T(8,128)(2,1)} %param.9) | copy-start | bytes 3145732
  0.6 18.6 %copy-start.1 = (bf16[256,512]{1,0:T(8,128)(2,1)S(1)}, bf16[256,512]{1,0:T(8,128)(2,1)}, u32[]{:S(2)}) copy-start(bf16[256,512]{1,0:T(8,128)(2,1)} %param.8) | copy-start | bytes 786436
  4.4 64.5 %all-to-all-start = ((bf16[64,128,128]{2,1,0:T(8,128)(2,1)}), bf16[64,128,128]{2,1,0:T(8,128)(2,1)S(1)}, u32[]{:S(2)}, u32[]{:S(2)}) async-start(bf16[64,128,128]{2,1,0:T(8,128)(2,1)} %gather_fusion), calls=%async_computation | async-start | bytes 4194304 | tf_op jit(solution)/shard_map/all_to_all | solution.py:262
  24.6 51.6 %copy-start.8 = (s32[256,32]{0,1:T(8,128)S(1)}, s32[256,32]{0,1:T(8,128)}, u32[]{:S(2)}) copy-start(s32[256,32]{0,1:T(8,128)} %param.12) | copy-start | bytes 98308
  24.6 53.1 %copy-start.10 = (s32[2]{0:T(128)S(1)}, s32[2]{0:T(128)}, u32[]{:S(2)}) copy-start(s32[2]{0:T(128)} %constant.27) | copy-start | bytes 28
  24.6 53.2 %copy-start.11 = (s32[2]{0:T(128)S(1)}, s32[2]{0:T(128)}, u32[]{:S(2)}) copy-start(s32[2]{0:T(128)} %constant.30) | copy-start | bytes 28
  24.6 56.6 %copy-start.2 = (bf16[256,128]{1,0:T(8,128)(2,1)S(1)}, bf16[256,128]{1,0:T(8,128)(2,1)}, u32[]{:S(2)}) copy-start(bf16[256,128]{1,0:T(8,128)(2,1)} %param.7) | copy-start | bytes 196612
  68.9 190.1 %all-to-all-start.1 = ((bf16[64,128,512]{2,1,0:T(8,128)(2,1)}), bf16[64,128,512]{2,1,0:T(8,128)(2,1)}, u32[]{:S(2)}, u32[]{:S(2)}) async-start(bf16[64,128,512]{2,1,0:T(8,128)(2,1)} %gather_fusion.2), calls=%async_computation.1 | async-start | bytes 16777216 | tf_op jit(solution)/shard_map/all_to_all | solution.py:263
  104.0 0.8 copy-start.4
  105.3 0.8 copy-start.6
  116.7 57.3 %copy-start.9 = (s32[256]{0:T(256)S(1)}, s32[256]{0:T(256)}, u32[]{:S(2)}) copy-start(s32[256]{0:T(256)} %param.13) | copy-start | bytes 3076
  259.1 10.6 %copy-start.3 = (f32[256,8192]{1,0:T(8,128)S(1)}, f32[256,8192]{1,0:T(8,128)}, u32[]{:S(2)}) copy-start(f32[256,8192]{1,0:T(8,128)} %reshape.74) | copy-start | bytes 25165828
  269.7 17.5 %copy-start.5 = (bf16[256,1024]{1,0:T(8,128)(2,1)S(1)}, bf16[256,1024]{1,0:T(8,128)(2,1)}, u32[]{:S(2)}) copy-start(bf16[256,1024]{1,0:T(8,128)(2,1)} %copy-done.4) | copy-start | bytes 1572868
  269.7 17.5 %copy-start.7 = (f32[256,512]{1,0:T(8,128)S(1)}, f32[256,512]{1,0:T(8,128)}, u32[]{:S(2)}) copy-start(f32[256,512]{1,0:T(8,128)} %copy-done.6) | copy-start | bytes 1572868

commit v5 on v4

--- a/solution.py
+++ b/solution.py
@@ -292,9 +292,9 @@
     )
     dense_hi = dense.astype(jnp.bfloat16)
     dense_lo = (dense - dense_hi.astype(jnp.float32)).astype(jnp.bfloat16)
-    spread = jnp.dot(dense_hi, pool_lab, preferred_element_type=jnp.float32) + jnp.dot(
-        dense_lo, pool_lab, preferred_element_type=jnp.float32
-    )
+    stacked = lax.optimization_barrier(jnp.concatenate([dense_hi, dense_lo], axis=0))
+    both = jnp.dot(stacked, pool_lab, preferred_element_type=jnp.float32)
+    spread = both[:rows] + both[rows:]
     target = 4.0 * spread + labels.astype(jnp.float32)
     z_local = jnp.max(target, axis=1)
     z_top, z_total = _combine_stats(

time: 356 us -> 350 us (0.983)
  other arithmetic: 53.4 us -> 71.5 us
  waiting for transfers between devices: 72.2 us -> 54.4 us
  matrix products: 21.9 us -> 15.6 us
    all_to_all x1, waiting for transfers between devices: 27.9 us -> 10.2 us  [on_device(): lax.all_to_all(out_lab, 'dp', split_axis=0, concat_axis=0, tiled=True)]
    convert_element_type x0 -> x1, other arithmetic: none -> 11 us  [on_device(): dense_lo = (dense - dense_hi.astype(jnp.float32)).astype(jnp.bfloat16)]
    concatenate x0 -> x1, other arithmetic: none -> 7.68 us  [on_device(): jnp.concatenate([dense_hi, dense_lo], axis=0)]
    dot_general x2 -> x1, matrix products: 16.5 us -> 9.59 us  [on_device(): both = jnp.dot(stacked, pool_lab, preferred_element_type=jnp.float32)]
  transfers between devices with their start and end apart: 2 -> 2, of which waited for: 2 -> 2; matrix products, arithmetic and copies ran while one was open for 29% -> 35% of each run, Pallas kernels for 3% -> 3%
where the time goes in v5:
time: 350 us; the launch traced here: 349 us
  Pallas kernels  82 us (23%)
  other arithmetic  71.5 us (20%)
  waiting for transfers between devices  54.4 us (16%)
  local copies, waits for them, and re-layouts  54.3 us (16%)
  blocking collectives  47.8 us (14%)
  starting transfers between devices  22.1 us (6%)
  matrix products  15.6 us (4%)
    pallas_call x1, Pallas kernels, grad_reduce(): pl.pallas_call(functools.partial(_grad_kernel, nk, nx, nz, ncls, scale, l...  63.7 us
    unnamed x4, other arithmetic  47.1 us
    all_to_all x1, waiting for transfers between devices, on_device(): lax.all_to_all(out_emb, 'dp', split_axis=0, concat_axis=0, tiled=True)  44.3 us
    gather x1, local copies, waits for them, and re-layouts, on_device(): near = pool_emb[located]  29.2 us
    psum x1, blocking collectives, on_device(): scores = lax.psum(partial_value, 'class')  25.1 us
    all_gather x1, blocking collectives, on_device(): full_emb = lax.all_gather(embeddings, 'class', axis=1, tiled=True)  22.7 us
    pallas_call x2, Pallas kernels, class_gather(): pl.pallas_call(functools.partial(_class_gather_kernel, ncls), out_shape=j...  18.2 us
    all_to_all x1, starting transfers between devices, on_device(): lax.all_to_all(out_emb, 'dp', split_axis=0, concat_axis=0, tiled=True)  14.8 us
  transfers between devices with their start and end apart: 2, of which 2 were waited for; matrix products, arithmetic and copies ran while one was open for 35% of the time, Pallas kernels for 3%

profile of v5, /device:TPU:1, one launch (start us, length us, event | category | flops | bytes accessed | tf_op | source)
XLA Modules:
  0.0 348.6 jit_solution(7131382736982992780)
XLA Ops:
  1.4 3.0 gather_fusion
  4.5 14.8 %all-to-all-start = ((bf16[64,128,128]{2,1,0:T(8,128)(2,1)}), bf16[64,128,128]{2,1,0:T(8,128)(2,1)S(1)}, u32[]{:S(2)}, u32[]{:S(2)}) async-start(bf16[64,128,128]{2,1,0:T(8,128)(2,1)} %gather_fusion), calls=%async_computation | async-start | bytes 4194304 | tf_op jit(solution)/shard_map/all_to_all | solution.py:262
  19.3 5.4 %gather_fusion.2 = bf16[64,128,512]{2,1,0:T(8,128)(2,1)} fusion(bf16[2,128,512]{2,1,0:T(8,128)(2,1)S(1)} %bitcast.49, s32[1024]{0:T(1024)S(1)} %pad_clamp_fusion), kind=kCustom, calls=%fused_computation.2 | custom fusion | bytes 16777472 | tf_op jit(solution)/shard_map/gather | solution.py:261
  24.7 44.3 %all-to-all-done = bf16[64,128,128]{2,1,0:T(8,128)(2,1)S(1)} async-done(((bf16[64,128,128]{2,1,0:T(8,128)(2,1)}), bf16[64,128,128]{2,1,0:T(8,128)(2,1)S(1)}, u32[]{:S(2)}, u32[]{:S(2)}) %all-to-all-start) | async-done | bytes 2097184 | tf_op jit(solution)/shard_map/all_to_all | solution.py:262
  69.0 7.3 %all-to-all-start.1 = ((bf16[64,128,512]{2,1,0:T(8,128)(2,1)}), bf16[64,128,512]{2,1,0:T(8,128)(2,1)}, u32[]{:S(2)}, u32[]{:S(2)}) async-start(bf16[64,128,512]{2,1,0:T(8,128)(2,1)} %gather_fusion.2), calls=%async_computation.1 | async-start | bytes 16777216 | tf_op jit(solution)/shard_map/all_to_all | solution.py:263
  77.7 22.7 %all_gather.3 = bf16[256,1024]{1,0:T(8,128)(2,1)S(1)} all-gather(bf16[256,128]{1,0:T(8,128)(2,1)S(1)} %copy-done.3), channel_id=1, replica_groups=mesh['dp'=64,'class'=8] {'class'}, dimensions={1}, use_global_device_ids=true | all-gather | bytes 589824 | tf_op jit(solution)/shard_map/all_gather | solution.py:269
  101.2 1.2 fusion.26
  102.5 2.0 copy.26
  104.5 1.3 exponential_reduce_fusion.1
  106.4 8.9 %shard_map.86 = f32[8,2,256]{2,1,0:T(2,128)} custom-call(f32[2,256]{1,0:T(2,128)} %pad_maximum_fusion.1.x_ref), custom_call_target="tpu_custom_call" | custom-call | tf_op jit(solution)/shard_map/pallas_call | solution.py:235
  116.2 29.2 %gather_fusion.1 = bf16[8192,128]{1,0:T(8,128)(2,1)} fusion(bf16[8192,128]{1,0:T(8,128)(2,1)S(1)} %bitcast.50, s32[8192]{0:T(1024)S(1)} %broadcast_clamp_fusion), kind=kCustom, calls=%fused_computation.1 | custom fusion | bytes 4227072 | tf_op jit(solution)/shard_map/gather | solution.py:278
  145.4 2.8 fusion.9
  148.2 25.1 %psum.7 = f32[256,32]{1,0:T(8,128)S(1)} all-reduce(f32[256,32]{1,0:T(8,128)S(1)} %bitcast.56), channel_id=1, replica_groups=mesh['dp'=64,'class'=8] {'class'}, use_global_device_ids=true, to_apply=%region_0.0 | all-reduce | flops 8192 | bytes 65536 | tf_op jit(solution)/shard_map/psum | solution.py:282
  174.0 46.9 %scatter_custom_fusion = f32[2097152]{0:T(1024)} fusion(s32[8192]{0:T(1024)S(1)} %reshape.99, f32[8192]{0:T(1024)S(1)} %reshape.101, f32[]{:T(128)} %constant.10.clone.1), kind=kCustom, calls=%fused_computation.6 | custom fusion | flops 8192 | bytes 8388612
  220.9 9.4 %reshape.74 = f32[256,8192]{1,0:T(8,128)} reshape(f32[2097152]{0:T(1024)} %scatter_custom_fusion) | data formatting | bytes 16777216 | tf_op jit(solution)/shard_map/scatter-add | solution.py:290
  230.3 11.0 %subtract_convert_fusion = (bf16[256,8192]{1,0:T(8,128)(2,1)}, bf16[256,8192]{1,0:T(8,128)(2,1)}) fusion(f32[256,8192]{1,0:T(8,128)} %reshape.74), kind=kLoop, calls=%fused_computation.5 | loop fusion | flops 8388608 | bytes 16777216 | tf_op jit(solution)/shard_map/convert_element_type | solution.py:294
  241.3 7.7 %pad_maximum_fusion = bf16[512,8192]{1,0:T(8,128)(2,1)} fusion(bf16[256,8192]{1,0:T(8,128)(2,1)} %get-tuple-element.10, bf16[256,8192]{1,0:T(8,128)(2,1)} %get-tuple-element.11), kind=kLoop, calls=%fused_computation.4 | loop fusion | flops 16777216 | bytes 16777216 | tf_op jit(solution)/shard_map/concatenate | solution.py:295
  249.0 10.2 %all-to-all-done.1 = bf16[64,128,512]{2,1,0:T(8,128)(2,1)} async-done(((bf16[64,128,512]{2,1,0:T(8,128)(2,1)}), bf16[64,128,512]{2,1,0:T(8,128)(2,1)}, u32[]{:S(2)}, u32[]{:S(2)}) %all-to-all-start.1) | async-done | bytes 8388640 | tf_op jit(solution)/shard_map/all_to_all | solution.py:263
  259.2 9.6 %fusion.27 = f32[512,512]{0,1:T(8,128)S(1)} fusion(bf16[512,8192]{1,0:T(8,128)(2,1)} %pad_maximum_fusion, bf16[8192,512]{1,0:T(8,128)(2,1)} %bitcast.10), kind=kOutput, calls=%fused_computation.55 | convolution fusion | flops 4294967296 | bytes 17825792 | tf_op jit(solution)/shard_map/dot_general | solution.py:296
  269.6 9.3 %shard_map.87 = f32[8,2,256]{2,1,0:T(2,128)} custom-call(f32[2,256]{1,0:T(2,128)} %pad_maximum_fusion.2.x_ref), custom_call_target="tpu_custom_call" | custom-call | tf_op jit(solution)/shard_map/pallas_call | solution.py:235
  279.8 2.0 convolution_bitcast_fusion.part_ref
  281.8 63.7 %shard_map.88 = bf16[1024,512]{1,0:T(8,128)(2,1)} custom-call(f32[1024,512]{1,0:T(8,128)} %convolution_bitcast_fusion.part_ref), custom_call_target="tpu_custom_call" | custom-call | tf_op jit(solution)/shard_map/pallas_call | solution.py:189
  345.5 0.8 copy.29
  346.3 2.3 copy.62
  (51 shorter events, 6.8 us)
Async XLA Ops:
  0.6 100.6 %copy-start = (bf16[1024,512]{1,0:T(8,128)(2,1)S(1)}, bf16[1024,512]{1,0:T(8,128)(2,1)}, u32[]{:S(2)}) copy-start(bf16[1024,512]{1,0:T(8,128)(2,1)} %param.9) | copy-start | bytes 3145732
  0.6 18.7 %copy-start.2 = (bf16[256,512]{1,0:T(8,128)(2,1)S(1)}, bf16[256,512]{1,0:T(8,128)(2,1)}, u32[]{:S(2)}) copy-start(bf16[256,512]{1,0:T(8,128)(2,1)} %param.8) | copy-start | bytes 786436
  4.5 64.5 %all-to-all-start = ((bf16[64,128,128]{2,1,0:T(8,128)(2,1)}), bf16[64,128,128]{2,1,0:T(8,128)(2,1)S(1)}, u32[]{:S(2)}, u32[]{:S(2)}) async-start(bf16[64,128,128]{2,1,0:T(8,128)(2,1)} %gather_fusion), calls=%async_computation | async-start | bytes 4194304 | tf_op jit(solution)/shard_map/all_to_all | solution.py:262
  24.7 52.4 %copy-start.8 = (s32[256,32]{0,1:T(8,128)S(1)}, s32[256,32]{0,1:T(8,128)}, u32[]{:S(2)}) copy-start(s32[256,32]{0,1:T(8,128)} %param.12) | copy-start | bytes 98308
  24.7 52.4 %copy-start.9 = (s32[256,32]{0,1:T(8,128)S(1)}, s32[256,32]{0,1:T(8,128)}, u32[]{:S(2)}) copy-start(s32[256,32]{0,1:T(8,128)} %param.11) | copy-start | bytes 98308
  24.7 52.6 %copy-start.11 = (s32[2]{0:T(128)S(1)}, s32[2]{0:T(128)}, u32[]{:S(2)}) copy-start(s32[2]{0:T(128)} %constant.27) | copy-start | bytes 28
  24.7 52.7 %copy-start.12 = (s32[2]{0:T(128)S(1)}, s32[2]{0:T(128)}, u32[]{:S(2)}) copy-start(s32[2]{0:T(128)} %constant.30) | copy-start | bytes 28
  24.7 53.0 %copy-start.3 = (bf16[256,128]{1,0:T(8,128)(2,1)S(1)}, bf16[256,128]{1,0:T(8,128)(2,1)}, u32[]{:S(2)}) copy-start(bf16[256,128]{1,0:T(8,128)(2,1)} %param.7) | copy-start | bytes 196612
  69.0 190.2 %all-to-all-start.1 = ((bf16[64,128,512]{2,1,0:T(8,128)(2,1)}), bf16[64,128,512]{2,1,0:T(8,128)(2,1)}, u32[]{:S(2)}, u32[]{:S(2)}) async-start(bf16[64,128,512]{2,1,0:T(8,128)(2,1)} %gather_fusion.2), calls=%async_computation.1 | async-start | bytes 16777216 | tf_op jit(solution)/shard_map/all_to_all | solution.py:263
  100.4 0.8 copy-start.4
  116.2 57.1 %copy-start.10 = (s32[256]{0:T(256)S(1)}, s32[256]{0:T(256)}, u32[]{:S(2)}) copy-start(s32[256]{0:T(256)} %param.13) | copy-start | bytes 3076
  259.1 9.6 %copy-start.6 = (bf16[256,512]{0,1:T(8,128)(2,1)S(1)}, bf16[256,512]{0,1:T(8,128)(2,1)}, u32[]{:S(2)}) copy-start(bf16[256,512]{0,1:T(8,128)(2,1)} %copy.24) | copy-start | bytes 786436
  259.2 20.6 %copy-start.5 = (bf16[256,1024]{1,0:T(8,128)(2,1)S(1)}, bf16[256,1024]{1,0:T(8,128)(2,1)}, u32[]{:S(2)}) copy-start(bf16[256,1024]{1,0:T(8,128)(2,1)} %copy-done.4) | copy-start | bytes 1572868
  259.2 20.7 %copy-start.7 = (f32[256,512]{0,1:T(8,128)S(1)}, f32[256,512]{0,1:T(8,128)}, u32[]{:S(2)}) copy-start(f32[256,512]{0,1:T(8,128)} %copy.26) | copy-start | bytes 1572868
  259.2 89.5 %copy-start.1 = (bf16[1024,512]{1,0:T(8,128)(2,1)S(1)}, bf16[1024,512]{1,0:T(8,128)(2,1)}, u32[]{:S(2)}) copy-start(bf16[1024,512]{1,0:T(8,128)(2,1)} %param.9) | copy-start | bytes 3145732

commit v6 on v5

--- a/solution.py
+++ b/solution.py
@@ -266,20 +266,25 @@
     pool_lab = pool_lab.reshape(pool_rows, class_part)
     located = nbr_source * BLOCK + nbr_offset
 
-    full_emb = lax.all_gather(embeddings, "class", axis=1, tiled=True)
+    ncls = lax.axis_size("class")
+    emb_all = class_gather(embeddings, ncls, 3)
+    full_emb = jnp.transpose(emb_all, (1, 0, 2)).reshape(rows, ncls * width_part)
     head = jnp.dot(full_emb, head_weight, preferred_element_type=jnp.float32)
-    h_top, h_total = _combine_stats(
-        jnp.max(head, axis=1),
-        jnp.sum(jnp.exp(head - jnp.max(head, axis=1, keepdims=True)), axis=1),
-        1,
-    )
-    prob_head = jnp.exp(head - h_top[:, None]) / h_total[:, None]
+    h_max = jnp.max(head, axis=1)
+    h_sum = jnp.sum(jnp.exp(head - h_max[:, None]), axis=1)
 
     near = pool_emb[located]
     partial_value = jnp.einsum(
-        "rd,rkd->rk", embeddings, near, preferred_element_type=jnp.float32
-    )
-    scores = lax.psum(partial_value, "class")
+        "rd,rkd->kr", embeddings, near, preferred_element_type=jnp.float32
+    )
+    packed = class_gather(
+        jnp.concatenate([partial_value, h_max[None, :], h_sum[None, :]], axis=0), ncls, 1
+    )
+    scores = jnp.sum(packed[:, :nbrs], axis=0).T
+    h_maxes, h_sums = packed[:, nbrs], packed[:, nbrs + 1]
+    h_top = jnp.max(h_maxes, axis=0)
+    h_total = jnp.sum(h_sums * jnp.exp(h_maxes - h_top[None, :]), axis=0)
+    prob_head = jnp.exp(head - h_top[:, None]) / h_total[:, None]
     valid = lax.broadcasted_iota(jnp.int32, (rows, nbrs), 1) < counts[:, None]
     logits = jnp.where(valid, scores / math.sqrt(D), -1e30)
     top = jnp.max(logits, axis=1, keepdims=True)

time: 350 us -> 350 us (level)
  blocking collectives: 47.8 us -> 0 us
  Pallas kernels: 82 us -> 107 us
  waiting for transfers between devices: 54.4 us -> 75.7 us
    psum x1 -> x0, blocking collectives: 25.1 us -> none  [on_device(): scores = lax.psum(partial_value, 'class')]
    pallas_call x2 -> x3, Pallas kernels: 18.2 us -> 43.1 us  [class_gather(): pl.pallas_call(functools.partial(_class_gather_kernel, ncls), out_shape=j...]
    all_gather x1 -> x0, blocking collectives: 22.7 us -> none  [on_device(): full_emb = lax.all_gather(embeddings, 'class', axis=1, tiled=True)]
    all_to_all x1, waiting for transfers between devices: 10.2 us -> 31.4 us  [on_device(): lax.all_to_all(out_lab, 'dp', split_axis=0, concat_axis=0, tiled=True)]
  transfers between devices with their start and end apart: 2 -> 2, of which waited for: 2 -> 2; matrix products, arithmetic and copies ran while one was open for 35% -> 35% of each run, Pallas kernels for 3% -> 10%
where the time goes in v6:
time: 350 us; the launch traced here: 349 us
  Pallas kernels  107 us (31%)
  waiting for transfers between devices  75.7 us (22%)
  other arithmetic  71.9 us (21%)
  local copies, waits for them, and re-layouts  55.5 us (16%)
  starting transfers between devices  22.1 us (6%)
  matrix products  15.9 us (5%)
    pallas_call x1, Pallas kernels, grad_reduce(): pl.pallas_call(functools.partial(_grad_kernel, nk, nx, nz, ncls, scale, l...  63.7 us
    unnamed x4, other arithmetic  47.9 us
    all_to_all x1, waiting for transfers between devices, on_device(): lax.all_to_all(out_emb, 'dp', split_axis=0, concat_axis=0, tiled=True)  44.3 us
    pallas_call x3, Pallas kernels, class_gather(): pl.pallas_call(functools.partial(_class_gather_kernel, ncls), out_shape=j...  43.1 us
    all_to_all x1, waiting for transfers between devices, on_device(): lax.all_to_all(out_lab, 'dp', split_axis=0, concat_axis=0, tiled=True)  31.4 us
    gather x1, local copies, waits for them, and re-layouts, on_device(): near = pool_emb[located]  29.2 us
    all_to_all x1, starting transfers between devices, on_device(): lax.all_to_all(out_emb, 'dp', split_axis=0, concat_axis=0, tiled=True)  14.8 us
    convert_element_type x1, other arithmetic, on_device(): dense_lo = (dense - dense_hi.astype(jnp.float32)).astype(jnp.bfloat16)  11 us
  transfers between devices with their start and end apart: 2, of which 2 were waited for; matrix products, arithmetic and copies ran while one was open for 35% of the time, Pallas kernels for 10%

profile of v6, /device:TPU:1, one launch (start us, length us, event | category | flops | bytes accessed | tf_op | source)
XLA Modules:
  0.0 348.7 jit_solution(8420980408017293767)
XLA Ops:
  1.4 3.0 gather_fusion
  4.5 14.8 %all-to-all-start = ((bf16[64,128,128]{2,1,0:T(8,128)(2,1)}), bf16[64,128,128]{2,1,0:T(8,128)(2,1)S(1)}, u32[]{:S(2)}, u32[]{:S(2)}) async-start(bf16[64,128,128]{2,1,0:T(8,128)(2,1)} %gather_fusion), calls=%async_computation | async-start | bytes 4194304 | tf_op jit(solution)/shard_map/all_to_all | solution.py:262
  19.3 5.4 %gather_fusion.2 = bf16[64,128,512]{2,1,0:T(8,128)(2,1)} fusion(bf16[2,128,512]{2,1,0:T(8,128)(2,1)S(1)} %bitcast.64, s32[1024]{0:T(1024)S(1)} %pad_clamp_fusion), kind=kCustom, calls=%fused_computation.2 | custom fusion | bytes 16777472 | tf_op jit(solution)/shard_map/gather | solution.py:261
  24.7 44.3 %all-to-all-done = bf16[64,128,128]{2,1,0:T(8,128)(2,1)S(1)} async-done(((bf16[64,128,128]{2,1,0:T(8,128)(2,1)}), bf16[64,128,128]{2,1,0:T(8,128)(2,1)S(1)}, u32[]{:S(2)}, u32[]{:S(2)}) %all-to-all-start) | async-done | bytes 2097184 | tf_op jit(solution)/shard_map/all_to_all | solution.py:262
  69.0 7.3 %all-to-all-start.1 = ((bf16[64,128,512]{2,1,0:T(8,128)(2,1)}), bf16[64,128,512]{2,1,0:T(8,128)(2,1)}, u32[]{:S(2)}, u32[]{:S(2)}) async-start(bf16[64,128,512]{2,1,0:T(8,128)(2,1)} %gather_fusion.2), calls=%async_computation.1 | async-start | bytes 16777216 | tf_op jit(solution)/shard_map/all_to_all | solution.py:263
  76.3 20.3 %shard_map.86 = bf16[8,256,128]{2,1,0:T(8,128)(2,1)} custom-call(bf16[256,128]{1,0:T(8,128)(2,1)} %x_ref.1), custom_call_target="tpu_custom_call" | custom-call | tf_op jit(solution)/shard_map/pallas_call | solution.py:235
  99.7 1.0 reshape.89
  100.7 2.0 copy.23
  102.8 1.6 fusion.26
  105.2 29.2 %gather_fusion.1 = bf16[8192,128]{1,0:T(8,128)(2,1)} fusion(bf16[8192,128]{1,0:T(8,128)(2,1)S(1)} %bitcast.65, s32[8192]{0:T(1024)S(1)} %broadcast_clamp_fusion), kind=kCustom, calls=%fused_computation.1 | custom fusion | bytes 4227072 | tf_op jit(solution)/shard_map/gather | solution.py:276
  134.4 2.8 fusion.9
  137.9 13.5 %shard_map.87 = f32[8,34,256]{2,1,0:T(8,128)} custom-call(f32[34,256]{1,0:T(8,128)} %pad_maximum_fusion.1.x_ref), custom_call_target="tpu_custom_call" | custom-call | tf_op jit(solution)/shard_map/pallas_call | solution.py:235
  151.3 1.0 slice_reduce_fusion
  152.6 47.1 %scatter_custom_fusion = f32[2097152]{0:T(1024)} fusion(s32[8192]{0:T(1024)} %reshape.103, f32[8192]{0:T(1024)S(1)} %reshape.105, f32[]{:T(128)} %constant.10.clone.1), kind=kCustom, calls=%fused_computation.6 | custom fusion | flops 8192 | bytes 8389120
  199.7 9.4 %reshape.78 = f32[256,8192]{1,0:T(8,128)} reshape(f32[2097152]{0:T(1024)} %scatter_custom_fusion) | data formatting | bytes 16777216 | tf_op jit(solution)/shard_map/scatter-add | solution.py:295
  209.1 11.0 %subtract_convert_fusion = (bf16[256,8192]{1,0:T(8,128)(2,1)}, bf16[256,8192]{1,0:T(8,128)(2,1)}) fusion(f32[256,8192]{1,0:T(8,128)} %reshape.78), kind=kLoop, calls=%fused_computation.5 | loop fusion | flops 8388608 | bytes 16777216 | tf_op jit(solution)/shard_map/convert_element_type | solution.py:299
  220.1 7.7 %pad_maximum_fusion = bf16[512,8192]{1,0:T(8,128)(2,1)} fusion(bf16[256,8192]{1,0:T(8,128)(2,1)} %get-tuple-element.4, bf16[256,8192]{1,0:T(8,128)(2,1)} %get-tuple-element.5), kind=kLoop, calls=%fused_computation.4 | loop fusion | flops 16777216 | bytes 16777216 | tf_op jit(solution)/shard_map/concatenate | solution.py:300
  227.7 31.4 %all-to-all-done.1 = bf16[64,128,512]{2,1,0:T(8,128)(2,1)} async-done(((bf16[64,128,512]{2,1,0:T(8,128)(2,1)}), bf16[64,128,512]{2,1,0:T(8,128)(2,1)}, u32[]{:S(2)}, u32[]{:S(2)}) %all-to-all-start.1) | async-done | bytes 8388640 | tf_op jit(solution)/shard_map/all_to_all | solution.py:263
  259.2 9.5 %fusion.27 = f32[512,512]{1,0:T(8,128)S(1)} fusion(bf16[512,8192]{1,0:T(8,128)(2,1)} %pad_maximum_fusion, bf16[8192,512]{1,0:T(8,128)(2,1)} %bitcast.15), kind=kOutput, calls=%fused_computation.56 | convolution fusion | flops 4294967296 | bytes 17825792 | tf_op jit(solution)/shard_map/dot_general | solution.py:301
  270.3 9.3 %shard_map.88 = f32[8,2,256]{2,1,0:T(2,128)} custom-call(f32[2,256]{1,0:T(2,128)} %pad_maximum_fusion.2.x_ref), custom_call_target="tpu_custom_call" | custom-call | tf_op jit(solution)/shard_map/pallas_call | solution.py:235
  279.6 1.0 slice_reduce_fusion.1
  280.7 2.0 convolution_bitcast_fusion.part_ref
  282.7 63.7 %shard_map.89 = bf16[1024,512]{1,0:T(8,128)(2,1)} custom-call(f32[1024,512]{1,0:T(8,128)} %convolution_bitcast_fusion.part_ref), custom_call_target="tpu_custom_call" | custom-call | tf_op jit(solution)/shard_map/pallas_call | solution.py:189
  346.4 2.3 copy.63
  (46 shorter events, 7.4 us)
Async XLA Ops:
  0.6 102.2 %copy-start = (bf16[1024,512]{1,0:T(8,128)(2,1)S(1)}, bf16[1024,512]{1,0:T(8,128)(2,1)}, u32[]{:S(2)}) copy-start(bf16[1024,512]{1,0:T(8,128)(2,1)} %param.9) | copy-start | bytes 3145732
  0.6 18.7 %copy-start.1 = (bf16[256,512]{1,0:T(8,128)(2,1)S(1)}, bf16[256,512]{1,0:T(8,128)(2,1)}, u32[]{:S(2)}) copy-start(bf16[256,512]{1,0:T(8,128)(2,1)} %param.8) | copy-start | bytes 786436
  4.5 64.5 %all-to-all-start = ((bf16[64,128,128]{2,1,0:T(8,128)(2,1)}), bf16[64,128,128]{2,1,0:T(8,128)(2,1)S(1)}, u32[]{:S(2)}, u32[]{:S(2)}) async-start(bf16[64,128,128]{2,1,0:T(8,128)(2,1)} %gather_fusion), calls=%async_computation | async-start | bytes 4194304 | tf_op jit(solution)/shard_map/all_to_all | solution.py:262
  24.7 71.9 %copy-start.6 = (s32[256,32]{0,1:T(8,128)S(1)}, s32[256,32]{0,1:T(8,128)}, u32[]{:S(2)}) copy-start(s32[256,32]{0,1:T(8,128)} %param.12) | copy-start | bytes 98308
  24.7 71.9 %copy-start.7 = (s32[256,32]{0,1:T(8,128)S(1)}, s32[256,32]{0,1:T(8,128)}, u32[]{:S(2)}) copy-start(s32[256,32]{0,1:T(8,128)} %param.11) | copy-start | bytes 98308
  24.7 72.7 %copy-start.9 = (s32[2]{0:T(128)S(1)}, s32[2]{0:T(128)}, u32[]{:S(2)}) copy-start(s32[2]{0:T(128)} %constant.27) | copy-start | bytes 28
  24.7 72.8 %copy-start.10 = (s32[2]{0:T(128)S(1)}, s32[2]{0:T(128)}, u32[]{:S(2)}) copy-start(s32[2]{0:T(128)} %constant.30) | copy-start | bytes 28
  69.0 190.2 %all-to-all-start.1 = ((bf16[64,128,512]{2,1,0:T(8,128)(2,1)}), bf16[64,128,512]{2,1,0:T(8,128)(2,1)}, u32[]{:S(2)}, u32[]{:S(2)}) async-start(bf16[64,128,512]{2,1,0:T(8,128)(2,1)} %gather_fusion.2), calls=%async_computation.1 | async-start | bytes 16777216 | tf_op jit(solution)/shard_map/all_to_all | solution.py:263
  104.4 0.8 copy-start.4
  105.2 29.2 %copy-start.2 = (bf16[256,128]{1,0:T(8,128)(2,1)S(1)}, bf16[256,128]{1,0:T(8,128)(2,1)}, u32[]{:S(2)}) copy-start(bf16[256,128]{1,0:T(8,128)(2,1)} %x_ref.1) | copy-start | bytes 196612
  105.2 47.1 %copy-start.8 = (s32[256]{0:T(256)S(1)}, s32[256]{0:T(256)}, u32[]{:S(2)}) copy-start(s32[256]{0:T(256)} %param.13) | copy-start | bytes 3076
  259.1 21.5 %copy-start.3 = (bf16[256,8,128]{0,2,1:T(8,128)(2,1)S(1)}, bf16[256,8,128]{0,2,1:T(8,128)(2,1)}, u32[]{:S(2)}) copy-start(bf16[256,8,128]{0,2,1:T(8,128)(2,1)} %copy.23) | copy-start | bytes 1572868
  259.1 21.5 %copy-start.5 = (f32[256,512]{1,0:T(8,128)S(1)}, f32[256,512]{1,0:T(8,128)}, u32[]{:S(2)}) copy-start(f32[256,512]{1,0:T(8,128)} %copy-done.4) | copy-start | bytes 1572868

commit v7 on v6

--- a/solution.py
+++ b/solution.py
@@ -242,6 +242,48 @@
     )(x)
 
 
+def _exchange_kernel(n, src_ref, out_ref, buf, ssem, rsem):
+    me = lax.axis_index("dp")
+    cj = lax.axis_index("class")
+    barrier = pltpu.get_barrier_semaphore()
+
+    def greet(d, c):
+        pl.semaphore_signal(barrier, 1, device_id=(lax.rem(me + d, n), cj), device_id_type=MESH)
+        return c
+    lax.fori_loop(1, n, greet, 0)
+    pl.semaphore_wait(barrier, n - 1)
+
+    def desc(t, s):
+        return pltpu.make_async_remote_copy(
+            src_ref=src_ref.at[t], dst_ref=buf.at[s], send_sem=ssem.at[t], recv_sem=rsem.at[s],
+            device_id=(t, cj), device_id_type=MESH)
+
+    def start(d, c):
+        desc(lax.rem(me + d, n), me).start()
+        return c
+    lax.fori_loop(1, n, start, 0)
+    buf[me] = src_ref[me]
+
+    def wait(d, c):
+        desc(lax.rem(me + d, n), me).wait_send()
+        desc(me, lax.rem(me + d, n)).wait_recv()
+        return c
+    lax.fori_loop(1, n, wait, 0)
+    out_ref[...] = buf[...]
+
+
+def dp_exchange(blocks, n, cid):
+    dma = pltpu.SemaphoreType.DMA
+    return pl.pallas_call(
+        functools.partial(_exchange_kernel, n),
+        out_shape=jax.ShapeDtypeStruct(blocks.shape, blocks.dtype),
+        in_specs=[pl.BlockSpec(memory_space=pltpu.VMEM)],
+        out_specs=pl.BlockSpec(memory_space=pltpu.VMEM),
+        scratch_shapes=[pltpu.VMEM(blocks.shape, blocks.dtype), dma((n,)), dma((n,))],
+        compiler_params=pltpu.CompilerParams(collective_id=cid, has_side_effects=True),
+    )(blocks)
+
+
 def _combine_stats(local_max, local_sum, cid):
     both = class_gather(jnp.stack([local_max, local_sum], axis=0), lax.axis_size("class"), cid)
     maxes, sums = both[:, 0], both[:, 1]
@@ -259,8 +301,8 @@
     picks = send_blocks[0]
     out_emb = embeddings.reshape(rows // BLOCK, BLOCK, width_part)[picks]
     out_lab = labels.reshape(rows // BLOCK, BLOCK, class_part)[picks]
-    pool_emb = lax.all_to_all(out_emb, "dp", split_axis=0, concat_axis=0, tiled=True)
     pool_lab = lax.all_to_all(out_lab, "dp", split_axis=0, concat_axis=0, tiled=True)
+    pool_emb = dp_exchange(out_emb, dp_count, 4)
     pool_rows = dp_count * BLOCK
     pool_emb = pool_emb.reshape(pool_rows, width_part)
     pool_lab = pool_lab.reshape(pool_rows, class_part)

time: 350 us -> 462 us (1.32)
  Pallas kernels: 107 us -> 313 us
  waiting for transfers between devices: 75.7 us -> 0.01 us
  local copies, waits for them, and re-layouts: 55.5 us -> 46.6 us
  starting transfers between devices: 22.1 us -> 15.2 us
    pallas_call x0 -> x1, Pallas kernels: none -> 205 us  [dp_exchange(): pl.pallas_call(functools.partial(_exchange_kernel, n), out_shape=jax.Shap...]
    all_to_all x1 -> x0, waiting for transfers between devices: 44.3 us -> none  [on_device(): lax.all_to_all(out_emb, 'dp', split_axis=0, concat_axis=0, tiled=True)]
    all_to_all x1, waiting for transfers between devices: 31.4 us -> 0.01 us  [on_device(): lax.all_to_all(out_lab, 'dp', split_axis=0, concat_axis=0, tiled=True)]
    all_to_all x1 -> x0, starting transfers between devices: 14.8 us -> none  [on_device(): lax.all_to_all(out_emb, 'dp', split_axis=0, concat_axis=0, tiled=True)]
    all_to_all x1, starting transfers between devices: 7.26 us -> 15.2 us  [on_device(): lax.all_to_all(out_lab, 'dp', split_axis=0, concat_axis=0, tiled=True)]
    gather x1, local copies, waits for them, and re-layouts: 29.2 us -> 23.8 us  [on_device(): near = pool_emb[located]]
  transfers between devices with their start and end apart: 2 -> 1, of which waited for: 2 -> 0; matrix products, arithmetic and copies ran while one was open for 35% -> 24% of each run, Pallas kernels for 10% -> 52%
where the time goes in v7:
time: 462 us; the launch traced here: 461 us
  Pallas kernels  313 us (68%)
  other arithmetic  71.1 us (15%)
  local copies, waits for them, and re-layouts  46.6 us (10%)
  starting transfers between devices  15.2 us (3%)
  matrix products  14.3 us (3%)
    pallas_call x1, Pallas kernels, dp_exchange(): pl.pallas_call(functools.partial(_exchange_kernel, n), out_shape=jax.Shap...  205 us
    pallas_call x1, Pallas kernels, grad_reduce(): pl.pallas_call(functools.partial(_grad_kernel, nk, nx, nz, ncls, scale, l...  63.2 us
    unnamed x4, other arithmetic  47.1 us
    pallas_call x3, Pallas kernels, class_gather(): pl.pallas_call(functools.partial(_class_gather_kernel, ncls), out_shape=j...  44.8 us
    gather x1, local copies, waits for them, and re-layouts, on_device(): near = pool_emb[located]  23.8 us
    all_to_all x1, starting transfers between devices, on_device(): lax.all_to_all(out_lab, 'dp', split_axis=0, concat_axis=0, tiled=True)  15.2 us
    convert_element_type x1, other arithmetic, on_device(): dense_lo = (dense - dense_hi.astype(jnp.float32)).astype(jnp.bfloat16)  11 us
    dot_general x1, matrix products, on_device(): both = jnp.dot(stacked, pool_lab, preferred_element_type=jnp.float32)  9.52 us
  transfers between devices with their start and end apart: 1, of which 0 were waited for; matrix products, arithmetic and copies ran while one was open for 24% of the time, Pallas kernels for 52%

profile of v7, /device:TPU:1, one launch (start us, length us, event | category | flops | bytes accessed | tf_op | source)
XLA Modules:
  0.0 461.2 jit_solution(17394386019846139009)
XLA Ops:
  0.6 0.7 fusion.22
  1.4 6.3 %gather_fusion.2 = bf16[64,128,512]{2,1,0:T(8,128)(2,1)} fusion(bf16[2,128,512]{2,1,0:T(8,128)(2,1)} %bitcast.64, s32[1024]{0:T(1024)S(1)} %pad_clamp_fusion), kind=kCustom, calls=%fused_computation.2 | custom fusion | bytes 16777472 | tf_op jit(solution)/shard_map/gather | solution.py:303
  7.7 15.2 %all-to-all-start = ((bf16[64,128,512]{2,1,0:T(8,128)(2,1)}), bf16[64,128,512]{2,1,0:T(8,128)(2,1)}, u32[]{:S(2)}, u32[]{:S(2)}) async-start(bf16[64,128,512]{2,1,0:T(8,128)(2,1)} %gather_fusion.2), calls=%async_computation | async-start | bytes 16777216 | tf_op jit(solution)/shard_map/all_to_all | solution.py:304
  23.6 20.4 %shard_map.87 = bf16[8,256,128]{2,1,0:T(8,128)(2,1)} custom-call(bf16[256,128]{1,0:T(8,128)(2,1)} %x_ref.1), custom_call_target="tpu_custom_call" | custom-call | tf_op jit(solution)/shard_map/pallas_call | solution.py:235
  44.0 2.0 copy.23
  46.1 2.2 gather_fusion
  48.2 205.2 %shard_map.86 = bf16[64,128,128]{2,1,0:T(8,128)(2,1)} custom-call(bf16[64,128,128]{2,1,0:T(8,128)(2,1)} %gather_fusion), custom_call_target="tpu_custom_call" | custom-call | tf_op jit(solution)/shard_map/pallas_call | solution.py:277
  253.4 23.8 %gather_fusion.1 = bf16[8192,128]{1,0:T(8,128)(2,1)S(1)} fusion(bf16[8192,128]{1,0:T(8,128)(2,1)} %bitcast.65, s32[8192]{0:T(1024)S(1)} %broadcast_clamp_fusion), kind=kCustom, calls=%fused_computation.1 | custom fusion | bytes 4227072 | tf_op jit(solution)/shard_map/gather | solution.py:318
  277.2 1.2 fusion.9
  278.5 1.6 fusion.26
  280.3 0.6 pad_maximum_fusion.1.x_ref
  280.9 15.7 %shard_map.88 = f32[8,34,256]{2,1,0:T(8,128)} custom-call(f32[34,256]{1,0:T(8,128)} %pad_maximum_fusion.1.x_ref), custom_call_target="tpu_custom_call" | custom-call | tf_op jit(solution)/shard_map/pallas_call | solution.py:235
  296.6 1.0 slice_reduce_fusion
  297.9 46.9 %scatter_custom_fusion = f32[2097152]{0:T(1024)} fusion(s32[8192]{0:T(1024)S(1)} %reshape.103, f32[8192]{0:T(1024)S(1)} %reshape.105, f32[]{:T(128)} %constant.10.clone.1), kind=kCustom, calls=%fused_computation.6 | custom fusion | flops 8192 | bytes 8388612
  344.8 9.4 %reshape.78 = f32[256,8192]{1,0:T(8,128)} reshape(f32[2097152]{0:T(1024)} %scatter_custom_fusion) | data formatting | bytes 16777216 | tf_op jit(solution)/shard_map/scatter-add | solution.py:337
  354.2 11.0 %subtract_convert_fusion = (bf16[256,8192]{1,0:T(8,128)(2,1)}, bf16[256,8192]{1,0:T(8,128)(2,1)}) fusion(f32[256,8192]{1,0:T(8,128)} %reshape.78), kind=kLoop, calls=%fused_computation.5 | loop fusion | flops 8388608 | bytes 16777216 | tf_op jit(solution)/shard_map/convert_element_type | solution.py:341
  365.2 7.7 %pad_maximum_fusion = bf16[512,8192]{1,0:T(8,128)(2,1)} fusion(bf16[256,8192]{1,0:T(8,128)(2,1)} %get-tuple-element.4, bf16[256,8192]{1,0:T(8,128)(2,1)} %get-tuple-element.5), kind=kLoop, calls=%fused_computation.4 | loop fusion | flops 16777216 | bytes 16777216 | tf_op jit(solution)/shard_map/concatenate | solution.py:342
  372.9 9.5 %fusion.27 = f32[512,512]{1,0:T(8,128)S(1)} fusion(bf16[512,8192]{1,0:T(8,128)(2,1)} %pad_maximum_fusion, bf16[8192,512]{1,0:T(8,128)(2,1)} %bitcast.15), kind=kOutput, calls=%fused_computation.56 | convolution fusion | flops 4294967296 | bytes 17825792 | tf_op jit(solution)/shard_map/dot_general | solution.py:343
  382.6 0.9 exponential_reduce_fusion
  384.0 8.7 %shard_map.89 = f32[8,2,256]{2,1,0:T(2,128)} custom-call(f32[2,256]{1,0:T(2,128)} %pad_maximum_fusion.2.x_ref), custom_call_target="tpu_custom_call" | custom-call | tf_op jit(solution)/shard_map/pallas_call | solution.py:235
  392.7 1.0 slice_reduce_fusion.1
  393.7 2.0 convolution_bitcast_fusion.part_ref
  395.8 63.2 %shard_map.90 = bf16[1024,512]{1,0:T(8,128)(2,1)} custom-call(f32[1024,512]{1,0:T(8,128)} %convolution_bitcast_fusion.part_ref), custom_call_target="tpu_custom_call" | custom-call | tf_op jit(solution)/shard_map/pallas_call | solution.py:189
  459.0 2.3 copy.63
  (41 shorter events, 2.0 us)
Async XLA Ops:
  0.6 277.8 %copy-start = (bf16[1024,512]{1,0:T(8,128)(2,1)S(1)}, bf16[1024,512]{1,0:T(8,128)(2,1)}, u32[]{:S(2)}) copy-start(bf16[1024,512]{1,0:T(8,128)(2,1)} %param.9) | copy-start | bytes 3145732
  7.7 15.2 %copy-start.4 = (s32[256,32]{0,1:T(8,128)S(1)}, s32[256,32]{0,1:T(8,128)}, u32[]{:S(2)}) copy-start(s32[256,32]{0,1:T(8,128)} %param.12) | copy-start | bytes 98308
  7.7 15.2 %copy-start.5 = (s32[256,32]{0,1:T(8,128)S(1)}, s32[256,32]{0,1:T(8,128)}, u32[]{:S(2)}) copy-start(s32[256,32]{0,1:T(8,128)} %param.11) | copy-start | bytes 98308
  7.7 15.4 %copy-start.7 = (s32[2]{0:T(128)S(1)}, s32[2]{0:T(128)}, u32[]{:S(2)}) copy-start(s32[2]{0:T(128)} %constant.27) | copy-start | bytes 28
  7.7 15.5 %copy-start.8 = (s32[2]{0:T(128)S(1)}, s32[2]{0:T(128)}, u32[]{:S(2)}) copy-start(s32[2]{0:T(128)} %constant.30) | copy-start | bytes 28
  7.7 38.3 %copy-start.2 = (bf16[256,128]{1,0:T(8,128)(2,1)S(1)}, bf16[256,128]{1,0:T(8,128)(2,1)}, u32[]{:S(2)}) copy-start(bf16[256,128]{1,0:T(8,128)(2,1)} %x_ref.1) | copy-start | bytes 196612
  7.7 365.1 %all-to-all-start = ((bf16[64,128,512]{2,1,0:T(8,128)(2,1)}), bf16[64,128,512]{2,1,0:T(8,128)(2,1)}, u32[]{:S(2)}, u32[]{:S(2)}) async-start(bf16[64,128,512]{2,1,0:T(8,128)(2,1)} %gather_fusion.2), calls=%async_computation | async-start | bytes 16777216 | tf_op jit(solution)/shard_map/all_to_all | solution.py:304
  253.4 44.2 %copy-start.6 = (s32[256]{0:T(256)S(1)}, s32[256]{0:T(256)}, u32[]{:S(2)}) copy-start(s32[256]{0:T(256)} %param.13) | copy-start | bytes 3076
  372.9 9.5 %copy-start.1 = (bf16[256,512]{1,0:T(8,128)(2,1)S(1)}, bf16[256,512]{1,0:T(8,128)(2,1)}, u32[]{:S(2)}) copy-start(bf16[256,512]{1,0:T(8,128)(2,1)} %param.8) | copy-start | bytes 786436
  372.9 20.9 %copy-start.3 = (bf16[256,8,128]{0,2,1:T(8,128)(2,1)S(1)}, bf16[256,8,128]{0,2,1:T(8,128)(2,1)}, u32[]{:S(2)}) copy-start(bf16[256,8,128]{0,2,1:T(8,128)(2,1)} %copy.23) | copy-start | bytes 1572868

commit v8 on v7

--- a/solution.py
+++ b/solution.py
@@ -301,8 +301,9 @@
     picks = send_blocks[0]
     out_emb = embeddings.reshape(rows // BLOCK, BLOCK, width_part)[picks]
     out_lab = labels.reshape(rows // BLOCK, BLOCK, class_part)[picks]
+    pool_emb = dp_exchange(out_emb, dp_count, 4)
+    pool_emb, out_lab = lax.optimization_barrier((pool_emb, out_lab))
     pool_lab = lax.all_to_all(out_lab, "dp", split_axis=0, concat_axis=0, tiled=True)
-    pool_emb = dp_exchange(out_emb, dp_count, 4)
     pool_rows = dp_count * BLOCK
     pool_emb = pool_emb.reshape(pool_rows, width_part)
     pool_lab = pool_lab.reshape(pool_rows, class_part)

time: 462 us -> 359 us (0.78)
  Pallas kernels: 313 us -> 169 us
  waiting for transfers between devices: 0.01 us -> 31.5 us
  local copies, waits for them, and re-layouts: 46.6 us -> 54.9 us
    pallas_call x1, Pallas kernels: 205 us -> 62.9 us  [dp_exchange(): pl.pallas_call(functools.partial(_exchange_kernel, n), out_shape=jax.Shap...]
    all_to_all x1, waiting for transfers between devices: 0.01 us -> 31.5 us  [on_device(): lax.all_to_all(out_lab, 'dp', split_axis=0, concat_axis=0, tiled=True)]
    gather x1, local copies, waits for them, and re-layouts: 23.8 us -> 29.2 us  [on_device(): near = pool_emb[located]]
  transfers between devices with their start and end apart: 1 -> 1, of which waited for: 0 -> 1; matrix products, arithmetic and copies ran while one was open for 24% -> 33% of each run, Pallas kernels for 52% -> 9%
where the time goes in v8:
time: 359 us; the launch traced here: 358 us
  Pallas kernels  169 us (47%)
  other arithmetic  71.9 us (20%)
  local copies, waits for them, and re-layouts  54.9 us (15%)
  waiting for transfers between devices  31.5 us (9%)
  matrix products  15.8 us (4%)
  starting transfers between devices  13.4 us (4%)
    pallas_call x1, Pallas kernels, grad_reduce(): pl.pallas_call(functools.partial(_grad_kernel, nk, nx, nz, ncls, scale, l...  63.3 us
    pallas_call x1, Pallas kernels, dp_exchange(): pl.pallas_call(functools.partial(_exchange_kernel, n), out_shape=jax.Shap...  62.9 us
    unnamed x4, other arithmetic  47.9 us
    pallas_call x3, Pallas kernels, class_gather(): pl.pallas_call(functools.partial(_class_gather_kernel, ncls), out_shape=j...  43 us
    all_to_all x1, waiting for transfers between devices, on_device(): lax.all_to_all(out_lab, 'dp', split_axis=0, concat_axis=0, tiled=True)  31.5 us
    gather x1, local copies, waits for them, and re-layouts, on_device(): near = pool_emb[located]  29.2 us
    all_to_all x1, starting transfers between devices, on_device(): lax.all_to_all(out_lab, 'dp', split_axis=0, concat_axis=0, tiled=True)  13.4 us
    convert_element_type x1, other arithmetic, on_device(): dense_lo = (dense - dense_hi.astype(jnp.float32)).astype(jnp.bfloat16)  11 us
  transfers between devices with their start and end apart: 1, of which 1 were waited for; matrix products, arithmetic and copies ran while one was open for 33% of the time, Pallas kernels for 9%

profile of v8, /device:TPU:1, one launch (start us, length us, event | category | flops | bytes accessed | tf_op | source)
XLA Modules:
  0.0 357.6 jit_solution(9450855055921623290)
XLA Ops:
  1.4 3.0 gather_fusion
  4.4 62.9 %shard_map.86 = bf16[64,128,128]{2,1,0:T(8,128)(2,1)} custom-call(bf16[64,128,128]{2,1,0:T(8,128)(2,1)} %gather_fusion), custom_call_target="tpu_custom_call" | custom-call | tf_op jit(solution)/shard_map/pallas_call | solution.py:277
  67.4 5.4 %gather_fusion.1 = bf16[64,128,512]{2,1,0:T(8,128)(2,1)} fusion(bf16[2,128,512]{2,1,0:T(8,128)(2,1)S(1)} %bitcast.64, s32[1024]{0:T(1024)S(1)} %pad_clamp_fusion), kind=kCustom, calls=%fused_computation.1 | custom fusion | bytes 16777472 | tf_op jit(solution)/shard_map/gather | solution.py:303
  72.8 13.4 %all-to-all-start = ((bf16[64,128,512]{2,1,0:T(8,128)(2,1)}), bf16[64,128,512]{2,1,0:T(8,128)(2,1)}, u32[]{:S(2)}, u32[]{:S(2)}) async-start(bf16[64,128,512]{2,1,0:T(8,128)(2,1)} %gather_fusion.1), calls=%async_computation | async-start | bytes 16777216 | tf_op jit(solution)/shard_map/all_to_all | solution.py:306
  86.2 20.4 %shard_map.87 = bf16[8,256,128]{2,1,0:T(8,128)(2,1)} custom-call(bf16[256,128]{1,0:T(8,128)(2,1)} %x_ref.1), custom_call_target="tpu_custom_call" | custom-call | tf_op jit(solution)/shard_map/pallas_call | solution.py:235
  109.8 1.0 reshape.97
  110.8 2.0 copy.23
  112.8 29.2 %gather_fusion.2 = bf16[8192,128]{1,0:T(8,128)(2,1)} fusion(bf16[8192,128]{1,0:T(8,128)(2,1)S(1)} %bitcast.65, s32[8192]{0:T(1024)S(1)} %broadcast_clamp_fusion), kind=kCustom, calls=%fused_computation.2 | custom fusion | bytes 4227072 | tf_op jit(solution)/shard_map/gather | solution.py:319
  142.1 2.8 fusion.9
  144.9 1.6 fusion.26
  147.4 13.3 %shard_map.88 = f32[8,34,256]{2,1,0:T(8,128)} custom-call(f32[34,256]{1,0:T(8,128)} %pad_maximum_fusion.1.x_ref), custom_call_target="tpu_custom_call" | custom-call | tf_op jit(solution)/shard_map/pallas_call | solution.py:235
  160.7 1.0 slice_reduce_fusion
  161.9 47.1 %scatter_custom_fusion = f32[2097152]{0:T(1024)} fusion(s32[8192]{0:T(1024)} %reshape.103, f32[8192]{0:T(1024)S(1)} %reshape.105, f32[]{:T(128)} %constant.10.clone.1), kind=kCustom, calls=%fused_computation.6 | custom fusion | flops 8192 | bytes 8389120
  209.0 9.4 %reshape.78 = f32[256,8192]{1,0:T(8,128)} reshape(f32[2097152]{0:T(1024)} %scatter_custom_fusion) | data formatting | bytes 16777216 | tf_op jit(solution)/shard_map/scatter-add | solution.py:338
  218.4 11.0 %subtract_convert_fusion = (bf16[256,8192]{1,0:T(8,128)(2,1)}, bf16[256,8192]{1,0:T(8,128)(2,1)}) fusion(f32[256,8192]{1,0:T(8,128)} %reshape.78), kind=kLoop, calls=%fused_computation.5 | loop fusion | flops 8388608 | bytes 16777216 | tf_op jit(solution)/shard_map/convert_element_type | solution.py:342
  229.4 7.7 %pad_maximum_fusion = bf16[512,8192]{1,0:T(8,128)(2,1)} fusion(bf16[256,8192]{1,0:T(8,128)(2,1)} %get-tuple-element.8, bf16[256,8192]{1,0:T(8,128)(2,1)} %get-tuple-element.9), kind=kLoop, calls=%fused_computation.4 | loop fusion | flops 16777216 | bytes 16777216 | tf_op jit(solution)/shard_map/concatenate | solution.py:343
  237.1 31.5 %all-to-all-done = bf16[64,128,512]{2,1,0:T(8,128)(2,1)} async-done(((bf16[64,128,512]{2,1,0:T(8,128)(2,1)}), bf16[64,128,512]{2,1,0:T(8,128)(2,1)}, u32[]{:S(2)}, u32[]{:S(2)}) %all-to-all-start) | async-done | bytes 8388640 | tf_op jit(solution)/shard_map/all_to_all | solution.py:306
  268.6 9.5 %fusion.27 = f32[512,512]{1,0:T(8,128)S(1)} fusion(bf16[512,8192]{1,0:T(8,128)(2,1)} %pad_maximum_fusion, bf16[8192,512]{1,0:T(8,128)(2,1)} %bitcast.15), kind=kOutput, calls=%fused_computation.56 | convolution fusion | flops 4294967296 | bytes 17825792 | tf_op jit(solution)/shard_map/dot_general | solution.py:344
  278.2 0.9 exponential_reduce_fusion
  279.7 9.3 %shard_map.89 = f32[8,2,256]{2,1,0:T(2,128)} custom-call(f32[2,256]{1,0:T(2,128)} %pad_maximum_fusion.2.x_ref), custom_call_target="tpu_custom_call" | custom-call | tf_op jit(solution)/shard_map/pallas_call | solution.py:235
  289.0 1.0 slice_reduce_fusion.1
  290.0 2.0 convolution_bitcast_fusion.part_ref
  292.1 63.3 %shard_map.90 = bf16[1024,512]{1,0:T(8,128)(2,1)} custom-call(f32[1024,512]{1,0:T(8,128)} %convolution_bitcast_fusion.part_ref), custom_call_target="tpu_custom_call" | custom-call | tf_op jit(solution)/shard_map/pallas_call | solution.py:189
  355.3 2.3 copy.63
  (43 shorter events, 6.0 us)
Async XLA Ops:
  0.6 144.3 %copy-start = (bf16[1024,512]{1,0:T(8,128)(2,1)S(1)}, bf16[1024,512]{1,0:T(8,128)(2,1)}, u32[]{:S(2)}) copy-start(bf16[1024,512]{1,0:T(8,128)(2,1)} %param.9) | copy-start | bytes 3145732
  0.6 66.7 %copy-start.1 = (bf16[256,512]{1,0:T(8,128)(2,1)S(1)}, bf16[256,512]{1,0:T(8,128)(2,1)}, u32[]{:S(2)}) copy-start(bf16[256,512]{1,0:T(8,128)(2,1)} %param.8) | copy-start | bytes 786436
  72.7 33.9 %copy-start.5 = (s32[256,32]{0,1:T(8,128)S(1)}, s32[256,32]{0,1:T(8,128)}, u32[]{:S(2)}) copy-start(s32[256,32]{0,1:T(8,128)} %param.12) | copy-start | bytes 98308
  72.7 33.9 %copy-start.6 = (s32[256,32]{0,1:T(8,128)S(1)}, s32[256,32]{0,1:T(8,128)}, u32[]{:S(2)}) copy-start(s32[256,32]{0,1:T(8,128)} %param.11) | copy-start | bytes 98308
  72.7 34.7 %copy-start.8 = (s32[2]{0:T(128)S(1)}, s32[2]{0:T(128)}, u32[]{:S(2)}) copy-start(s32[2]{0:T(128)} %constant.27) | copy-start | bytes 28
  72.7 34.8 %copy-start.9 = (s32[2]{0:T(128)S(1)}, s32[2]{0:T(128)}, u32[]{:S(2)}) copy-start(s32[2]{0:T(128)} %constant.30) | copy-start | bytes 28
  72.7 40.1 %copy-start.2 = (bf16[64,128,128]{2,1,0:T(8,128)(2,1)S(1)}, bf16[64,128,128]{2,1,0:T(8,128)(2,1)}, u32[]{:S(2)}) copy-start(bf16[64,128,128]{2,1,0:T(8,128)(2,1)} %shard_map.86) | copy-start | bytes 6291460
  72.8 195.8 %all-to-all-start = ((bf16[64,128,512]{2,1,0:T(8,128)(2,1)}), bf16[64,128,512]{2,1,0:T(8,128)(2,1)}, u32[]{:S(2)}, u32[]{:S(2)}) async-start(bf16[64,128,512]{2,1,0:T(8,128)(2,1)} %gather_fusion.1), calls=%async_computation | async-start | bytes 16777216 | tf_op jit(solution)/shard_map/all_to_all | solution.py:306
  112.8 29.2 %copy-start.3 = (bf16[256,128]{1,0:T(8,128)(2,1)S(1)}, bf16[256,128]{1,0:T(8,128)(2,1)}, u32[]{:S(2)}) copy-start(bf16[256,128]{1,0:T(8,128)(2,1)} %x_ref.1) | copy-start | bytes 196612
  112.8 48.8 %copy-start.7 = (s32[256]{0:T(256)S(1)}, s32[256]{0:T(256)}, u32[]{:S(2)}) copy-start(s32[256]{0:T(256)} %param.13) | copy-start | bytes 3076
  268.6 21.5 %copy-start.4 = (bf16[256,8,128]{0,2,1:T(8,128)(2,1)S(1)}, bf16[256,8,128]{0,2,1:T(8,128)(2,1)}, u32[]{:S(2)}) copy-start(bf16[256,8,128]{0,2,1:T(8,128)(2,1)} %copy.23) | copy-start | bytes 1572868

commit v9 on v5

--- a/solution.py
+++ b/solution.py
@@ -14,7 +14,7 @@
 
 MESH = pl.DeviceIdType.MESH
 
-def _grad_kernel(nk, nx, nz, ncls, scale, limit, part_ref, out_ref,
+def _grad_kernel(nk, nx, nz, nch, ncls, scale, limit, part_ref, out_ref,
                  recv1, acc1, recv2, acc2, recv3, gath, nrm_dp, nrm_cls,
                  s1, r1, s2, r2, s3, r3, sb, rb, sc, rc, g3s, g3r, g2s, g2r, g1s, g1r):
     n = nk * nx * nz
@@ -53,15 +53,26 @@
 
     k_peers = [lax.rem(kc + e, nk) for e in range(1, nk)]
 
-    def m1(p, mine):
+    chunk = half // nch
+
+    def m1(p, mine, c):
+        part = rows(c * chunk, chunk)
         if mine:
             return pltpu.make_async_remote_copy(
-                src_ref=part_ref.at[rows(p * half, half)], dst_ref=recv1.at[kc],
-                send_sem=s1.at[p], recv_sem=r1.at[kc], device_id=dev(zc, xc, p), device_id_type=MESH)
-        return pltpu.make_async_remote_copy(
-            src_ref=part_ref.at[rows(kc * half, half)], dst_ref=recv1.at[p],
-            send_sem=s1.at[kc], recv_sem=r1.at[p], device_id=dev(zc, xc, p), device_id_type=MESH)
-    exchange(k_peers, m1)
+                src_ref=part_ref.at[rows(p * half + c * chunk, chunk)], dst_ref=recv1.at[kc, part],
+                send_sem=s1.at[p * nch + c], recv_sem=r1.at[kc * nch + c],
+                device_id=dev(zc, xc, p), device_id_type=MESH)
+        return pltpu.make_async_remote_copy(
+            src_ref=part_ref.at[rows(kc * half + c * chunk, chunk)], dst_ref=recv1.at[p, part],
+            send_sem=s1.at[kc * nch + c], recv_sem=r1.at[p * nch + c],
+            device_id=dev(zc, xc, p), device_id_type=MESH)
+    for p in k_peers:
+        for c in range(nch):
+            m1(p, True, c).start()
+    for p in k_peers:
+        for c in range(nch):
+            m1(p, True, c).wait_send()
+            m1(p, False, c).wait_recv()
     a1 = part_ref[rows(kc * half, half), :]
     for p in k_peers:
         a1 = a1 + recv1[p]
@@ -156,14 +167,15 @@
         g2(p, True).wait_send()
         g2(p, False).wait_recv()
 
-    def g1(p, mine):
-        src = (kc if mine else p) * half
-        return pltpu.make_async_remote_copy(
-            src_ref=gath.at[rows(src, half)], dst_ref=gath.at[rows(src, half)],
-            send_sem=g1s.at[p], recv_sem=g1r.at[kc if mine else p],
+    def g1(p, mine, c):
+        src = (kc if mine else p) * half + c * chunk
+        return pltpu.make_async_remote_copy(
+            src_ref=gath.at[rows(src, chunk)], dst_ref=gath.at[rows(src, chunk)],
+            send_sem=g1s.at[p * nch + c], recv_sem=g1r.at[(kc if mine else p) * nch + c],
             device_id=dev(zc, xc, p), device_id_type=MESH)
     for p in k_peers:
-        g1(p, True).start()
+        for c in range(nch):
+            g1(p, True, c).start()
     for t in c_peers:
         c_desc(t, cj).wait_send()
         c_desc(cj, t).wait_recv()
@@ -172,13 +184,14 @@
         tot = tot + nrm_cls[t]
     factor = jnp.minimum(1.0, limit / jnp.sqrt(tot))
     for p in k_peers:
-        g1(p, True).wait_send()
-        g1(p, False).wait_recv()
+        for c in range(nch):
+            g1(p, True, c).wait_send()
+            g1(p, False, c).wait_recv()
     fac = jnp.broadcast_to(factor[0:1, 0:1], out_ref.shape)
     out_ref[...] = (gath[...].astype(jnp.float32) * fac).astype(out_ref.dtype)
 
 
-def grad_reduce(part_grad, n, ncls, scale, limit, nk=2, nx=4):
+def grad_reduce(part_grad, n, ncls, scale, limit, nk=2, nx=4, nch=4):
     nz = n // (nk * nx)
     width = part_grad.shape[1]
     total = part_grad.shape[0]
@@ -187,7 +200,7 @@
     piece = quarter // nz
     dma = pltpu.SemaphoreType.DMA
     return pl.pallas_call(
-        functools.partial(_grad_kernel, nk, nx, nz, ncls, scale, limit),
+        functools.partial(_grad_kernel, nk, nx, nz, nch, ncls, scale, limit),
         out_shape=jax.ShapeDtypeStruct((total, width), jnp.bfloat16),
         in_specs=[pl.BlockSpec(memory_space=pltpu.VMEM)],
         out_specs=pl.BlockSpec(memory_space=pltpu.VMEM),
@@ -200,9 +213,9 @@
             pltpu.VMEM((total, width), jnp.bfloat16),
             pltpu.VMEM((n, 8, 128), jnp.float32),
             pltpu.VMEM((ncls, 8, 128), jnp.float32),
-            dma((nk,)), dma((nk,)), dma((nx,)), dma((nx,)), dma((nz,)), dma((nz,)),
+            dma((nk * nch,)), dma((nk * nch,)), dma((nx,)), dma((nx,)), dma((nz,)), dma((nz,)),
             dma((n,)), dma((n,)), dma((ncls,)), dma((ncls,)),
-            dma((nz,)), dma((nz,)), dma((nx,)), dma((nx,)), dma((nk,)), dma((nk,)),
+            dma((nz,)), dma((nz,)), dma((nx,)), dma((nx,)), dma((nk * nch,)), dma((nk * nch,)),
         ],
         compiler_params=pltpu.CompilerParams(collective_id=0, has_side_effects=True),
     )(part_grad)

time: 350 us -> 350 us (level)
  no operation moved by 1% of the time
where the time goes in v9:
time: 350 us; the launch traced here: 349 us
  Pallas kernels  82.2 us (23%)
  other arithmetic  71.5 us (20%)
  local copies, waits for them, and re-layouts  54.4 us (16%)
  waiting for transfers between devices  54.4 us (16%)
  blocking collectives  47.8 us (14%)
  starting transfers between devices  22.1 us (6%)
  matrix products  15.6 us (4%)
    pallas_call x1, Pallas kernels, grad_reduce(): pl.pallas_call(functools.partial(_grad_kernel, nk, nx, nz, nch, ncls, sca...  63.9 us
    unnamed x4, other arithmetic  47.1 us
    all_to_all x1, waiting for transfers between devices, on_device(): lax.all_to_all(out_emb, 'dp', split_axis=0, concat_axis=0, tiled=True)  44.2 us
    gather x1, local copies, waits for them, and re-layouts, on_device(): near = pool_emb[located]  29.2 us
    psum x1, blocking collectives, on_device(): scores = lax.psum(partial_value, 'class')  25.1 us
    all_gather x1, blocking collectives, on_device(): full_emb = lax.all_gather(embeddings, 'class', axis=1, tiled=True)  22.7 us
    pallas_call x2, Pallas kernels, class_gather(): pl.pallas_call(functools.partial(_class_gather_kernel, ncls), out_shape=j...  18.2 us
    all_to_all x1, starting transfers between devices, on_device(): lax.all_to_all(out_emb, 'dp', split_axis=0, concat_axis=0, tiled=True)  14.8 us
  transfers between devices with their start and end apart: 2, of which 2 were waited for; matrix products, arithmetic and copies ran while one was open for 35% of the time, Pallas kernels for 3%

profile of v9, /device:TPU:1, one launch (start us, length us, event | category | flops | bytes accessed | tf_op | source)
XLA Modules:
  0.0 348.8 jit_solution(13533962236170844850)
XLA Ops:
  1.4 3.0 gather_fusion
  4.5 14.8 %all-to-all-start = ((bf16[64,128,128]{2,1,0:T(8,128)(2,1)}), bf16[64,128,128]{2,1,0:T(8,128)(2,1)S(1)}, u32[]{:S(2)}, u32[]{:S(2)}) async-start(bf16[64,128,128]{2,1,0:T(8,128)(2,1)} %gather_fusion), calls=%async_computation | async-start | bytes 4194304 | tf_op jit(solution)/shard_map/all_to_all | solution.py:275
  19.3 5.4 %gather_fusion.2 = bf16[64,128,512]{2,1,0:T(8,128)(2,1)} fusion(bf16[2,128,512]{2,1,0:T(8,128)(2,1)S(1)} %bitcast.49, s32[1024]{0:T(1024)S(1)} %pad_clamp_fusion), kind=kCustom, calls=%fused_computation.2 | custom fusion | bytes 16777472 | tf_op jit(solution)/shard_map/gather | solution.py:274
  24.8 44.2 %all-to-all-done = bf16[64,128,128]{2,1,0:T(8,128)(2,1)S(1)} async-done(((bf16[64,128,128]{2,1,0:T(8,128)(2,1)}), bf16[64,128,128]{2,1,0:T(8,128)(2,1)S(1)}, u32[]{:S(2)}, u32[]{:S(2)}) %all-to-all-start) | async-done | bytes 2097184 | tf_op jit(solution)/shard_map/all_to_all | solution.py:275
  69.0 7.3 %all-to-all-start.1 = ((bf16[64,128,512]{2,1,0:T(8,128)(2,1)}), bf16[64,128,512]{2,1,0:T(8,128)(2,1)}, u32[]{:S(2)}, u32[]{:S(2)}) async-start(bf16[64,128,512]{2,1,0:T(8,128)(2,1)} %gather_fusion.2), calls=%async_computation.1 | async-start | bytes 16777216 | tf_op jit(solution)/shard_map/all_to_all | solution.py:276
  77.7 22.7 %all_gather.3 = bf16[256,1024]{1,0:T(8,128)(2,1)S(1)} all-gather(bf16[256,128]{1,0:T(8,128)(2,1)S(1)} %copy-done.3), channel_id=1, replica_groups=mesh['dp'=64,'class'=8] {'class'}, dimensions={1}, use_global_device_ids=true | all-gather | bytes 589824 | tf_op jit(solution)/shard_map/all_gather | solution.py:282
  101.2 1.2 fusion.26
  102.5 2.0 copy.26
  104.5 1.3 exponential_reduce_fusion.1
  106.4 8.9 %shard_map.86 = f32[8,2,256]{2,1,0:T(2,128)} custom-call(f32[2,256]{1,0:T(2,128)} %pad_maximum_fusion.1.x_ref), custom_call_target="tpu_custom_call" | custom-call | tf_op jit(solution)/shard_map/pallas_call | solution.py:248
  116.2 29.2 %gather_fusion.1 = bf16[8192,128]{1,0:T(8,128)(2,1)} fusion(bf16[8192,128]{1,0:T(8,128)(2,1)S(1)} %bitcast.50, s32[8192]{0:T(1024)S(1)} %broadcast_clamp_fusion), kind=kCustom, calls=%fused_computation.1 | custom fusion | bytes 4227072 | tf_op jit(solution)/shard_map/gather | solution.py:291
  145.4 2.8 fusion.9
  148.2 25.1 %psum.7 = f32[256,32]{1,0:T(8,128)S(1)} all-reduce(f32[256,32]{1,0:T(8,128)S(1)} %bitcast.56), channel_id=1, replica_groups=mesh['dp'=64,'class'=8] {'class'}, use_global_device_ids=true, to_apply=%region_0.0 | all-reduce | flops 8192 | bytes 65536 | tf_op jit(solution)/shard_map/psum | solution.py:295
  174.0 46.9 %scatter_custom_fusion = f32[2097152]{0:T(1024)} fusion(s32[8192]{0:T(1024)S(1)} %reshape.99, f32[8192]{0:T(1024)S(1)} %reshape.101, f32[]{:T(128)} %constant.10.clone.1), kind=kCustom, calls=%fused_computation.6 | custom fusion | flops 8192 | bytes 8388612
  220.9 9.4 %reshape.74 = f32[256,8192]{1,0:T(8,128)} reshape(f32[2097152]{0:T(1024)} %scatter_custom_fusion) | data formatting | bytes 16777216 | tf_op jit(solution)/shard_map/scatter-add | solution.py:303
  230.3 11.0 %subtract_convert_fusion = (bf16[256,8192]{1,0:T(8,128)(2,1)}, bf16[256,8192]{1,0:T(8,128)(2,1)}) fusion(f32[256,8192]{1,0:T(8,128)} %reshape.74), kind=kLoop, calls=%fused_computation.5 | loop fusion | flops 8388608 | bytes 16777216 | tf_op jit(solution)/shard_map/convert_element_type | solution.py:307
  241.3 7.7 %pad_maximum_fusion = bf16[512,8192]{1,0:T(8,128)(2,1)} fusion(bf16[256,8192]{1,0:T(8,128)(2,1)} %get-tuple-element.10, bf16[256,8192]{1,0:T(8,128)(2,1)} %get-tuple-element.11), kind=kLoop, calls=%fused_computation.4 | loop fusion | flops 16777216 | bytes 16777216 | tf_op jit(solution)/shard_map/concatenate | solution.py:308
  249.0 10.2 %all-to-all-done.1 = bf16[64,128,512]{2,1,0:T(8,128)(2,1)} async-done(((bf16[64,128,512]{2,1,0:T(8,128)(2,1)}), bf16[64,128,512]{2,1,0:T(8,128)(2,1)}, u32[]{:S(2)}, u32[]{:S(2)}) %all-to-all-start.1) | async-done | bytes 8388640 | tf_op jit(solution)/shard_map/all_to_all | solution.py:276
  259.2 9.6 %fusion.27 = f32[512,512]{0,1:T(8,128)S(1)} fusion(bf16[512,8192]{1,0:T(8,128)(2,1)} %pad_maximum_fusion, bf16[8192,512]{1,0:T(8,128)(2,1)} %bitcast.10), kind=kOutput, calls=%fused_computation.55 | convolution fusion | flops 4294967296 | bytes 17825792 | tf_op jit(solution)/shard_map/dot_general | solution.py:309
  269.6 9.3 %shard_map.87 = f32[8,2,256]{2,1,0:T(2,128)} custom-call(f32[2,256]{1,0:T(2,128)} %pad_maximum_fusion.2.x_ref), custom_call_target="tpu_custom_call" | custom-call | tf_op jit(solution)/shard_map/pallas_call | solution.py:248
  279.8 2.0 convolution_bitcast_fusion.part_ref
  281.8 63.9 %shard_map.88 = bf16[1024,512]{1,0:T(8,128)(2,1)} custom-call(f32[1024,512]{1,0:T(8,128)} %convolution_bitcast_fusion.part_ref), custom_call_target="tpu_custom_call" | custom-call | tf_op jit(solution)/shard_map/pallas_call | solution.py:202
  345.7 0.8 copy.29
  346.6 2.3 copy.62
  (51 shorter events, 6.8 us)
Async XLA Ops:
  0.6 100.6 %copy-start = (bf16[1024,512]{1,0:T(8,128)(2,1)S(1)}, bf16[1024,512]{1,0:T(8,128)(2,1)}, u32[]{:S(2)}) copy-start(bf16[1024,512]{1,0:T(8,128)(2,1)} %param.9) | copy-start | bytes 3145732
  0.6 18.7 %copy-start.2 = (bf16[256,512]{1,0:T(8,128)(2,1)S(1)}, bf16[256,512]{1,0:T(8,128)(2,1)}, u32[]{:S(2)}) copy-start(bf16[256,512]{1,0:T(8,128)(2,1)} %param.8) | copy-start | bytes 786436
  4.5 64.5 %all-to-all-start = ((bf16[64,128,128]{2,1,0:T(8,128)(2,1)}), bf16[64,128,128]{2,1,0:T(8,128)(2,1)S(1)}, u32[]{:S(2)}, u32[]{:S(2)}) async-start(bf16[64,128,128]{2,1,0:T(8,128)(2,1)} %gather_fusion), calls=%async_computation | async-start | bytes 4194304 | tf_op jit(solution)/shard_map/all_to_all | solution.py:275
  24.7 52.4 %copy-start.8 = (s32[256,32]{0,1:T(8,128)S(1)}, s32[256,32]{0,1:T(8,128)}, u32[]{:S(2)}) copy-start(s32[256,32]{0,1:T(8,128)} %param.12) | copy-start | bytes 98308
  24.7 52.4 %copy-start.9 = (s32[256,32]{0,1:T(8,128)S(1)}, s32[256,32]{0,1:T(8,128)}, u32[]{:S(2)}) copy-start(s32[256,32]{0,1:T(8,128)} %param.11) | copy-start | bytes 98308
  24.7 52.6 %copy-start.11 = (s32[2]{0:T(128)S(1)}, s32[2]{0:T(128)}, u32[]{:S(2)}) copy-start(s32[2]{0:T(128)} %constant.27) | copy-start | bytes 28
  24.7 52.7 %copy-start.12 = (s32[2]{0:T(128)S(1)}, s32[2]{0:T(128)}, u32[]{:S(2)}) copy-start(s32[2]{0:T(128)} %constant.30) | copy-start | bytes 28
  24.7 53.0 %copy-start.3 = (bf16[256,128]{1,0:T(8,128)(2,1)S(1)}, bf16[256,128]{1,0:T(8,128)(2,1)}, u32[]{:S(2)}) copy-start(bf16[256,128]{1,0:T(8,128)(2,1)} %param.7) | copy-start | bytes 196612
  69.0 190.2 %all-to-all-start.1 = ((bf16[64,128,512]{2,1,0:T(8,128)(2,1)}), bf16[64,128,512]{2,1,0:T(8,128)(2,1)}, u32[]{:S(2)}, u32[]{:S(2)}) async-start(bf16[64,128,512]{2,1,0:T(8,128)(2,1)} %gather_fusion.2), calls=%async_computation.1 | async-start | bytes 16777216 | tf_op jit(solution)/shard_map/all_to_all | solution.py:276
  100.4 0.8 copy-start.4
  116.2 57.1 %copy-start.10 = (s32[256]{0:T(256)S(1)}, s32[256]{0:T(256)}, u32[]{:S(2)}) copy-start(s32[256]{0:T(256)} %param.13) | copy-start | bytes 3076
  259.1 9.6 %copy-start.6 = (bf16[256,512]{0,1:T(8,128)(2,1)S(1)}, bf16[256,512]{0,1:T(8,128)(2,1)}, u32[]{:S(2)}) copy-start(bf16[256,512]{0,1:T(8,128)(2,1)} %copy.24) | copy-start | bytes 786436
  259.2 20.6 %copy-start.5 = (bf16[256,1024]{1,0:T(8,128)(2,1)S(1)}, bf16[256,1024]{1,0:T(8,128)(2,1)}, u32[]{:S(2)}) copy-start(bf16[256,1024]{1,0:T(8,128)(2,1)} %copy-done.4) | copy-start | bytes 1572868
  259.2 20.7 %copy-start.7 = (f32[256,512]{0,1:T(8,128)S(1)}, f32[256,512]{0,1:T(8,128)}, u32[]{:S(2)}) copy-start(f32[256,512]{0,1:T(8,128)} %copy.26) | copy-start | bytes 1572868
  259.2 89.7 %copy-start.1 = (bf16[1024,512]{1,0:T(8,128)(2,1)S(1)}, bf16[1024,512]{1,0:T(8,128)(2,1)}, u32[]{:S(2)}) copy-start(bf16[1024,512]{1,0:T(8,128)(2,1)} %param.9) | copy-start | bytes 3145732

commit v10 on v9

--- a/solution.py
+++ b/solution.py
@@ -14,9 +14,9 @@
 
 MESH = pl.DeviceIdType.MESH
 
-def _grad_kernel(nk, nx, nz, nch, ncls, scale, limit, part_ref, out_ref,
-                 recv1, acc1, recv2, acc2, recv3, gath, nrm_dp, nrm_cls,
-                 s1, r1, s2, r2, s3, r3, sb, rb, sc, rc, g3s, g3r, g2s, g2r, g1s, g1r):
+def _grad_kernel(nk, nx, nz, nch, ncls, scale, limit, stats_ref, zt_ref, qt_ref, embt_ref,
+                 out_ref, part_ref, sbuf, recv1, acc1, recv2, acc2, recv3, gath, nrm_dp, nrm_cls,
+                 ss, rs, s1, r1, s2, r2, s3, r3, sb, rb, sc, rc, g3s, g3r, g2s, g2r, g1s, g1r):
     n = nk * nx * nz
     me = lax.axis_index("dp")
     cj = lax.axis_index("class")
@@ -44,6 +44,29 @@
         pl.semaphore_signal(barrier, 1, device_id=(me, lax.rem(cj + e, ncls)), device_id_type=MESH)
     pl.semaphore_wait(barrier, n - 1 + ncls - 1)
 
+    c_peers = [lax.rem(cj + e, ncls) for e in range(1, ncls)]
+
+    def st_desc(t, s):
+        return pltpu.make_async_remote_copy(
+            src_ref=stats_ref, dst_ref=sbuf.at[s], send_sem=ss.at[t], recv_sem=rs.at[s],
+            device_id=(me, t), device_id_type=MESH)
+    for t in c_peers:
+        st_desc(t, cj).start()
+    sbuf[cj] = stats_ref[...]
+    for t in c_peers:
+        st_desc(t, cj).wait_send()
+        st_desc(cj, t).wait_recv()
+    top = sbuf[0, 0:1, :]
+    for e in range(1, ncls):
+        top = jnp.maximum(top, sbuf[e, 0:1, :])
+    tot_exp = sbuf[0, 1:2, :] * jnp.exp(sbuf[0, 0:1, :] - top)
+    for e in range(1, ncls):
+        tot_exp = tot_exp + sbuf[e, 1:2, :] * jnp.exp(sbuf[e, 0:1, :] - top)
+    prob_t = jnp.exp(zt_ref[...] - top) / tot_exp
+    diff_t = (qt_ref.shape[0] * ncls * (qt_ref[...] - prob_t)).astype(jnp.bfloat16)
+    part_ref[...] = lax.dot_general(
+        embt_ref[...], diff_t, (((1,), (1,)), ((), ())), preferred_element_type=jnp.float32)
+
     def exchange(peers, make):
         for p in peers:
             make(p, True).start()
@@ -160,7 +183,6 @@
             send_sem=sc.at[t], recv_sem=rc.at[s],
             device_id=(me, t), device_id_type=MESH)
 
-    c_peers = [lax.rem(cj + e, ncls) for e in range(1, ncls)]
     for t in c_peers:
         c_desc(t, cj).start()
     for p in x_peers:
@@ -191,20 +213,23 @@
     out_ref[...] = (gath[...].astype(jnp.float32) * fac).astype(out_ref.dtype)
 
 
-def grad_reduce(part_grad, n, ncls, scale, limit, nk=2, nx=4, nch=4):
+def grad_reduce(stats, z_t, q_t, emb_t, n, ncls, scale, limit, nk=2, nx=4, nch=4):
     nz = n // (nk * nx)
-    width = part_grad.shape[1]
-    total = part_grad.shape[0]
+    width = z_t.shape[0]
+    total = emb_t.shape[0]
     half = total // nk
     quarter = half // nx
     piece = quarter // nz
     dma = pltpu.SemaphoreType.DMA
+    vmem = pl.BlockSpec(memory_space=pltpu.VMEM)
     return pl.pallas_call(
         functools.partial(_grad_kernel, nk, nx, nz, nch, ncls, scale, limit),
         out_shape=jax.ShapeDtypeStruct((total, width), jnp.bfloat16),
-        in_specs=[pl.BlockSpec(memory_space=pltpu.VMEM)],
-        out_specs=pl.BlockSpec(memory_space=pltpu.VMEM),
+        in_specs=[vmem] * 4,
+        out_specs=vmem,
         scratch_shapes=[
+            pltpu.VMEM((total, width), jnp.float32),
+            pltpu.VMEM((ncls,) + stats.shape, jnp.float32),
             pltpu.VMEM((nk, half, width), jnp.float32),
             pltpu.VMEM((half, width), jnp.float32),
             pltpu.VMEM((nx, quarter, width), jnp.float32),
@@ -213,12 +238,13 @@
             pltpu.VMEM((total, width), jnp.bfloat16),
             pltpu.VMEM((n, 8, 128), jnp.float32),
             pltpu.VMEM((ncls, 8, 128), jnp.float32),
+            dma((ncls,)), dma((ncls,)),
             dma((nk * nch,)), dma((nk * nch,)), dma((nx,)), dma((nx,)), dma((nz,)), dma((nz,)),
             dma((n,)), dma((n,)), dma((ncls,)), dma((ncls,)),
             dma((nz,)), dma((nz,)), dma((nx,)), dma((nx,)), dma((nk * nch,)), dma((nk * nch,)),
         ],
         compiler_params=pltpu.CompilerParams(collective_id=0, has_side_effects=True),
-    )(part_grad)
+    )(stats, z_t, q_t, emb_t)
 
 
 def _class_gather_kernel(ncls, x_ref, out_ref, buf, ssem, rsem):
@@ -310,17 +336,13 @@
     spread = both[:rows] + both[rows:]
     target = 4.0 * spread + labels.astype(jnp.float32)
     z_local = jnp.max(target, axis=1)
-    z_top, z_total = _combine_stats(
-        z_local, jnp.sum(jnp.exp(target - z_local[:, None]), axis=1), 2
-    )
-    prob_target = jnp.exp(target - z_top[:, None]) / z_total[:, None]
-    diff = (C * (prob_head - prob_target)).astype(jnp.bfloat16)
-    part_grad = lax.dot_general(
-        full_emb, diff, (((0,), (0,)), ((), ())), preferred_element_type=jnp.float32
-    )
+    z_sum = jnp.sum(jnp.exp(target - z_local[:, None]), axis=1)
     scale = 1.0 / math.sqrt(rows * dp_count)
     limit = 0.5 * math.sqrt(D * C)
-    head_grad = grad_reduce(part_grad, dp_count, lax.axis_size("class"), scale, limit)
+    head_grad = grad_reduce(
+        jnp.stack([z_local, z_sum], axis=0), target.T, prob_head.T, full_emb.T,
+        dp_count, lax.axis_size("class"), scale, limit,
+    )
     return (target.astype(jnp.bfloat16), head_grad)
 
 

time: 350 us -> 341 us (0.974)
  Pallas kernels: 82.2 us -> 76.1 us
  waiting for transfers between devices: 54.4 us -> 50.8 us
    pallas_call x2 -> x1, Pallas kernels: 18.2 us -> 8.93 us  [class_gather(): pl.pallas_call(functools.partial(_class_gather_kernel, ncls), out_shape=j...]
    all_to_all x1, waiting for transfers between devices: 10.2 us -> 6.53 us  [on_device(): lax.all_to_all(out_lab, 'dp', split_axis=0, concat_axis=0, tiled=True)]
  transfers between devices with their start and end apart: 2 -> 2, of which waited for: 2 -> 2; matrix products, arithmetic and copies ran while one was open for 35% -> 36% of each run, Pallas kernels for 3% -> 3%
where the time goes in v10:
time: 341 us; the launch traced here: 340 us
  Pallas kernels  76.1 us (22%)
  other arithmetic  72.6 us (21%)
  local copies, waits for them, and re-layouts  54.5 us (16%)
  waiting for transfers between devices  50.8 us (15%)
  blocking collectives  49.4 us (14%)
  starting transfers between devices  22.1 us (6%)
  matrix products  13.5 us (4%)
    pallas_call x1, Pallas kernels, grad_reduce(): pl.pallas_call(functools.partial(_grad_kernel, nk, nx, nz, nch, ncls, sca...  67.2 us
    unnamed x4, other arithmetic  47.1 us
    all_to_all x1, waiting for transfers between devices, on_device(): lax.all_to_all(out_emb, 'dp', split_axis=0, concat_axis=0, tiled=True)  44.3 us
    gather x1, local copies, waits for them, and re-layouts, on_device(): near = pool_emb[located]  29.2 us
    psum x1, blocking collectives, on_device(): scores = lax.psum(partial_value, 'class')  25.8 us
    all_gather x1, blocking collectives, on_device(): full_emb = lax.all_gather(embeddings, 'class', axis=1, tiled=True)  23.6 us
    all_to_all x1, starting transfers between devices, on_device(): lax.all_to_all(out_emb, 'dp', split_axis=0, concat_axis=0, tiled=True)  14.8 us
    convert_element_type x1, other arithmetic, on_device(): dense_lo = (dense - dense_hi.astype(jnp.float32)).astype(jnp.bfloat16)  11 us
  transfers between devices with their start and end apart: 2, of which 2 were waited for; matrix products, arithmetic and copies ran while one was open for 36% of the time, Pallas kernels for 3%

profile of v10, /device:TPU:1, one launch (start us, length us, event | category | flops | bytes accessed | tf_op | source)
XLA Modules:
  0.0 339.9 jit_solution(728511320753382238)
XLA Ops:
  1.4 3.0 gather_fusion
  4.5 14.8 %all-to-all-start = ((bf16[64,128,128]{2,1,0:T(8,128)(2,1)}), bf16[64,128,128]{2,1,0:T(8,128)(2,1)S(1)}, u32[]{:S(2)}, u32[]{:S(2)}) async-start(bf16[64,128,128]{2,1,0:T(8,128)(2,1)} %gather_fusion), calls=%async_computation | async-start | bytes 4194304 | tf_op jit(solution)/shard_map/all_to_all | solution.py:301
  19.3 5.4 %gather_fusion.2 = bf16[64,128,512]{2,1,0:T(8,128)(2,1)} fusion(bf16[2,128,512]{2,1,0:T(8,128)(2,1)S(1)} %bitcast.38, s32[1024]{0:T(1024)S(1)} %pad_clamp_fusion), kind=kCustom, calls=%fused_computation.2 | custom fusion | bytes 16777472 | tf_op jit(solution)/shard_map/gather | solution.py:300
  24.7 44.3 %all-to-all-done = bf16[64,128,128]{2,1,0:T(8,128)(2,1)S(1)} async-done(((bf16[64,128,128]{2,1,0:T(8,128)(2,1)}), bf16[64,128,128]{2,1,0:T(8,128)(2,1)S(1)}, u32[]{:S(2)}, u32[]{:S(2)}) %all-to-all-start) | async-done | bytes 2097184 | tf_op jit(solution)/shard_map/all_to_all | solution.py:301
  69.0 7.3 %all-to-all-start.1 = ((bf16[64,128,512]{2,1,0:T(8,128)(2,1)}), bf16[64,128,512]{2,1,0:T(8,128)(2,1)}, u32[]{:S(2)}, u32[]{:S(2)}) async-start(bf16[64,128,512]{2,1,0:T(8,128)(2,1)} %gather_fusion.2), calls=%async_computation.1 | async-start | bytes 16777216 | tf_op jit(solution)/shard_map/all_to_all | solution.py:302
  76.3 0.8 copy.22
  77.9 23.6 %all_gather.3 = bf16[256,1024]{0,1:T(8,128)(2,1)S(1)} all-gather(bf16[256,128]{0,1:T(8,128)(2,1)S(1)} %copy.23), channel_id=1, replica_groups=mesh['dp'=64,'class'=8] {'class'}, dimensions={1}, use_global_device_ids=true | all-gather | bytes 589824 | tf_op jit(solution)/shard_map/all_gather | solution.py:308
  102.3 1.3 fusion.16
  103.5 2.0 copy.25
  105.6 1.3 exponential_reduce_fusion
  107.4 8.9 %shard_map.86 = f32[8,2,256]{2,1,0:T(2,128)} custom-call(f32[2,256]{1,0:T(2,128)} %pad_maximum_fusion.2.x_ref), custom_call_target="tpu_custom_call" | custom-call | tf_op jit(solution)/shard_map/pallas_call | solution.py:274
  117.2 1.9 divide_bitcast_fusion.qt_ref
  119.2 29.2 %gather_fusion.1 = bf16[8192,128]{1,0:T(8,128)(2,1)} fusion(bf16[8192,128]{1,0:T(8,128)(2,1)S(1)} %bitcast.39, s32[8192]{0:T(1024)S(1)} %broadcast_clamp_fusion), kind=kCustom, calls=%fused_computation.1 | custom fusion | bytes 4227072 | tf_op jit(solution)/shard_map/gather | solution.py:317
  148.4 2.8 fusion.4
  151.1 25.8 %psum.7 = f32[256,32]{1,0:T(8,128)S(1)} all-reduce(f32[256,32]{1,0:T(8,128)S(1)} %bitcast.47), channel_id=1, replica_groups=mesh['dp'=64,'class'=8] {'class'}, use_global_device_ids=true, to_apply=%region_0.0 | all-reduce | flops 8192 | bytes 65536 | tf_op jit(solution)/shard_map/psum | solution.py:321
  177.7 46.9 %scatter_custom_fusion = f32[2097152]{0:T(1024)} fusion(s32[8192]{0:T(1024)S(1)} %reshape.96, f32[8192]{0:T(1024)S(1)} %reshape.98, f32[]{:T(128)} %constant.9.clone.1), kind=kCustom, calls=%fused_computation.6 | custom fusion | flops 8192 | bytes 8388612
  224.6 9.4 %reshape.71 = f32[256,8192]{1,0:T(8,128)} reshape(f32[2097152]{0:T(1024)} %scatter_custom_fusion) | data formatting | bytes 16777216 | tf_op jit(solution)/shard_map/scatter-add | solution.py:329
  233.9 11.0 %subtract_convert_fusion = (bf16[256,8192]{1,0:T(8,128)(2,1)}, bf16[256,8192]{1,0:T(8,128)(2,1)}) fusion(f32[256,8192]{1,0:T(8,128)} %reshape.71), kind=kLoop, calls=%fused_computation.5 | loop fusion | flops 8388608 | bytes 16777216 | tf_op jit(solution)/shard_map/convert_element_type | solution.py:333
  244.9 7.7 %pad_maximum_fusion = bf16[512,8192]{1,0:T(8,128)(2,1)} fusion(bf16[256,8192]{1,0:T(8,128)(2,1)} %get-tuple-element.10, bf16[256,8192]{1,0:T(8,128)(2,1)} %get-tuple-element.11), kind=kLoop, calls=%fused_computation.4 | loop fusion | flops 16777216 | bytes 16777216 | tf_op jit(solution)/shard_map/concatenate | solution.py:334
  252.6 6.5 %all-to-all-done.1 = bf16[64,128,512]{2,1,0:T(8,128)(2,1)} async-done(((bf16[64,128,512]{2,1,0:T(8,128)(2,1)}), bf16[64,128,512]{2,1,0:T(8,128)(2,1)}, u32[]{:S(2)}, u32[]{:S(2)}) %all-to-all-start.1) | async-done | bytes 8388640 | tf_op jit(solution)/shard_map/all_to_all | solution.py:302
  259.2 9.5 %fusion.17 = f32[512,512]{0,1:T(8,128)S(1)} fusion(bf16[512,8192]{1,0:T(8,128)(2,1)} %pad_maximum_fusion, bf16[8192,512]{1,0:T(8,128)(2,1)} %bitcast.10), kind=kOutput, calls=%fused_computation.42 | convolution fusion | flops 4294967296 | bytes 17825792 | tf_op jit(solution)/shard_map/dot_general | solution.py:335
  269.6 67.2 %shard_map.87 = bf16[1024,512]{1,0:T(8,128)(2,1)} custom-call(f32[2,256]{1,0:T(2,128)} %pad_maximum_fusion.1.stats_ref, f32[512,256]{1,0:T(8,128)} %bitcast.42, f32[512,256]{1,0:T(8,128)} %divide_bitcast_fusion.qt_ref, bf16[1024,256]{1,0:T(8,128)(2,1)} %bitcast.44), custom_call_target="tpu_custom_call" | custom-call | tf_op jit(solution)/shard_map/pallas_call | solution.py:225
  336.8 0.8 copy.26
  337.6 2.3 copy.45
  (45 shorter events, 5.3 us)
Async XLA Ops:
  0.6 101.7 %copy-start = (bf16[1024,512]{1,0:T(8,128)(2,1)S(1)}, bf16[1024,512]{1,0:T(8,128)(2,1)}, u32[]{:S(2)}) copy-start(bf16[1024,512]{1,0:T(8,128)(2,1)} %param.9) | copy-start | bytes 3145732
  0.6 18.7 %copy-start.1 = (bf16[256,512]{1,0:T(8,128)(2,1)S(1)}, bf16[256,512]{1,0:T(8,128)(2,1)}, u32[]{:S(2)}) copy-start(bf16[256,512]{1,0:T(8,128)(2,1)} %param.8) | copy-start | bytes 786436
  4.5 64.5 %all-to-all-start = ((bf16[64,128,128]{2,1,0:T(8,128)(2,1)}), bf16[64,128,128]{2,1,0:T(8,128)(2,1)S(1)}, u32[]{:S(2)}, u32[]{:S(2)}) async-start(bf16[64,128,128]{2,1,0:T(8,128)(2,1)} %gather_fusion), calls=%async_computation | async-start | bytes 4194304 | tf_op jit(solution)/shard_map/all_to_all | solution.py:301
  24.7 52.4 %copy-start.2 = (bf16[256,128]{1,0:T(8,128)(2,1)S(1)}, bf16[256,128]{1,0:T(8,128)(2,1)}, u32[]{:S(2)}) copy-start(bf16[256,128]{1,0:T(8,128)(2,1)} %param.7) | copy-start | bytes 196612
  24.7 52.5 %copy-start.6 = (s32[256,32]{0,1:T(8,128)S(1)}, s32[256,32]{0,1:T(8,128)}, u32[]{:S(2)}) copy-start(s32[256,32]{0,1:T(8,128)} %param.12) | copy-start | bytes 98308
  24.7 52.5 %copy-start.7 = (s32[256,32]{0,1:T(8,128)S(1)}, s32[256,32]{0,1:T(8,128)}, u32[]{:S(2)}) copy-start(s32[256,32]{0,1:T(8,128)} %param.11) | copy-start | bytes 98308
  24.7 52.8 %copy-start.9 = (s32[2]{0:T(128)S(1)}, s32[2]{0:T(128)}, u32[]{:S(2)}) copy-start(s32[2]{0:T(128)} %constant.25) | copy-start | bytes 28
  24.7 52.9 %copy-start.10 = (s32[2]{0:T(128)S(1)}, s32[2]{0:T(128)}, u32[]{:S(2)}) copy-start(s32[2]{0:T(128)} %constant.28) | copy-start | bytes 28
  69.0 190.2 %all-to-all-start.1 = ((bf16[64,128,512]{2,1,0:T(8,128)(2,1)}), bf16[64,128,512]{2,1,0:T(8,128)(2,1)}, u32[]{:S(2)}, u32[]{:S(2)}) async-start(bf16[64,128,512]{2,1,0:T(8,128)(2,1)} %gather_fusion.2), calls=%async_computation.1 | async-start | bytes 16777216 | tf_op jit(solution)/shard_map/all_to_all | solution.py:302
  101.5 0.8 copy-start.4
  119.2 57.8 %copy-start.8 = (s32[256]{0:T(256)S(1)}, s32[256]{0:T(256)}, u32[]{:S(2)}) copy-start(s32[256]{0:T(256)} %param.13) | copy-start | bytes 3076
  259.1 9.5 %copy-start.5 = (bf16[256,512]{0,1:T(8,128)(2,1)S(1)}, bf16[256,512]{0,1:T(8,128)(2,1)}, u32[]{:S(2)}) copy-start(bf16[256,512]{0,1:T(8,128)(2,1)} %copy.22) | copy-start | bytes 786436
  268.8 0.8 copy-start.3

commit v11 on v10

--- a/solution.py
+++ b/solution.py
@@ -54,7 +54,6 @@
         st_desc(t, cj).start()
     sbuf[cj] = stats_ref[...]
     for t in c_peers:
-        st_desc(t, cj).wait_send()
         st_desc(cj, t).wait_recv()
     top = sbuf[0, 0:1, :]
     for e in range(1, ncls):
@@ -67,11 +66,13 @@
     part_ref[...] = lax.dot_general(
         embt_ref[...], diff_t, (((1,), (1,)), ((), ())), preferred_element_type=jnp.float32)
 
+    sent = []
+
     def exchange(peers, make):
         for p in peers:
             make(p, True).start()
+            sent.append(make(p, True))
         for p in peers:
-            make(p, True).wait_send()
             make(p, False).wait_recv()
 
     k_peers = [lax.rem(kc + e, nk) for e in range(1, nk)]
@@ -94,7 +95,7 @@
             m1(p, True, c).start()
     for p in k_peers:
         for c in range(nch):
-            m1(p, True, c).wait_send()
+            sent.append(m1(p, True, c))
             m1(p, False, c).wait_recv()
     a1 = part_ref[rows(kc * half, half), :]
     for p in k_peers:
@@ -167,7 +168,6 @@
         g2(p, True).start()
 
     def b_wait(d, c):
-        b_desc(lax.rem(me + d, n), me).wait_send()
         b_desc(me, lax.rem(me + d, n)).wait_recv()
         return c
     lax.fori_loop(1, n, b_wait, 0)
@@ -186,7 +186,7 @@
     for t in c_peers:
         c_desc(t, cj).start()
     for p in x_peers:
-        g2(p, True).wait_send()
+        sent.append(g2(p, True))
         g2(p, False).wait_recv()
 
     def g1(p, mine, c):
@@ -199,7 +199,7 @@
         for c in range(nch):
             g1(p, True, c).start()
     for t in c_peers:
-        c_desc(t, cj).wait_send()
+        sent.append(c_desc(t, cj))
         c_desc(cj, t).wait_recv()
     tot = col
     for t in c_peers:
@@ -207,10 +207,19 @@
     factor = jnp.minimum(1.0, limit / jnp.sqrt(tot))
     for p in k_peers:
         for c in range(nch):
-            g1(p, True, c).wait_send()
+            sent.append(g1(p, True, c))
             g1(p, False, c).wait_recv()
     fac = jnp.broadcast_to(factor[0:1, 0:1], out_ref.shape)
     out_ref[...] = (gath[...].astype(jnp.float32) * fac).astype(out_ref.dtype)
+    for t in c_peers:
+        st_desc(t, cj).wait_send()
+    for desc in sent:
+        desc.wait_send()
+
+    def b_sent(d, c):
+        b_desc(lax.rem(me + d, n), me).wait_send()
+        return c
+    lax.fori_loop(1, n, b_sent, 0)
 
 
 def grad_reduce(stats, z_t, q_t, emb_t, n, ncls, scale, limit, nk=2, nx=4, nch=4):

time: 341 us -> 342 us (level)
  no operation moved by 1% of the time
where the time goes in v11:
time: 342 us; the launch traced here: 341 us
  Pallas kernels  77.3 us (23%)
  other arithmetic  72.6 us (21%)
  local copies, waits for them, and re-layouts  54.5 us (16%)
  waiting for transfers between devices  50.8 us (15%)
  blocking collectives  49.4 us (14%)
  starting transfers between devices  22.1 us (6%)
  matrix products  13.5 us (4%)
    pallas_call x1, Pallas kernels, grad_reduce(): pl.pallas_call(functools.partial(_grad_kernel, nk, nx, nz, nch, ncls, sca...  68.3 us
    unnamed x4, other arithmetic  47.1 us
    all_to_all x1, waiting for transfers between devices, on_device(): lax.all_to_all(out_emb, 'dp', split_axis=0, concat_axis=0, tiled=True)  44.3 us
    gather x1, local copies, waits for them, and re-layouts, on_device(): near = pool_emb[located]  29.2 us
    psum x1, blocking collectives, on_device(): scores = lax.psum(partial_value, 'class')  25.8 us
    all_gather x1, blocking collectives, on_device(): full_emb = lax.all_gather(embeddings, 'class', axis=1, tiled=True)  23.6 us
    all_to_all x1, starting transfers between devices, on_device(): lax.all_to_all(out_emb, 'dp', split_axis=0, concat_axis=0, tiled=True)  14.8 us
    convert_element_type x1, other arithmetic, on_device(): dense_lo = (dense - dense_hi.astype(jnp.float32)).astype(jnp.bfloat16)  11 us
  transfers between devices with their start and end apart: 2, of which 2 were waited for; matrix products, arithmetic and copies ran while one was open for 36% of the time, Pallas kernels for 3%

profile of v11, /device:TPU:1, one launch (start us, length us, event | category | flops | bytes accessed | tf_op | source)
XLA Modules:
  0.0 341.0 jit_solution(2040527977571061542)
XLA Ops:
  1.4 3.0 gather_fusion
  4.5 14.8 %all-to-all-start = ((bf16[64,128,128]{2,1,0:T(8,128)(2,1)}), bf16[64,128,128]{2,1,0:T(8,128)(2,1)S(1)}, u32[]{:S(2)}, u32[]{:S(2)}) async-start(bf16[64,128,128]{2,1,0:T(8,128)(2,1)} %gather_fusion), calls=%async_computation | async-start | bytes 4194304 | tf_op jit(solution)/shard_map/all_to_all | solution.py:310
  19.3 5.4 %gather_fusion.2 = bf16[64,128,512]{2,1,0:T(8,128)(2,1)} fusion(bf16[2,128,512]{2,1,0:T(8,128)(2,1)S(1)} %bitcast.38, s32[1024]{0:T(1024)S(1)} %pad_clamp_fusion), kind=kCustom, calls=%fused_computation.2 | custom fusion | bytes 16777472 | tf_op jit(solution)/shard_map/gather | solution.py:309
  24.7 44.3 %all-to-all-done = bf16[64,128,128]{2,1,0:T(8,128)(2,1)S(1)} async-done(((bf16[64,128,128]{2,1,0:T(8,128)(2,1)}), bf16[64,128,128]{2,1,0:T(8,128)(2,1)S(1)}, u32[]{:S(2)}, u32[]{:S(2)}) %all-to-all-start) | async-done | bytes 2097184 | tf_op jit(solution)/shard_map/all_to_all | solution.py:310
  69.0 7.3 %all-to-all-start.1 = ((bf16[64,128,512]{2,1,0:T(8,128)(2,1)}), bf16[64,128,512]{2,1,0:T(8,128)(2,1)}, u32[]{:S(2)}, u32[]{:S(2)}) async-start(bf16[64,128,512]{2,1,0:T(8,128)(2,1)} %gather_fusion.2), calls=%async_computation.1 | async-start | bytes 16777216 | tf_op jit(solution)/shard_map/all_to_all | solution.py:311
  76.3 0.8 copy.22
  77.9 23.6 %all_gather.3 = bf16[256,1024]{0,1:T(8,128)(2,1)S(1)} all-gather(bf16[256,128]{0,1:T(8,128)(2,1)S(1)} %copy.23), channel_id=1, replica_groups=mesh['dp'=64,'class'=8] {'class'}, dimensions={1}, use_global_device_ids=true | all-gather | bytes 589824 | tf_op jit(solution)/shard_map/all_gather | solution.py:317
  102.3 1.3 fusion.16
  103.5 2.0 copy.25
  105.6 1.3 exponential_reduce_fusion
  107.4 8.9 %shard_map.86 = f32[8,2,256]{2,1,0:T(2,128)} custom-call(f32[2,256]{1,0:T(2,128)} %pad_maximum_fusion.2.x_ref), custom_call_target="tpu_custom_call" | custom-call | tf_op jit(solution)/shard_map/pallas_call | solution.py:283
  117.2 1.9 divide_bitcast_fusion.qt_ref
  119.2 29.2 %gather_fusion.1 = bf16[8192,128]{1,0:T(8,128)(2,1)} fusion(bf16[8192,128]{1,0:T(8,128)(2,1)S(1)} %bitcast.39, s32[8192]{0:T(1024)S(1)} %broadcast_clamp_fusion), kind=kCustom, calls=%fused_computation.1 | custom fusion | bytes 4227072 | tf_op jit(solution)/shard_map/gather | solution.py:326
  148.4 2.8 fusion.4
  151.1 25.8 %psum.7 = f32[256,32]{1,0:T(8,128)S(1)} all-reduce(f32[256,32]{1,0:T(8,128)S(1)} %bitcast.47), channel_id=1, replica_groups=mesh['dp'=64,'class'=8] {'class'}, use_global_device_ids=true, to_apply=%region_0.0 | all-reduce | flops 8192 | bytes 65536 | tf_op jit(solution)/shard_map/psum | solution.py:330
  177.7 46.9 %scatter_custom_fusion = f32[2097152]{0:T(1024)} fusion(s32[8192]{0:T(1024)S(1)} %reshape.96, f32[8192]{0:T(1024)S(1)} %reshape.98, f32[]{:T(128)} %constant.9.clone.1), kind=kCustom, calls=%fused_computation.6 | custom fusion | flops 8192 | bytes 8388612
  224.6 9.4 %reshape.71 = f32[256,8192]{1,0:T(8,128)} reshape(f32[2097152]{0:T(1024)} %scatter_custom_fusion) | data formatting | bytes 16777216 | tf_op jit(solution)/shard_map/scatter-add | solution.py:338
  233.9 11.0 %subtract_convert_fusion = (bf16[256,8192]{1,0:T(8,128)(2,1)}, bf16[256,8192]{1,0:T(8,128)(2,1)}) fusion(f32[256,8192]{1,0:T(8,128)} %reshape.71), kind=kLoop, calls=%fused_computation.5 | loop fusion | flops 8388608 | bytes 16777216 | tf_op jit(solution)/shard_map/convert_element_type | solution.py:342
  244.9 7.7 %pad_maximum_fusion = bf16[512,8192]{1,0:T(8,128)(2,1)} fusion(bf16[256,8192]{1,0:T(8,128)(2,1)} %get-tuple-element.10, bf16[256,8192]{1,0:T(8,128)(2,1)} %get-tuple-element.11), kind=kLoop, calls=%fused_computation.4 | loop fusion | flops 16777216 | bytes 16777216 | tf_op jit(solution)/shard_map/concatenate | solution.py:343
  252.6 6.5 %all-to-all-done.1 = bf16[64,128,512]{2,1,0:T(8,128)(2,1)} async-done(((bf16[64,128,512]{2,1,0:T(8,128)(2,1)}), bf16[64,128,512]{2,1,0:T(8,128)(2,1)}, u32[]{:S(2)}, u32[]{:S(2)}) %all-to-all-start.1) | async-done | bytes 8388640 | tf_op jit(solution)/shard_map/all_to_all | solution.py:311
  259.2 9.5 %fusion.17 = f32[512,512]{0,1:T(8,128)S(1)} fusion(bf16[512,8192]{1,0:T(8,128)(2,1)} %pad_maximum_fusion, bf16[8192,512]{1,0:T(8,128)(2,1)} %bitcast.10), kind=kOutput, calls=%fused_computation.42 | convolution fusion | flops 4294967296 | bytes 17825792 | tf_op jit(solution)/shard_map/dot_general | solution.py:344
  269.6 68.3 %shard_map.87 = bf16[1024,512]{1,0:T(8,128)(2,1)} custom-call(f32[2,256]{1,0:T(2,128)} %pad_maximum_fusion.1.stats_ref, f32[512,256]{1,0:T(8,128)} %bitcast.42, f32[512,256]{1,0:T(8,128)} %divide_bitcast_fusion.qt_ref, bf16[1024,256]{1,0:T(8,128)(2,1)} %bitcast.44), custom_call_target="tpu_custom_call" | custom-call | tf_op jit(solution)/shard_map/pallas_call | solution.py:234
  337.9 0.8 copy.26
  338.8 2.3 copy.45
  (45 shorter events, 5.3 us)
Async XLA Ops:
  0.6 101.7 %copy-start = (bf16[1024,512]{1,0:T(8,128)(2,1)S(1)}, bf16[1024,512]{1,0:T(8,128)(2,1)}, u32[]{:S(2)}) copy-start(bf16[1024,512]{1,0:T(8,128)(2,1)} %param.9) | copy-start | bytes 3145732
  0.6 18.7 %copy-start.1 = (bf16[256,512]{1,0:T(8,128)(2,1)S(1)}, bf16[256,512]{1,0:T(8,128)(2,1)}, u32[]{:S(2)}) copy-start(bf16[256,512]{1,0:T(8,128)(2,1)} %param.8) | copy-start | bytes 786436
  4.5 64.5 %all-to-all-start = ((bf16[64,128,128]{2,1,0:T(8,128)(2,1)}), bf16[64,128,128]{2,1,0:T(8,128)(2,1)S(1)}, u32[]{:S(2)}, u32[]{:S(2)}) async-start(bf16[64,128,128]{2,1,0:T(8,128)(2,1)} %gather_fusion), calls=%async_computation | async-start | bytes 4194304 | tf_op jit(solution)/shard_map/all_to_all | solution.py:310
  24.7 52.4 %copy-start.2 = (bf16[256,128]{1,0:T(8,128)(2,1)S(1)}, bf16[256,128]{1,0:T(8,128)(2,1)}, u32[]{:S(2)}) copy-start(bf16[256,128]{1,0:T(8,128)(2,1)} %param.7) | copy-start | bytes 196612
  24.7 52.5 %copy-start.6 = (s32[256,32]{0,1:T(8,128)S(1)}, s32[256,32]{0,1:T(8,128)}, u32[]{:S(2)}) copy-start(s32[256,32]{0,1:T(8,128)} %param.12) | copy-start | bytes 98308
  24.7 52.5 %copy-start.7 = (s32[256,32]{0,1:T(8,128)S(1)}, s32[256,32]{0,1:T(8,128)}, u32[]{:S(2)}) copy-start(s32[256,32]{0,1:T(8,128)} %param.11) | copy-start | bytes 98308
  24.7 52.8 %copy-start.9 = (s32[2]{0:T(128)S(1)}, s32[2]{0:T(128)}, u32[]{:S(2)}) copy-start(s32[2]{0:T(128)} %constant.25) | copy-start | bytes 28
  24.7 52.8 %copy-start.10 = (s32[2]{0:T(128)S(1)}, s32[2]{0:T(128)}, u32[]{:S(2)}) copy-start(s32[2]{0:T(128)} %constant.28) | copy-start | bytes 28
  69.0 190.2 %all-to-all-start.1 = ((bf16[64,128,512]{2,1,0:T(8,128)(2,1)}), bf16[64,128,512]{2,1,0:T(8,128)(2,1)}, u32[]{:S(2)}, u32[]{:S(2)}) async-start(bf16[64,128,512]{2,1,0:T(8,128)(2,1)} %gather_fusion.2), calls=%async_computation.1 | async-start | bytes 16777216 | tf_op jit(solution)/shard_map/all_to_all | solution.py:311
  101.5 0.8 copy-start.4
  119.2 57.8 %copy-start.8 = (s32[256]{0:T(256)S(1)}, s32[256]{0:T(256)}, u32[]{:S(2)}) copy-start(s32[256]{0:T(256)} %param.13) | copy-start | bytes 3076
  259.1 9.5 %copy-start.5 = (bf16[256,512]{0,1:T(8,128)(2,1)S(1)}, bf16[256,512]{0,1:T(8,128)(2,1)}, u32[]{:S(2)}) copy-start(bf16[256,512]{0,1:T(8,128)(2,1)} %copy.22) | copy-start | bytes 786436
  268.8 0.8 copy-start.3

commit v12 on v10

--- a/solution.py
+++ b/solution.py
@@ -305,20 +305,25 @@
     pool_lab = pool_lab.reshape(pool_rows, class_part)
     located = nbr_source * BLOCK + nbr_offset
 
-    full_emb = lax.all_gather(embeddings, "class", axis=1, tiled=True)
+    ncls = lax.axis_size("class")
+    emb_all = class_gather(embeddings, ncls, 3)
+    full_emb = jnp.transpose(emb_all, (1, 0, 2)).reshape(rows, ncls * width_part)
     head = jnp.dot(full_emb, head_weight, preferred_element_type=jnp.float32)
-    h_top, h_total = _combine_stats(
-        jnp.max(head, axis=1),
-        jnp.sum(jnp.exp(head - jnp.max(head, axis=1, keepdims=True)), axis=1),
-        1,
-    )
-    prob_head = jnp.exp(head - h_top[:, None]) / h_total[:, None]
+    h_max = jnp.max(head, axis=1)
+    h_sum = jnp.sum(jnp.exp(head - h_max[:, None]), axis=1)
 
     near = pool_emb[located]
     partial_value = jnp.einsum(
-        "rd,rkd->rk", embeddings, near, preferred_element_type=jnp.float32
-    )
-    scores = lax.psum(partial_value, "class")
+        "rd,rkd->kr", embeddings, near, preferred_element_type=jnp.float32
+    )
+    packed = class_gather(
+        jnp.concatenate([partial_value, h_max[None, :], h_sum[None, :]], axis=0), ncls, 1
+    )
+    scores = jnp.sum(packed[:, :nbrs], axis=0).T
+    h_maxes, h_sums = packed[:, nbrs], packed[:, nbrs + 1]
+    h_top = jnp.max(h_maxes, axis=0)
+    h_total = jnp.sum(h_sums * jnp.exp(h_maxes - h_top[None, :]), axis=0)
+    prob_head = jnp.exp(head - h_top[:, None]) / h_total[:, None]
     valid = lax.broadcasted_iota(jnp.int32, (rows, nbrs), 1) < counts[:, None]
     logits = jnp.where(valid, scores / math.sqrt(D), -1e30)
     top = jnp.max(logits, axis=1, keepdims=True)

time: 341 us -> 341 us (level)
  blocking collectives: 49.4 us -> 0 us
  Pallas kernels: 76.1 us -> 101 us
  waiting for transfers between devices: 50.8 us -> 73.3 us
    psum x1 -> x0, blocking collectives: 25.8 us -> none  [on_device(): scores = lax.psum(partial_value, 'class')]
    pallas_call x1 -> x2, Pallas kernels: 8.93 us -> 33.8 us  [class_gather(): pl.pallas_call(functools.partial(_class_gather_kernel, ncls), out_shape=j...]
    all_gather x1 -> x0, blocking collectives: 23.6 us -> none  [on_device(): full_emb = lax.all_gather(embeddings, 'class', axis=1, tiled=True)]
    all_to_all x1, waiting for transfers between devices: 6.53 us -> 29 us  [on_device(): lax.all_to_all(out_lab, 'dp', split_axis=0, concat_axis=0, tiled=True)]
  transfers between devices with their start and end apart: 2 -> 2, of which waited for: 2 -> 2; matrix products, arithmetic and copies ran while one was open for 36% -> 37% of each run, Pallas kernels for 3% -> 10%
where the time goes in v12:
time: 341 us; the launch traced here: 340 us
  Pallas kernels  101 us (30%)
  waiting for transfers between devices  73.3 us (21%)
  other arithmetic  72.3 us (21%)
  local copies, waits for them, and re-layouts  55.8 us (16%)
  starting transfers between devices  22.1 us (6%)
  matrix products  14.5 us (4%)
    pallas_call x1, Pallas kernels, grad_reduce(): pl.pallas_call(functools.partial(_grad_kernel, nk, nx, nz, nch, ncls, sca...  67.2 us
    unnamed x4, other arithmetic  47.1 us
    all_to_all x1, waiting for transfers between devices, on_device(): lax.all_to_all(out_emb, 'dp', split_axis=0, concat_axis=0, tiled=True)  44.3 us
    pallas_call x2, Pallas kernels, class_gather(): pl.pallas_call(functools.partial(_class_gather_kernel, ncls), out_shape=j...  33.8 us
    gather x1, local copies, waits for them, and re-layouts, on_device(): near = pool_emb[located]  29.2 us
    all_to_all x1, waiting for transfers between devices, on_device(): lax.all_to_all(out_lab, 'dp', split_axis=0, concat_axis=0, tiled=True)  29 us
    all_to_all x1, starting transfers between devices, on_device(): lax.all_to_all(out_emb, 'dp', split_axis=0, concat_axis=0, tiled=True)  14.8 us
    convert_element_type x1, other arithmetic, on_device(): dense_lo = (dense - dense_hi.astype(jnp.float32)).astype(jnp.bfloat16)  11 us
  transfers between devices with their start and end apart: 2, of which 2 were waited for; matrix products, arithmetic and copies ran while one was open for 37% of the time, Pallas kernels for 10%

profile of v12, /device:TPU:1, one launch (start us, length us, event | category | flops | bytes accessed | tf_op | source)
XLA Modules:
  0.0 339.9 jit_solution(2925377663084885611)
XLA Ops:
  1.4 3.0 gather_fusion
  4.5 14.8 %all-to-all-start = ((bf16[64,128,128]{2,1,0:T(8,128)(2,1)}), bf16[64,128,128]{2,1,0:T(8,128)(2,1)S(1)}, u32[]{:S(2)}, u32[]{:S(2)}) async-start(bf16[64,128,128]{2,1,0:T(8,128)(2,1)} %gather_fusion), calls=%async_computation | async-start | bytes 4194304 | tf_op jit(solution)/shard_map/all_to_all | solution.py:301
  19.3 5.4 %gather_fusion.2 = bf16[64,128,512]{2,1,0:T(8,128)(2,1)} fusion(bf16[2,128,512]{2,1,0:T(8,128)(2,1)S(1)} %bitcast.54, s32[1024]{0:T(1024)S(1)} %pad_clamp_fusion), kind=kCustom, calls=%fused_computation.2 | custom fusion | bytes 16777472 | tf_op jit(solution)/shard_map/gather | solution.py:300
  24.7 44.3 %all-to-all-done = bf16[64,128,128]{2,1,0:T(8,128)(2,1)S(1)} async-done(((bf16[64,128,128]{2,1,0:T(8,128)(2,1)}), bf16[64,128,128]{2,1,0:T(8,128)(2,1)S(1)}, u32[]{:S(2)}, u32[]{:S(2)}) %all-to-all-start) | async-done | bytes 2097184 | tf_op jit(solution)/shard_map/all_to_all | solution.py:301
  69.0 7.3 %all-to-all-start.1 = ((bf16[64,128,512]{2,1,0:T(8,128)(2,1)}), bf16[64,128,512]{2,1,0:T(8,128)(2,1)}, u32[]{:S(2)}, u32[]{:S(2)}) async-start(bf16[64,128,512]{2,1,0:T(8,128)(2,1)} %gather_fusion.2), calls=%async_computation.1 | async-start | bytes 16777216 | tf_op jit(solution)/shard_map/all_to_all | solution.py:302
  77.1 20.3 %shard_map.86 = bf16[8,256,128]{2,1,0:T(8,128)(2,1)} custom-call(bf16[256,128]{1,0:T(8,128)(2,1)} %x_ref.1), custom_call_target="tpu_custom_call" | custom-call | tf_op jit(solution)/shard_map/pallas_call | solution.py:274
  98.1 2.0 copy.22
  100.1 2.3 fusion.16
  102.4 2.0 copy.26
  104.4 1.3 exponential_reduce_fusion.1
  105.7 29.2 %gather_fusion.1 = bf16[8192,128]{1,0:T(8,128)(2,1)} fusion(bf16[8192,128]{1,0:T(8,128)(2,1)S(1)} %bitcast.55, s32[8192]{0:T(1024)S(1)} %broadcast_clamp_fusion), kind=kCustom, calls=%fused_computation.1 | custom fusion | bytes 4227072 | tf_op jit(solution)/shard_map/gather | solution.py:315
  135.0 2.8 fusion.4
  138.5 13.5 %shard_map.87 = f32[8,34,256]{2,1,0:T(8,128)} custom-call(f32[34,256]{1,0:T(8,128)} %pad_maximum_fusion.1.x_ref), custom_call_target="tpu_custom_call" | custom-call | tf_op jit(solution)/shard_map/pallas_call | solution.py:274
  151.9 1.0 slice_reduce_fusion
  153.2 46.9 %scatter_custom_fusion = f32[2097152]{0:T(1024)} fusion(s32[8192]{0:T(1024)S(1)} %reshape.100, f32[8192]{0:T(1024)S(1)} %reshape.102, f32[]{:T(128)} %constant.9.clone.1), kind=kCustom, calls=%fused_computation.6 | custom fusion | flops 8192 | bytes 8388612
  200.1 9.4 %reshape.75 = f32[256,8192]{1,0:T(8,128)} reshape(f32[2097152]{0:T(1024)} %scatter_custom_fusion) | data formatting | bytes 16777216 | tf_op jit(solution)/shard_map/scatter-add | solution.py:334
  209.5 11.0 %subtract_convert_fusion = (bf16[256,8192]{1,0:T(8,128)(2,1)}, bf16[256,8192]{1,0:T(8,128)(2,1)}) fusion(f32[256,8192]{1,0:T(8,128)} %reshape.75), kind=kLoop, calls=%fused_computation.5 | loop fusion | flops 8388608 | bytes 16777216 | tf_op jit(solution)/shard_map/convert_element_type | solution.py:338
  220.5 7.7 %pad_maximum_fusion = bf16[512,8192]{1,0:T(8,128)(2,1)} fusion(bf16[256,8192]{1,0:T(8,128)(2,1)} %get-tuple-element.10, bf16[256,8192]{1,0:T(8,128)(2,1)} %get-tuple-element.11), kind=kLoop, calls=%fused_computation.4 | loop fusion | flops 16777216 | bytes 16777216 | tf_op jit(solution)/shard_map/concatenate | solution.py:339
  228.2 0.9 slice_reduce_fusion.1
  229.2 0.9 divide_bitcast_fusion.qt_ref
  230.1 29.0 %all-to-all-done.1 = bf16[64,128,512]{2,1,0:T(8,128)(2,1)} async-done(((bf16[64,128,512]{2,1,0:T(8,128)(2,1)}), bf16[64,128,512]{2,1,0:T(8,128)(2,1)}, u32[]{:S(2)}, u32[]{:S(2)}) %all-to-all-start.1) | async-done | bytes 8388640 | tf_op jit(solution)/shard_map/all_to_all | solution.py:302
  259.1 9.5 %fusion.17 = f32[512,512]{0,1:T(8,128)S(1)} fusion(bf16[512,8192]{1,0:T(8,128)(2,1)} %pad_maximum_fusion, bf16[8192,512]{1,0:T(8,128)(2,1)} %bitcast.15), kind=kOutput, calls=%fused_computation.43 | convolution fusion | flops 4294967296 | bytes 17825792 | tf_op jit(solution)/shard_map/dot_general | solution.py:340
  269.6 67.2 %shard_map.88 = bf16[1024,512]{1,0:T(8,128)(2,1)} custom-call(f32[2,256]{1,0:T(2,128)} %pad_maximum_fusion.2.stats_ref, f32[512,256]{1,0:T(8,128)} %bitcast.58, f32[512,256]{1,0:T(8,128)} %divide_bitcast_fusion.qt_ref, bf16[1024,256]{1,0:T(8,128)(2,1)} %bitcast.62), custom_call_target="tpu_custom_call" | custom-call | tf_op jit(solution)/shard_map/pallas_call | solution.py:225
  337.6 2.3 copy.46
  (47 shorter events, 5.0 us)
Async XLA Ops:
  0.6 99.5 %copy-start = (bf16[1024,512]{1,0:T(8,128)(2,1)S(1)}, bf16[1024,512]{1,0:T(8,128)(2,1)}, u32[]{:S(2)}) copy-start(bf16[1024,512]{1,0:T(8,128)(2,1)} %param.9) | copy-start | bytes 3145732
  0.6 18.7 %copy-start.1 = (bf16[256,512]{1,0:T(8,128)(2,1)S(1)}, bf16[256,512]{1,0:T(8,128)(2,1)}, u32[]{:S(2)}) copy-start(bf16[256,512]{1,0:T(8,128)(2,1)} %param.8) | copy-start | bytes 786436
  4.5 64.5 %all-to-all-start = ((bf16[64,128,128]{2,1,0:T(8,128)(2,1)}), bf16[64,128,128]{2,1,0:T(8,128)(2,1)S(1)}, u32[]{:S(2)}, u32[]{:S(2)}) async-start(bf16[64,128,128]{2,1,0:T(8,128)(2,1)} %gather_fusion), calls=%async_computation | async-start | bytes 4194304 | tf_op jit(solution)/shard_map/all_to_all | solution.py:301
  24.7 72.7 %copy-start.6 = (s32[256,32]{0,1:T(8,128)S(1)}, s32[256,32]{0,1:T(8,128)}, u32[]{:S(2)}) copy-start(s32[256,32]{0,1:T(8,128)} %param.12) | copy-start | bytes 98308
  24.7 72.7 %copy-start.7 = (s32[256,32]{0,1:T(8,128)S(1)}, s32[256,32]{0,1:T(8,128)}, u32[]{:S(2)}) copy-start(s32[256,32]{0,1:T(8,128)} %param.11) | copy-start | bytes 98308
  24.7 72.9 %copy-start.9 = (s32[2]{0:T(128)S(1)}, s32[2]{0:T(128)}, u32[]{:S(2)}) copy-start(s32[2]{0:T(128)} %constant.25) | copy-start | bytes 28
  24.7 73.0 %copy-start.10 = (s32[2]{0:T(128)S(1)}, s32[2]{0:T(128)}, u32[]{:S(2)}) copy-start(s32[2]{0:T(128)} %constant.28) | copy-start | bytes 28
  69.0 190.2 %all-to-all-start.1 = ((bf16[64,128,512]{2,1,0:T(8,128)(2,1)}), bf16[64,128,512]{2,1,0:T(8,128)(2,1)}, u32[]{:S(2)}, u32[]{:S(2)}) async-start(bf16[64,128,512]{2,1,0:T(8,128)(2,1)} %gather_fusion.2), calls=%async_computation.1 | async-start | bytes 16777216 | tf_op jit(solution)/shard_map/all_to_all | solution.py:302
  105.7 29.2 %copy-start.2 = (bf16[256,128]{1,0:T(8,128)(2,1)S(1)}, bf16[256,128]{1,0:T(8,128)(2,1)}, u32[]{:S(2)}) copy-start(bf16[256,128]{1,0:T(8,128)(2,1)} %x_ref.1) | copy-start | bytes 196612
  105.7 47.2 %copy-start.8 = (s32[256]{0:T(256)S(1)}, s32[256]{0:T(256)}, u32[]{:S(2)}) copy-start(s32[256]{0:T(256)} %param.13) | copy-start | bytes 3076
  220.5 8.7 %copy-start.4 = (f32[256,512]{0,1:T(8,128)S(1)}, f32[256,512]{0,1:T(8,128)}, u32[]{:S(2)}) copy-start(f32[256,512]{0,1:T(8,128)} %copy.26) | copy-start | bytes 1572868
  259.1 9.5 %copy-start.5 = (bf16[256,512]{0,1:T(8,128)(2,1)S(1)}, bf16[256,512]{0,1:T(8,128)(2,1)}, u32[]{:S(2)}) copy-start(bf16[256,512]{0,1:T(8,128)(2,1)} %copy.24) | copy-start | bytes 786436
  268.8 0.8 copy-start.3

commit v13 on v10

--- a/solution.py
+++ b/solution.py
@@ -15,7 +15,7 @@
 MESH = pl.DeviceIdType.MESH
 
 def _grad_kernel(nk, nx, nz, nch, ncls, scale, limit, stats_ref, zt_ref, qt_ref, embt_ref,
-                 out_ref, part_ref, sbuf, recv1, acc1, recv2, acc2, recv3, gath, nrm_dp, nrm_cls,
+                 out_ref, fac_ref, part_ref, sbuf, recv1, acc1, recv2, acc2, recv3, gath, nrm_dp, nrm_cls,
                  ss, rs, s1, r1, s2, r2, s3, r3, sb, rb, sc, rc, g3s, g3r, g2s, g2r, g1s, g1r):
     n = nk * nx * nz
     me = lax.axis_index("dp")
@@ -209,8 +209,8 @@
         for c in range(nch):
             g1(p, True, c).wait_send()
             g1(p, False, c).wait_recv()
-    fac = jnp.broadcast_to(factor[0:1, 0:1], out_ref.shape)
-    out_ref[...] = (gath[...].astype(jnp.float32) * fac).astype(out_ref.dtype)
+    fac_ref[...] = jnp.broadcast_to(factor[0:1, 0:1], fac_ref.shape)
+    out_ref[...] = gath[...]
 
 
 def grad_reduce(stats, z_t, q_t, emb_t, n, ncls, scale, limit, nk=2, nx=4, nch=4):
@@ -224,9 +224,12 @@
     vmem = pl.BlockSpec(memory_space=pltpu.VMEM)
     return pl.pallas_call(
         functools.partial(_grad_kernel, nk, nx, nz, nch, ncls, scale, limit),
-        out_shape=jax.ShapeDtypeStruct((total, width), jnp.bfloat16),
+        out_shape=(
+            jax.ShapeDtypeStruct((total, width), jnp.bfloat16),
+            jax.ShapeDtypeStruct((8, 128), jnp.float32),
+        ),
         in_specs=[vmem] * 4,
-        out_specs=vmem,
+        out_specs=(vmem, vmem),
         scratch_shapes=[
             pltpu.VMEM((total, width), jnp.float32),
             pltpu.VMEM((ncls,) + stats.shape, jnp.float32),
@@ -339,10 +342,11 @@
     z_sum = jnp.sum(jnp.exp(target - z_local[:, None]), axis=1)
     scale = 1.0 / math.sqrt(rows * dp_count)
     limit = 0.5 * math.sqrt(D * C)
-    head_grad = grad_reduce(
+    gathered, factor = grad_reduce(
         jnp.stack([z_local, z_sum], axis=0), target.T, prob_head.T, full_emb.T,
         dp_count, lax.axis_size("class"), scale, limit,
     )
+    head_grad = (gathered.astype(jnp.float32) * factor[0, 0]).astype(jnp.bfloat16)
     return (target.astype(jnp.bfloat16), head_grad)
 
 

time: 341 us -> 342 us (level)
  no operation moved by 1% of the time
where the time goes in v13:
time: 342 us; the launch traced here: 341 us
  Pallas kernels  75.8 us (22%)
  other arithmetic  75.6 us (22%)
  local copies, waits for them, and re-layouts  53.4 us (16%)
  waiting for transfers between devices  50.8 us (15%)
  blocking collectives  49.4 us (14%)
  starting transfers between devices  22.1 us (6%)
  matrix products  13.5 us (4%)
    pallas_call x1, Pallas kernels, grad_reduce(): pl.pallas_call(functools.partial(_grad_kernel, nk, nx, nz, nch, ncls, sca...  66.9 us
    unnamed x4, other arithmetic  47.1 us
    all_to_all x1, waiting for transfers between devices, on_device(): lax.all_to_all(out_emb, 'dp', split_axis=0, concat_axis=0, tiled=True)  44.2 us
    gather x1, local copies, waits for them, and re-layouts, on_device(): near = pool_emb[located]  29.2 us
    psum x1, blocking collectives, on_device(): scores = lax.psum(partial_value, 'class')  25.8 us
    all_gather x1, blocking collectives, on_device(): full_emb = lax.all_gather(embeddings, 'class', axis=1, tiled=True)  23.6 us
    all_to_all x1, starting transfers between devices, on_device(): lax.all_to_all(out_emb, 'dp', split_axis=0, concat_axis=0, tiled=True)  14.8 us
    convert_element_type x1, other arithmetic, on_device(): dense_lo = (dense - dense_hi.astype(jnp.float32)).astype(jnp.bfloat16)  11 us
  transfers between devices with their start and end apart: 2, of which 2 were waited for; matrix products, arithmetic and copies ran while one was open for 36% of the time, Pallas kernels for 3%

profile of v13, /device:TPU:1, one launch (start us, length us, event | category | flops | bytes accessed | tf_op | source)
XLA Modules:
  0.0 341.4 jit_solution(3935552661051550577)
XLA Ops:
  1.4 3.0 gather_fusion
  4.5 14.8 %all-to-all-start = ((bf16[64,128,128]{2,1,0:T(8,128)(2,1)}), bf16[64,128,128]{2,1,0:T(8,128)(2,1)S(1)}, u32[]{:S(2)}, u32[]{:S(2)}) async-start(bf16[64,128,128]{2,1,0:T(8,128)(2,1)} %gather_fusion), calls=%async_computation | async-start | bytes 4194304 | tf_op jit(solution)/shard_map/all_to_all | solution.py:304
  19.3 5.4 %gather_fusion.2 = bf16[64,128,512]{2,1,0:T(8,128)(2,1)} fusion(bf16[2,128,512]{2,1,0:T(8,128)(2,1)S(1)} %bitcast.39, s32[1024]{0:T(1024)S(1)} %pad_clamp_fusion), kind=kCustom, calls=%fused_computation.2 | custom fusion | bytes 16777472 | tf_op jit(solution)/shard_map/gather | solution.py:303
  24.8 44.2 %all-to-all-done = bf16[64,128,128]{2,1,0:T(8,128)(2,1)S(1)} async-done(((bf16[64,128,128]{2,1,0:T(8,128)(2,1)}), bf16[64,128,128]{2,1,0:T(8,128)(2,1)S(1)}, u32[]{:S(2)}, u32[]{:S(2)}) %all-to-all-start) | async-done | bytes 2097184 | tf_op jit(solution)/shard_map/all_to_all | solution.py:304
  69.0 7.3 %all-to-all-start.1 = ((bf16[64,128,512]{2,1,0:T(8,128)(2,1)}), bf16[64,128,512]{2,1,0:T(8,128)(2,1)}, u32[]{:S(2)}, u32[]{:S(2)}) async-start(bf16[64,128,512]{2,1,0:T(8,128)(2,1)} %gather_fusion.2), calls=%async_computation.1 | async-start | bytes 16777216 | tf_op jit(solution)/shard_map/all_to_all | solution.py:305
  77.9 23.6 %all_gather.3 = bf16[256,1024]{0,1:T(8,128)(2,1)S(1)} all-gather(bf16[256,128]{0,1:T(8,128)(2,1)S(1)} %copy.23), channel_id=1, replica_groups=mesh['dp'=64,'class'=8] {'class'}, dimensions={1}, use_global_device_ids=true | all-gather | bytes 589824 | tf_op jit(solution)/shard_map/all_gather | solution.py:311
  102.3 1.3 fusion.16
  103.5 2.0 copy.25
  105.6 1.3 exponential_reduce_fusion
  107.4 8.9 %shard_map.86 = f32[8,2,256]{2,1,0:T(2,128)} custom-call(f32[2,256]{1,0:T(2,128)} %pad_maximum_fusion.2.x_ref), custom_call_target="tpu_custom_call" | custom-call | tf_op jit(solution)/shard_map/pallas_call | solution.py:277
  117.2 1.9 divide_bitcast_fusion.qt_ref
  119.2 29.2 %gather_fusion.1 = bf16[8192,128]{1,0:T(8,128)(2,1)} fusion(bf16[8192,128]{1,0:T(8,128)(2,1)S(1)} %bitcast.40, s32[8192]{0:T(1024)S(1)} %broadcast_clamp_fusion), kind=kCustom, calls=%fused_computation.1 | custom fusion | bytes 4227072 | tf_op jit(solution)/shard_map/gather | solution.py:320
  148.4 2.8 fusion.4
  151.1 25.8 %psum.7 = f32[256,32]{1,0:T(8,128)S(1)} all-reduce(f32[256,32]{1,0:T(8,128)S(1)} %bitcast.48), channel_id=1, replica_groups=mesh['dp'=64,'class'=8] {'class'}, use_global_device_ids=true, to_apply=%region_0.0 | all-reduce | flops 8192 | bytes 65536 | tf_op jit(solution)/shard_map/psum | solution.py:324
  177.7 46.9 %scatter_custom_fusion = f32[2097152]{0:T(1024)} fusion(s32[8192]{0:T(1024)S(1)} %reshape.96, f32[8192]{0:T(1024)S(1)} %reshape.98, f32[]{:T(128)} %constant.9.clone.1), kind=kCustom, calls=%fused_computation.6 | custom fusion | flops 8192 | bytes 8388612
  224.6 9.4 %reshape.71 = f32[256,8192]{1,0:T(8,128)} reshape(f32[2097152]{0:T(1024)} %scatter_custom_fusion) | data formatting | bytes 16777216 | tf_op jit(solution)/shard_map/scatter-add | solution.py:332
  233.9 11.0 %subtract_convert_fusion = (bf16[256,8192]{1,0:T(8,128)(2,1)}, bf16[256,8192]{1,0:T(8,128)(2,1)}) fusion(f32[256,8192]{1,0:T(8,128)} %reshape.71), kind=kLoop, calls=%fused_computation.5 | loop fusion | flops 8388608 | bytes 16777216 | tf_op jit(solution)/shard_map/convert_element_type | solution.py:336
  244.9 7.7 %pad_maximum_fusion = bf16[512,8192]{1,0:T(8,128)(2,1)} fusion(bf16[256,8192]{1,0:T(8,128)(2,1)} %get-tuple-element.14, bf16[256,8192]{1,0:T(8,128)(2,1)} %get-tuple-element.15), kind=kLoop, calls=%fused_computation.4 | loop fusion | flops 16777216 | bytes 16777216 | tf_op jit(solution)/shard_map/concatenate | solution.py:337
  252.6 6.5 %all-to-all-done.1 = bf16[64,128,512]{2,1,0:T(8,128)(2,1)} async-done(((bf16[64,128,512]{2,1,0:T(8,128)(2,1)}), bf16[64,128,512]{2,1,0:T(8,128)(2,1)}, u32[]{:S(2)}, u32[]{:S(2)}) %all-to-all-start.1) | async-done | bytes 8388640 | tf_op jit(solution)/shard_map/all_to_all | solution.py:305
  259.2 9.5 %fusion.17 = f32[512,512]{0,1:T(8,128)S(1)} fusion(bf16[512,8192]{1,0:T(8,128)(2,1)} %pad_maximum_fusion, bf16[8192,512]{1,0:T(8,128)(2,1)} %bitcast.10), kind=kOutput, calls=%fused_computation.43 | convolution fusion | flops 4294967296 | bytes 17825792 | tf_op jit(solution)/shard_map/dot_general | solution.py:338
  269.6 66.9 %shard_map.87 = (bf16[1024,512]{1,0:T(8,128)(2,1)}, f32[8,128]{1,0:T(8,128)}) custom-call(f32[2,256]{1,0:T(2,128)} %pad_maximum_fusion.1.stats_ref, f32[512,256]{1,0:T(8,128)} %bitcast.43, f32[512,256]{1,0:T(8,128)} %divide_bitcast_fusion.qt_ref, bf16[1024,256]{1,0:T(8,128)(2,1)} %bitcast.45), custom_call_target="tpu_custom_call" | custom-call | tf_op jit(solution)/shard_map/pallas_call | solution.py:225
  336.5 1.2 slice.19
  337.6 0.8 copy.26
  338.5 2.9 multiply_convert_fusion
  (46 shorter events, 6.2 us)
Async XLA Ops:
  0.6 101.7 %copy-start = (bf16[1024,512]{1,0:T(8,128)(2,1)S(1)}, bf16[1024,512]{1,0:T(8,128)(2,1)}, u32[]{:S(2)}) copy-start(bf16[1024,512]{1,0:T(8,128)(2,1)} %param.9) | copy-start | bytes 3145732
  0.6 18.7 %copy-start.1 = (bf16[256,512]{1,0:T(8,128)(2,1)S(1)}, bf16[256,512]{1,0:T(8,128)(2,1)}, u32[]{:S(2)}) copy-start(bf16[256,512]{1,0:T(8,128)(2,1)} %param.8) | copy-start | bytes 786436
  4.5 64.5 %all-to-all-start = ((bf16[64,128,128]{2,1,0:T(8,128)(2,1)}), bf16[64,128,128]{2,1,0:T(8,128)(2,1)S(1)}, u32[]{:S(2)}, u32[]{:S(2)}) async-start(bf16[64,128,128]{2,1,0:T(8,128)(2,1)} %gather_fusion), calls=%async_computation | async-start | bytes 4194304 | tf_op jit(solution)/shard_map/all_to_all | solution.py:304
  24.7 52.4 %copy-start.2 = (bf16[256,128]{1,0:T(8,128)(2,1)S(1)}, bf16[256,128]{1,0:T(8,128)(2,1)}, u32[]{:S(2)}) copy-start(bf16[256,128]{1,0:T(8,128)(2,1)} %param.7) | copy-start | bytes 196612
  24.7 52.5 %copy-start.6 = (s32[256,32]{0,1:T(8,128)S(1)}, s32[256,32]{0,1:T(8,128)}, u32[]{:S(2)}) copy-start(s32[256,32]{0,1:T(8,128)} %param.12) | copy-start | bytes 98308
  24.7 52.5 %copy-start.7 = (s32[256,32]{0,1:T(8,128)S(1)}, s32[256,32]{0,1:T(8,128)}, u32[]{:S(2)}) copy-start(s32[256,32]{0,1:T(8,128)} %param.11) | copy-start | bytes 98308
  24.7 52.7 %copy-start.9 = (s32[2]{0:T(128)S(1)}, s32[2]{0:T(128)}, u32[]{:S(2)}) copy-start(s32[2]{0:T(128)} %constant.25) | copy-start | bytes 28
  24.7 52.8 %copy-start.10 = (s32[2]{0:T(128)S(1)}, s32[2]{0:T(128)}, u32[]{:S(2)}) copy-start(s32[2]{0:T(128)} %constant.28) | copy-start | bytes 28
  69.0 190.2 %all-to-all-start.1 = ((bf16[64,128,512]{2,1,0:T(8,128)(2,1)}), bf16[64,128,512]{2,1,0:T(8,128)(2,1)}, u32[]{:S(2)}, u32[]{:S(2)}) async-start(bf16[64,128,512]{2,1,0:T(8,128)(2,1)} %gather_fusion.2), calls=%async_computation.1 | async-start | bytes 16777216 | tf_op jit(solution)/shard_map/all_to_all | solution.py:305
  101.5 0.8 copy-start.4
  119.2 57.8 %copy-start.8 = (s32[256]{0:T(256)S(1)}, s32[256]{0:T(256)}, u32[]{:S(2)}) copy-start(s32[256]{0:T(256)} %param.13) | copy-start | bytes 3076
  259.1 9.5 %copy-start.5 = (bf16[256,512]{0,1:T(8,128)(2,1)S(1)}, bf16[256,512]{0,1:T(8,128)(2,1)}, u32[]{:S(2)}) copy-start(bf16[256,512]{0,1:T(8,128)(2,1)} %copy.22) | copy-start | bytes 786436
  268.8 0.8 copy-start.3

commit v14 on v10

--- a/solution.py
+++ b/solution.py
@@ -14,7 +14,7 @@
 
 MESH = pl.DeviceIdType.MESH
 
-def _grad_kernel(nk, nx, nz, nch, ncls, scale, limit, stats_ref, zt_ref, qt_ref, embt_ref,
+def _grad_kernel(nk, nx, nz, nch, ncls, scale, limit, zt_ref, qt_ref, embt_ref,
                  out_ref, part_ref, sbuf, recv1, acc1, recv2, acc2, recv3, gath, nrm_dp, nrm_cls,
                  ss, rs, s1, r1, s2, r2, s3, r3, sb, rb, sc, rc, g3s, g3r, g2s, g2r, g1s, g1r):
     n = nk * nx * nz
@@ -46,13 +46,17 @@
 
     c_peers = [lax.rem(cj + e, ncls) for e in range(1, ncls)]
 
+    z_t = zt_ref[...]
+    z_max = jnp.max(z_t, axis=0, keepdims=True)
+    sbuf[cj, 0:1, :] = z_max
+    sbuf[cj, 1:2, :] = jnp.sum(jnp.exp(z_t - z_max), axis=0, keepdims=True)
+
     def st_desc(t, s):
         return pltpu.make_async_remote_copy(
-            src_ref=stats_ref, dst_ref=sbuf.at[s], send_sem=ss.at[t], recv_sem=rs.at[s],
+            src_ref=sbuf.at[s], dst_ref=sbuf.at[s], send_sem=ss.at[t], recv_sem=rs.at[s],
             device_id=(me, t), device_id_type=MESH)
     for t in c_peers:
         st_desc(t, cj).start()
-    sbuf[cj] = stats_ref[...]
     for t in c_peers:
         st_desc(t, cj).wait_send()
         st_desc(cj, t).wait_recv()
@@ -213,7 +217,7 @@
     out_ref[...] = (gath[...].astype(jnp.float32) * fac).astype(out_ref.dtype)
 
 
-def grad_reduce(stats, z_t, q_t, emb_t, n, ncls, scale, limit, nk=2, nx=4, nch=4):
+def grad_reduce(z_t, q_t, emb_t, n, ncls, scale, limit, nk=2, nx=4, nch=4):
     nz = n // (nk * nx)
     width = z_t.shape[0]
     total = emb_t.shape[0]
@@ -225,11 +229,11 @@
     return pl.pallas_call(
         functools.partial(_grad_kernel, nk, nx, nz, nch, ncls, scale, limit),
         out_shape=jax.ShapeDtypeStruct((total, width), jnp.bfloat16),
-        in_specs=[vmem] * 4,
+        in_specs=[vmem] * 3,
         out_specs=vmem,
         scratch_shapes=[
             pltpu.VMEM((total, width), jnp.float32),
-            pltpu.VMEM((ncls,) + stats.shape, jnp.float32),
+            pltpu.VMEM((ncls, 2, z_t.shape[1]), jnp.float32),
             pltpu.VMEM((nk, half, width), jnp.float32),
             pltpu.VMEM((half, width), jnp.float32),
             pltpu.VMEM((nx, quarter, width), jnp.float32),
@@ -244,7 +248,7 @@
             dma((nz,)), dma((nz,)), dma((nx,)), dma((nx,)), dma((nk * nch,)), dma((nk * nch,)),
         ],
         compiler_params=pltpu.CompilerParams(collective_id=0, has_side_effects=True),
-    )(stats, z_t, q_t, emb_t)
+    )(z_t, q_t, emb_t)
 
 
 def _class_gather_kernel(ncls, x_ref, out_ref, buf, ssem, rsem):
@@ -335,12 +339,10 @@
     both = jnp.dot(stacked, pool_lab, preferred_element_type=jnp.float32)
     spread = both[:rows] + both[rows:]
     target = 4.0 * spread + labels.astype(jnp.float32)
-    z_local = jnp.max(target, axis=1)
-    z_sum = jnp.sum(jnp.exp(target - z_local[:, None]), axis=1)
     scale = 1.0 / math.sqrt(rows * dp_count)
     limit = 0.5 * math.sqrt(D * C)
     head_grad = grad_reduce(
-        jnp.stack([z_local, z_sum], axis=0), target.T, prob_head.T, full_emb.T,
+        target.T, prob_head.T, full_emb.T,
         dp_count, lax.axis_size("class"), scale, limit,
     )
     return (target.astype(jnp.bfloat16), head_grad)

time: 341 us -> 341 us (level)
  no operation moved by 1% of the time
where the time goes in v14:
time: 341 us; the launch traced here: 340 us
  Pallas kernels  76.2 us (22%)
  other arithmetic  72.6 us (21%)
  local copies, waits for them, and re-layouts  54.4 us (16%)
  waiting for transfers between devices  50.8 us (15%)
  blocking collectives  49.4 us (14%)
  starting transfers between devices  22.1 us (6%)
  matrix products  13.5 us (4%)
    pallas_call x1, Pallas kernels, grad_reduce(): pl.pallas_call(functools.partial(_grad_kernel, nk, nx, nz, nch, ncls, sca...  67.3 us
    unnamed x4, other arithmetic  47.1 us
    all_to_all x1, waiting for transfers between devices, on_device(): lax.all_to_all(out_emb, 'dp', split_axis=0, concat_axis=0, tiled=True)  44.3 us
    gather x1, local copies, waits for them, and re-layouts, on_device(): near = pool_emb[located]  29.2 us
    psum x1, blocking collectives, on_device(): scores = lax.psum(partial_value, 'class')  25.8 us
    all_gather x1, blocking collectives, on_device(): full_emb = lax.all_gather(embeddings, 'class', axis=1, tiled=True)  23.6 us
    all_to_all x1, starting transfers between devices, on_device(): lax.all_to_all(out_emb, 'dp', split_axis=0, concat_axis=0, tiled=True)  14.8 us
    convert_element_type x1, other arithmetic, on_device(): dense_lo = (dense - dense_hi.astype(jnp.float32)).astype(jnp.bfloat16)  11 us
  transfers between devices with their start and end apart: 2, of which 2 were waited for; matrix products, arithmetic and copies ran while one was open for 36% of the time, Pallas kernels for 3%

profile of v14, /device:TPU:1, one launch (start us, length us, event | category | flops | bytes accessed | tf_op | source)
XLA Modules:
  0.0 340.0 jit_solution(16756020757552035046)
XLA Ops:
  1.4 3.0 gather_fusion
  4.5 14.8 %all-to-all-start = ((bf16[64,128,128]{2,1,0:T(8,128)(2,1)}), bf16[64,128,128]{2,1,0:T(8,128)(2,1)S(1)}, u32[]{:S(2)}, u32[]{:S(2)}) async-start(bf16[64,128,128]{2,1,0:T(8,128)(2,1)} %gather_fusion), calls=%async_computation | async-start | bytes 4194304 | tf_op jit(solution)/shard_map/all_to_all | solution.py:305
  19.3 5.4 %gather_fusion.2 = bf16[64,128,512]{2,1,0:T(8,128)(2,1)} fusion(bf16[2,128,512]{2,1,0:T(8,128)(2,1)S(1)} %bitcast.37, s32[1024]{0:T(1024)S(1)} %pad_clamp_fusion), kind=kCustom, calls=%fused_computation.2 | custom fusion | bytes 16777472 | tf_op jit(solution)/shard_map/gather | solution.py:304
  24.7 44.3 %all-to-all-done = bf16[64,128,128]{2,1,0:T(8,128)(2,1)S(1)} async-done(((bf16[64,128,128]{2,1,0:T(8,128)(2,1)}), bf16[64,128,128]{2,1,0:T(8,128)(2,1)S(1)}, u32[]{:S(2)}, u32[]{:S(2)}) %all-to-all-start) | async-done | bytes 2097184 | tf_op jit(solution)/shard_map/all_to_all | solution.py:305
  69.0 7.3 %all-to-all-start.1 = ((bf16[64,128,512]{2,1,0:T(8,128)(2,1)}), bf16[64,128,512]{2,1,0:T(8,128)(2,1)}, u32[]{:S(2)}, u32[]{:S(2)}) async-start(bf16[64,128,512]{2,1,0:T(8,128)(2,1)} %gather_fusion.2), calls=%async_computation.1 | async-start | bytes 16777216 | tf_op jit(solution)/shard_map/all_to_all | solution.py:306
  77.9 23.6 %all_gather.3 = bf16[256,1024]{0,1:T(8,128)(2,1)S(1)} all-gather(bf16[256,128]{0,1:T(8,128)(2,1)S(1)} %copy.29), channel_id=1, replica_groups=mesh['dp'=64,'class'=8] {'class'}, dimensions={1}, use_global_device_ids=true | all-gather | bytes 589824 | tf_op jit(solution)/shard_map/all_gather | solution.py:312
  102.3 1.3 fusion.16
  103.5 2.0 copy.31
  105.6 1.3 exponential_reduce_fusion
  107.4 8.9 %shard_map.86 = f32[8,2,256]{2,1,0:T(2,128)} custom-call(f32[2,256]{1,0:T(2,128)} %pad_maximum_fusion.1.x_ref), custom_call_target="tpu_custom_call" | custom-call | tf_op jit(solution)/shard_map/pallas_call | solution.py:278
  117.2 1.9 divide_bitcast_fusion.qt_ref
  119.2 29.2 %gather_fusion.1 = bf16[8192,128]{1,0:T(8,128)(2,1)} fusion(bf16[8192,128]{1,0:T(8,128)(2,1)S(1)} %bitcast.38, s32[8192]{0:T(1024)S(1)} %broadcast_clamp_fusion), kind=kCustom, calls=%fused_computation.1 | custom fusion | bytes 4227072 | tf_op jit(solution)/shard_map/gather | solution.py:321
  148.4 2.8 fusion.4
  151.1 25.8 %psum.7 = f32[256,32]{1,0:T(8,128)S(1)} all-reduce(f32[256,32]{1,0:T(8,128)S(1)} %bitcast.45), channel_id=1, replica_groups=mesh['dp'=64,'class'=8] {'class'}, use_global_device_ids=true, to_apply=%region_0.0 | all-reduce | flops 8192 | bytes 65536 | tf_op jit(solution)/shard_map/psum | solution.py:325
  177.7 46.9 %scatter_custom_fusion = f32[2097152]{0:T(1024)} fusion(s32[8192]{0:T(1024)S(1)} %reshape.95, f32[8192]{0:T(1024)S(1)} %reshape.97, f32[]{:T(128)} %constant.9.clone.1), kind=kCustom, calls=%fused_computation.6 | custom fusion | flops 8192 | bytes 8388612
  224.6 9.4 %reshape.70 = f32[256,8192]{1,0:T(8,128)} reshape(f32[2097152]{0:T(1024)} %scatter_custom_fusion) | data formatting | bytes 16777216 | tf_op jit(solution)/shard_map/scatter-add | solution.py:333
  233.9 11.0 %subtract_convert_fusion = (bf16[256,8192]{1,0:T(8,128)(2,1)}, bf16[256,8192]{1,0:T(8,128)(2,1)}) fusion(f32[256,8192]{1,0:T(8,128)} %reshape.70), kind=kLoop, calls=%fused_computation.5 | loop fusion | flops 8388608 | bytes 16777216 | tf_op jit(solution)/shard_map/convert_element_type | solution.py:337
  244.9 7.7 %pad_maximum_fusion = bf16[512,8192]{1,0:T(8,128)(2,1)} fusion(bf16[256,8192]{1,0:T(8,128)(2,1)} %get-tuple-element.8, bf16[256,8192]{1,0:T(8,128)(2,1)} %get-tuple-element.9), kind=kLoop, calls=%fused_computation.4 | loop fusion | flops 16777216 | bytes 16777216 | tf_op jit(solution)/shard_map/concatenate | solution.py:338
  252.6 6.5 %all-to-all-done.1 = bf16[64,128,512]{2,1,0:T(8,128)(2,1)} async-done(((bf16[64,128,512]{2,1,0:T(8,128)(2,1)}), bf16[64,128,512]{2,1,0:T(8,128)(2,1)}, u32[]{:S(2)}, u32[]{:S(2)}) %all-to-all-start.1) | async-done | bytes 8388640 | tf_op jit(solution)/shard_map/all_to_all | solution.py:306
  259.2 9.5 %fusion.17 = f32[512,512]{0,1:T(8,128)S(1)} fusion(bf16[512,8192]{1,0:T(8,128)(2,1)} %pad_maximum_fusion, bf16[8192,512]{1,0:T(8,128)(2,1)} %bitcast.10), kind=kOutput, calls=%fused_computation.41 | convolution fusion | flops 4294967296 | bytes 17825792 | tf_op jit(solution)/shard_map/dot_general | solution.py:339
  268.6 0.9 fusion.14
  269.5 67.3 %shard_map.87 = bf16[1024,512]{1,0:T(8,128)(2,1)} custom-call(f32[512,256]{1,0:T(8,128)} %get-tuple-element.10.zt_ref, f32[512,256]{1,0:T(8,128)} %divide_bitcast_fusion.qt_ref, bf16[1024,256]{1,0:T(8,128)(2,1)} %bitcast.42), custom_call_target="tpu_custom_call" | custom-call | tf_op jit(solution)/shard_map/pallas_call | solution.py:229
  336.9 0.8 copy.32
  337.7 2.3 copy.52
  (41 shorter events, 5.2 us)
Async XLA Ops:
  0.6 101.7 %copy-start = (bf16[1024,512]{1,0:T(8,128)(2,1)S(1)}, bf16[1024,512]{1,0:T(8,128)(2,1)}, u32[]{:S(2)}) copy-start(bf16[1024,512]{1,0:T(8,128)(2,1)} %param.9) | copy-start | bytes 3145732
  0.6 18.7 %copy-start.1 = (bf16[256,512]{1,0:T(8,128)(2,1)S(1)}, bf16[256,512]{1,0:T(8,128)(2,1)}, u32[]{:S(2)}) copy-start(bf16[256,512]{1,0:T(8,128)(2,1)} %param.8) | copy-start | bytes 786436
  4.5 64.5 %all-to-all-start = ((bf16[64,128,128]{2,1,0:T(8,128)(2,1)}), bf16[64,128,128]{2,1,0:T(8,128)(2,1)S(1)}, u32[]{:S(2)}, u32[]{:S(2)}) async-start(bf16[64,128,128]{2,1,0:T(8,128)(2,1)} %gather_fusion), calls=%async_computation | async-start | bytes 4194304 | tf_op jit(solution)/shard_map/all_to_all | solution.py:305
  24.7 52.4 %copy-start.2 = (bf16[256,128]{1,0:T(8,128)(2,1)S(1)}, bf16[256,128]{1,0:T(8,128)(2,1)}, u32[]{:S(2)}) copy-start(bf16[256,128]{1,0:T(8,128)(2,1)} %param.7) | copy-start | bytes 196612
  24.7 52.5 %copy-start.5 = (s32[256,32]{0,1:T(8,128)S(1)}, s32[256,32]{0,1:T(8,128)}, u32[]{:S(2)}) copy-start(s32[256,32]{0,1:T(8,128)} %param.12) | copy-start | bytes 98308
  24.7 52.5 %copy-start.6 = (s32[256,32]{0,1:T(8,128)S(1)}, s32[256,32]{0,1:T(8,128)}, u32[]{:S(2)}) copy-start(s32[256,32]{0,1:T(8,128)} %param.11) | copy-start | bytes 98308
  24.7 52.7 %copy-start.8 = (s32[2]{0:T(128)S(1)}, s32[2]{0:T(128)}, u32[]{:S(2)}) copy-start(s32[2]{0:T(128)} %constant.25) | copy-start | bytes 28
  24.7 52.8 %copy-start.9 = (s32[2]{0:T(128)S(1)}, s32[2]{0:T(128)}, u32[]{:S(2)}) copy-start(s32[2]{0:T(128)} %constant.28) | copy-start | bytes 28
  69.0 190.2 %all-to-all-start.1 = ((bf16[64,128,512]{2,1,0:T(8,128)(2,1)}), bf16[64,128,512]{2,1,0:T(8,128)(2,1)}, u32[]{:S(2)}, u32[]{:S(2)}) async-start(bf16[64,128,512]{2,1,0:T(8,128)(2,1)} %gather_fusion.2), calls=%async_computation.1 | async-start | bytes 16777216 | tf_op jit(solution)/shard_map/all_to_all | solution.py:306
  101.5 0.8 copy-start.3
  119.2 57.8 %copy-start.7 = (s32[256]{0:T(256)S(1)}, s32[256]{0:T(256)}, u32[]{:S(2)}) copy-start(s32[256]{0:T(256)} %param.13) | copy-start | bytes 3076
  259.1 9.5 %copy-start.4 = (bf16[256,512]{0,1:T(8,128)(2,1)S(1)}, bf16[256,512]{0,1:T(8,128)(2,1)}, u32[]{:S(2)}) copy-start(bf16[256,512]{0,1:T(8,128)(2,1)} %copy.28) | copy-start | bytes 786436

commit v15 on v10

--- a/solution.py
+++ b/solution.py
@@ -101,7 +101,7 @@
         a1 = a1 + recv1[p]
     acc1[...] = a1
 
-    x_peers = [lax.rem(xc + e, nx) for e in range(1, nx)]
+    x_peers = [lax.rem(xc + e, nx) for e in sorted(range(1, nx), key=lambda e: -min(e, nx - e))]
 
     def m2(p, mine):
         if mine:
@@ -117,7 +117,7 @@
         a2 = a2 + recv2[p]
     acc2[...] = a2
 
-    z_peers = [lax.rem(zc + e, nz) for e in range(1, nz)]
+    z_peers = [lax.rem(zc + e, nz) for e in sorted(range(1, nz), key=lambda e: -min(e, nz - e))]
 
     def m3(p, mine):
         if mine:

time: 341 us -> 340 us (level)
  no operation moved by 1% of the time
where the time goes in v15:
time: 340 us; the launch traced here: 339 us
  Pallas kernels  75.2 us (22%)
  other arithmetic  72.6 us (21%)
  local copies, waits for them, and re-layouts  54.5 us (16%)
  waiting for transfers between devices  50.7 us (15%)
  blocking collectives  49.4 us (15%)
  starting transfers between devices  22.1 us (6%)
  matrix products  13.5 us (4%)
    pallas_call x1, Pallas kernels, grad_reduce(): pl.pallas_call(functools.partial(_grad_kernel, nk, nx, nz, nch, ncls, sca...  66.2 us
    unnamed x4, other arithmetic  47.1 us
    all_to_all x1, waiting for transfers between devices, on_device(): lax.all_to_all(out_emb, 'dp', split_axis=0, concat_axis=0, tiled=True)  44.2 us
    gather x1, local copies, waits for them, and re-layouts, on_device(): near = pool_emb[located]  29.2 us
    psum x1, blocking collectives, on_device(): scores = lax.psum(partial_value, 'class')  25.8 us
    all_gather x1, blocking collectives, on_device(): full_emb = lax.all_gather(embeddings, 'class', axis=1, tiled=True)  23.6 us
    all_to_all x1, starting transfers between devices, on_device(): lax.all_to_all(out_emb, 'dp', split_axis=0, concat_axis=0, tiled=True)  14.8 us
    convert_element_type x1, other arithmetic, on_device(): dense_lo = (dense - dense_hi.astype(jnp.float32)).astype(jnp.bfloat16)  11 us
  transfers between devices with their start and end apart: 2, of which 2 were waited for; matrix products, arithmetic and copies ran while one was open for 36% of the time, Pallas kernels for 3%

profile of v15, /device:TPU:1, one launch (start us, length us, event | category | flops | bytes accessed | tf_op | source)
XLA Modules:
  0.0 338.9 jit_solution(6775212390675895821)
XLA Ops:
  1.4 3.0 gather_fusion
  4.5 14.8 %all-to-all-start = ((bf16[64,128,128]{2,1,0:T(8,128)(2,1)}), bf16[64,128,128]{2,1,0:T(8,128)(2,1)S(1)}, u32[]{:S(2)}, u32[]{:S(2)}) async-start(bf16[64,128,128]{2,1,0:T(8,128)(2,1)} %gather_fusion), calls=%async_computation | async-start | bytes 4194304 | tf_op jit(solution)/shard_map/all_to_all | solution.py:301
  19.3 5.4 %gather_fusion.2 = bf16[64,128,512]{2,1,0:T(8,128)(2,1)} fusion(bf16[2,128,512]{2,1,0:T(8,128)(2,1)S(1)} %bitcast.38, s32[1024]{0:T(1024)S(1)} %pad_clamp_fusion), kind=kCustom, calls=%fused_computation.2 | custom fusion | bytes 16777472 | tf_op jit(solution)/shard_map/gather | solution.py:300
  24.8 44.2 %all-to-all-done = bf16[64,128,128]{2,1,0:T(8,128)(2,1)S(1)} async-done(((bf16[64,128,128]{2,1,0:T(8,128)(2,1)}), bf16[64,128,128]{2,1,0:T(8,128)(2,1)S(1)}, u32[]{:S(2)}, u32[]{:S(2)}) %all-to-all-start) | async-done | bytes 2097184 | tf_op jit(solution)/shard_map/all_to_all | solution.py:301
  69.0 7.3 %all-to-all-start.1 = ((bf16[64,128,512]{2,1,0:T(8,128)(2,1)}), bf16[64,128,512]{2,1,0:T(8,128)(2,1)}, u32[]{:S(2)}, u32[]{:S(2)}) async-start(bf16[64,128,512]{2,1,0:T(8,128)(2,1)} %gather_fusion.2), calls=%async_computation.1 | async-start | bytes 16777216 | tf_op jit(solution)/shard_map/all_to_all | solution.py:302
  76.3 0.8 copy.22
  77.9 23.6 %all_gather.3 = bf16[256,1024]{0,1:T(8,128)(2,1)S(1)} all-gather(bf16[256,128]{0,1:T(8,128)(2,1)S(1)} %copy.23), channel_id=1, replica_groups=mesh['dp'=64,'class'=8] {'class'}, dimensions={1}, use_global_device_ids=true | all-gather | bytes 589824 | tf_op jit(solution)/shard_map/all_gather | solution.py:308
  102.3 1.3 fusion.16
  103.5 2.0 copy.25
  105.6 1.3 exponential_reduce_fusion
  107.4 8.9 %shard_map.86 = f32[8,2,256]{2,1,0:T(2,128)} custom-call(f32[2,256]{1,0:T(2,128)} %pad_maximum_fusion.2.x_ref), custom_call_target="tpu_custom_call" | custom-call | tf_op jit(solution)/shard_map/pallas_call | solution.py:274
  117.2 1.9 divide_bitcast_fusion.qt_ref
  119.2 29.2 %gather_fusion.1 = bf16[8192,128]{1,0:T(8,128)(2,1)} fusion(bf16[8192,128]{1,0:T(8,128)(2,1)S(1)} %bitcast.39, s32[8192]{0:T(1024)S(1)} %broadcast_clamp_fusion), kind=kCustom, calls=%fused_computation.1 | custom fusion | bytes 4227072 | tf_op jit(solution)/shard_map/gather | solution.py:317
  148.4 2.8 fusion.4
  151.1 25.8 %psum.7 = f32[256,32]{1,0:T(8,128)S(1)} all-reduce(f32[256,32]{1,0:T(8,128)S(1)} %bitcast.47), channel_id=1, replica_groups=mesh['dp'=64,'class'=8] {'class'}, use_global_device_ids=true, to_apply=%region_0.0 | all-reduce | flops 8192 | bytes 65536 | tf_op jit(solution)/shard_map/psum | solution.py:321
  177.7 46.9 %scatter_custom_fusion = f32[2097152]{0:T(1024)} fusion(s32[8192]{0:T(1024)S(1)} %reshape.96, f32[8192]{0:T(1024)S(1)} %reshape.98, f32[]{:T(128)} %constant.9.clone.1), kind=kCustom, calls=%fused_computation.6 | custom fusion | flops 8192 | bytes 8388612
  224.6 9.4 %reshape.71 = f32[256,8192]{1,0:T(8,128)} reshape(f32[2097152]{0:T(1024)} %scatter_custom_fusion) | data formatting | bytes 16777216 | tf_op jit(solution)/shard_map/scatter-add | solution.py:329
  233.9 11.0 %subtract_convert_fusion = (bf16[256,8192]{1,0:T(8,128)(2,1)}, bf16[256,8192]{1,0:T(8,128)(2,1)}) fusion(f32[256,8192]{1,0:T(8,128)} %reshape.71), kind=kLoop, calls=%fused_computation.5 | loop fusion | flops 8388608 | bytes 16777216 | tf_op jit(solution)/shard_map/convert_element_type | solution.py:333
  244.9 7.7 %pad_maximum_fusion = bf16[512,8192]{1,0:T(8,128)(2,1)} fusion(bf16[256,8192]{1,0:T(8,128)(2,1)} %get-tuple-element.10, bf16[256,8192]{1,0:T(8,128)(2,1)} %get-tuple-element.11), kind=kLoop, calls=%fused_computation.4 | loop fusion | flops 16777216 | bytes 16777216 | tf_op jit(solution)/shard_map/concatenate | solution.py:334
  252.6 6.5 %all-to-all-done.1 = bf16[64,128,512]{2,1,0:T(8,128)(2,1)} async-done(((bf16[64,128,512]{2,1,0:T(8,128)(2,1)}), bf16[64,128,512]{2,1,0:T(8,128)(2,1)}, u32[]{:S(2)}, u32[]{:S(2)}) %all-to-all-start.1) | async-done | bytes 8388640 | tf_op jit(solution)/shard_map/all_to_all | solution.py:302
  259.2 9.5 %fusion.17 = f32[512,512]{0,1:T(8,128)S(1)} fusion(bf16[512,8192]{1,0:T(8,128)(2,1)} %pad_maximum_fusion, bf16[8192,512]{1,0:T(8,128)(2,1)} %bitcast.10), kind=kOutput, calls=%fused_computation.42 | convolution fusion | flops 4294967296 | bytes 17825792 | tf_op jit(solution)/shard_map/dot_general | solution.py:335
  269.6 66.2 %shard_map.87 = bf16[1024,512]{1,0:T(8,128)(2,1)} custom-call(f32[2,256]{1,0:T(2,128)} %pad_maximum_fusion.1.stats_ref, f32[512,256]{1,0:T(8,128)} %bitcast.42, f32[512,256]{1,0:T(8,128)} %divide_bitcast_fusion.qt_ref, bf16[1024,256]{1,0:T(8,128)(2,1)} %bitcast.44), custom_call_target="tpu_custom_call" | custom-call | tf_op jit(solution)/shard_map/pallas_call | solution.py:225
  335.8 0.8 copy.26
  336.7 2.3 copy.45
  (45 shorter events, 5.3 us)
Async XLA Ops:
  0.6 101.7 %copy-start = (bf16[1024,512]{1,0:T(8,128)(2,1)S(1)}, bf16[1024,512]{1,0:T(8,128)(2,1)}, u32[]{:S(2)}) copy-start(bf16[1024,512]{1,0:T(8,128)(2,1)} %param.9) | copy-start | bytes 3145732
  0.6 18.7 %copy-start.1 = (bf16[256,512]{1,0:T(8,128)(2,1)S(1)}, bf16[256,512]{1,0:T(8,128)(2,1)}, u32[]{:S(2)}) copy-start(bf16[256,512]{1,0:T(8,128)(2,1)} %param.8) | copy-start | bytes 786436
  4.5 64.5 %all-to-all-start = ((bf16[64,128,128]{2,1,0:T(8,128)(2,1)}), bf16[64,128,128]{2,1,0:T(8,128)(2,1)S(1)}, u32[]{:S(2)}, u32[]{:S(2)}) async-start(bf16[64,128,128]{2,1,0:T(8,128)(2,1)} %gather_fusion), calls=%async_computation | async-start | bytes 4194304 | tf_op jit(solution)/shard_map/all_to_all | solution.py:301
  24.8 52.3 %copy-start.2 = (bf16[256,128]{1,0:T(8,128)(2,1)S(1)}, bf16[256,128]{1,0:T(8,128)(2,1)}, u32[]{:S(2)}) copy-start(bf16[256,128]{1,0:T(8,128)(2,1)} %param.7) | copy-start | bytes 196612
  24.8 52.5 %copy-start.6 = (s32[256,32]{0,1:T(8,128)S(1)}, s32[256,32]{0,1:T(8,128)}, u32[]{:S(2)}) copy-start(s32[256,32]{0,1:T(8,128)} %param.12) | copy-start | bytes 98308
  24.8 52.5 %copy-start.7 = (s32[256,32]{0,1:T(8,128)S(1)}, s32[256,32]{0,1:T(8,128)}, u32[]{:S(2)}) copy-start(s32[256,32]{0,1:T(8,128)} %param.11) | copy-start | bytes 98308
  24.8 52.7 %copy-start.9 = (s32[2]{0:T(128)S(1)}, s32[2]{0:T(128)}, u32[]{:S(2)}) copy-start(s32[2]{0:T(128)} %constant.25) | copy-start | bytes 28
  24.8 52.8 %copy-start.10 = (s32[2]{0:T(128)S(1)}, s32[2]{0:T(128)}, u32[]{:S(2)}) copy-start(s32[2]{0:T(128)} %constant.28) | copy-start | bytes 28
  69.0 190.2 %all-to-all-start.1 = ((bf16[64,128,512]{2,1,0:T(8,128)(2,1)}), bf16[64,128,512]{2,1,0:T(8,128)(2,1)}, u32[]{:S(2)}, u32[]{:S(2)}) async-start(bf16[64,128,512]{2,1,0:T(8,128)(2,1)} %gather_fusion.2), calls=%async_computation.1 | async-start | bytes 16777216 | tf_op jit(solution)/shard_map/all_to_all | solution.py:302
  101.5 0.8 copy-start.4
  119.2 57.8 %copy-start.8 = (s32[256]{0:T(256)S(1)}, s32[256]{0:T(256)}, u32[]{:S(2)}) copy-start(s32[256]{0:T(256)} %param.13) | copy-start | bytes 3076
  259.1 9.5 %copy-start.5 = (bf16[256,512]{0,1:T(8,128)(2,1)S(1)}, bf16[256,512]{0,1:T(8,128)(2,1)}, u32[]{:S(2)}) copy-start(bf16[256,512]{0,1:T(8,128)(2,1)} %copy.22) | copy-start | bytes 786436
  268.8 0.8 copy-start.3
